TPU v7x, 256 devices: a whole 4x4x8 slice. The times are simulated.
256 devices in a mesh: rows: 16 (over z, core), delay: 16 (over y, x).
Axes of the slice: x: 4, y: 4, z: 8, core: 2. Of those that a mesh axis runs over, the one named last changes fastest.
Arguments:
- retarded_tiles: bfloat16 [16, 1024, 4, 128, 128], P('delay', 'rows'), may hold values from -0.0625 to 0.0625
- wanted_blocks: int32 [16, 16, 16, 8], P('delay', 'rows'), may hold values from 0 to 63, as said below
- tile_slots: int32 [16, 1024, 4], P('delay', 'rows'), may hold values from 0 to 127, as said below
- diag_inverse: bfloat16 [1024, 128, 128], P('rows')
- excitation: float32 [4, 1024, 4, 128], P(None, 'rows'), may hold values from -6 to 6
- history_init: bfloat16 [16, 1024, 4, 128], P('delay', 'rows'), may hold values from -6 to 6
Outputs:
- currents: float32 [4, 1024, 4, 128], P(None, 'rows')
Inputs may be any that keep to these rules, and one draw needn't show every extreme that they name: `wanted_blocks`: for each bin, reader and owner, 8 distinct local block numbers of the owner. `tile_slots`: in each bin, every one of a reader's 16 * 8 taken blocks is the column block of at least one tile of the reader's row blocks.
All inputs are finite; a program needn't handle non-finite values.
Results may differ from a plain program's by a relative error of at most 0.0035.
Values may be sent and summed in bfloat16 or wider, within the bound.
No kernel may reach another device: no remote copies, remote signals or barrier semaphores. Data moves between devices by JAX's collectives and lax.ppermute only.
A program may use at most 64 MiB of HBM per device.

v0:
```python
import jax
import jax.numpy as jnp
from jax import lax
from jax.sharding import PartitionSpec as P

STEPS = 4


def in_blocks(array, dim, peers):
    shape = array.shape
    tiles = array.reshape(*shape[:dim], peers, shape[dim] // peers, *shape[dim + 1 :])
    return jnp.moveaxis(tiles, dim, 0)


def sent_and_summed(array, axis, dim):
    tiles = in_blocks(array, dim, lax.axis_size(axis))
    arrived = lax.all_to_all(tiles, axis, split_axis=0, concat_axis=0, tiled=True)
    return arrived.sum(axis=0)


def copy_for_each(array, axis):
    copies = jnp.broadcast_to(array, (lax.axis_size(axis), *array.shape))
    return lax.all_to_all(copies, axis, split_axis=0, concat_axis=0, tiled=True)


def laid_out(tiles, dim):
    shape = list(tiles.shape[1:])
    shape[dim] *= tiles.shape[0]
    return jnp.moveaxis(tiles, 0, dim).reshape(shape)


def gather_directly(array, axis, dim):
    tiles = copy_for_each(array, axis)
    return laid_out(tiles, dim)


def from_behind(array, axis, by):
    peers = lax.axis_size(axis)
    pairs = [(i, i + by) for i in range(peers) if 0 <= i + by < peers]
    return lax.ppermute(array, axis, pairs)


def body(retarded_tiles, wanted_blocks, tile_slots, diag_inverse, excitation, history_init):
    local_blocks = retarded_tiles.shape[1]
    listed = retarded_tiles.shape[2]
    requests = wanted_blocks[0, 0]
    slot_picks = tile_slots[0].reshape(-1)
    tile_block = retarded_tiles[0]
    position = lax.axis_index("delay")
    asked = lax.all_to_all(requests, "rows", split_axis=0, concat_axis=0, tiled=True)
    current = history_init[0]
    solved_list = []
    for moment in range(STEPS):
        looked_up = current[asked]
        arrived = lax.all_to_all(looked_up, "rows", split_axis=0, concat_axis=0, tiled=True)
        flat = arrived.reshape(-1, current.shape[1], current.shape[2])
        blocks = flat[slot_picks]
        blocks = blocks.reshape(local_blocks, listed, current.shape[1], current.shape[2])
        partial_value = jnp.einsum(
            "nleb,nlbc->nec", blocks, tile_block, preferred_element_type=jnp.float32
        )
        shared_sum = sent_and_summed(partial_value, "delay", 0)
        part_rows = shared_sum.shape[0]
        start = position * part_rows
        excite_part = lax.dynamic_slice_in_dim(excitation[moment], start, part_rows, 0)
        inverse_part = lax.dynamic_slice_in_dim(diag_inverse, start, part_rows, 0)
        driven = (excite_part - shared_sum).astype(jnp.bfloat16)
        solved_part = jnp.einsum(
            "neb,nbc->nec", driven, inverse_part, preferred_element_type=jnp.float32
        )
        solved = gather_directly(solved_part, "delay", 0)
        solved_list.append(solved)
        if moment + 1 < STEPS:
            rounded = solved.astype(jnp.bfloat16)
            shifted = from_behind(current, "delay", 1)
            current = jnp.where(position == 0, rounded, shifted)
    return jnp.stack(solved_list)


def solution(mesh):
    return jax.shard_map(
        body,
        mesh=mesh,
        in_specs=(
            P("delay", "rows", None, None, None),
            P("delay", "rows", None, None),
            P("delay", "rows", None),
            P("rows", None, None),
            P(None, "rows", None, None),
            P("delay", "rows", None, None),
        ),
        out_specs=P(None, "rows", None, None),
        check_vma=False,
    )
```

profile of v0, /device:TPU:2, one launch (start us, length us, event | category | flops | bytes accessed | tf_op | source)
XLA Modules:
  0.0 195.6 jit_solution(8003042012885467475)
XLA Ops:
  0.0 1.5 copy.10
  1.5 8.6 %all-to-all-start = ((s32[16,1,8]{2,1,0:T(1,128)}), s32[16,1,8]{2,1,0:T(1,128)S(1)}, u32[]{:S(2)}, u32[]{:S(2)}) async-start(s32[16,1,8]{2,1,0:T(1,128)} %copy.10), calls=%async_computation | async-start | bytes 16384 | tf_op jit(solution)/shard_map/all_to_all | solution.py:50
  10.1 0.8 copy.13
  10.9 0.1 reshape_squeeze.3
  11.0 6.6 %all-to-all-done = s32[16,1,8]{2,1,0:T(1,128)S(1)} async-done(((s32[16,1,8]{2,1,0:T(1,128)}), s32[16,1,8]{2,1,0:T(1,128)S(1)}, u32[]{:S(2)}, u32[]{:S(2)}) %all-to-all-start) | async-done | bytes 544 | tf_op jit(solution)/shard_map/all_to_all | solution.py:50
  17.9 2.2 %gather_fusion = bf16[128,4,128]{2,1,0:T(4,128)(2,1)} fusion(bf16[64,4,128]{2,1,0:T(4,128)(2,1)} %bitcast.96, s32[1024]{0:T(1024)S(1)} %pad_clamp_fusion.1), kind=kCustom, calls=%fused_computation | custom fusion | bytes 262656 | tf_op jit(solution)/shard_map/gather | solution.py:54
  20.1 3.6 %all-to-all-start.1 = ((bf16[16,8,4,128]{3,2,1,0:T(4,128)(2,1)}), bf16[16,8,4,128]{3,2,1,0:T(4,128)(2,1)S(1)}, u32[]{:S(2)}, u32[]{:S(2)}) async-start(bf16[16,8,4,128]{3,2,1,0:T(4,128)(2,1)} %bitcast.4), calls=%async_computation.1 | async-start | bytes 262144 | tf_op jit(solution)/shard_map/all_to_all | solution.py:55
  23.8 8.6 %all-to-all-done.1 = bf16[16,8,4,128]{3,2,1,0:T(4,128)(2,1)S(1)} async-done(((bf16[16,8,4,128]{3,2,1,0:T(4,128)(2,1)}), bf16[16,8,4,128]{3,2,1,0:T(4,128)(2,1)S(1)}, u32[]{:S(2)}, u32[]{:S(2)}) %all-to-all-start.1) | async-done | bytes 131104 | tf_op jit(solution)/shard_map/all_to_all | solution.py:55
  32.4 1.0 gather_fusion.1
  33.4 5.4 %fusion.6 = f32[64,4,128,1]{2,1,3,0:T(4,128)} fusion(bf16[64,4,4,128]{3,2,1,0:T(4,128)(2,1)S(1)} %bitcast.79, bf16[1,64,4,128,128]{4,3,2,1,0:T(8,128)(2,1)} %param.6), kind=kOutput, calls=%fused_computation.14 | convolution fusion | flops 33554432 | bytes 8781824 | tf_op jit(solution)/shard_map/nleb,nlbc->nec/dot_general | solution.py:59
  38.7 7.5 %all-to-all-start.2 = ((f32[16,4,4,128]{3,2,1,0:T(4,128)}), f32[16,4,4,128]{3,2,1,0:T(4,128)S(1)}, u32[]{:S(2)}, u32[]{:S(2)}) async-start(f32[16,4,4,128]{3,2,1,0:T(4,128)} %bitcast.11), calls=%async_computation.2 | async-start | bytes 262144 | tf_op jit(solution)/shard_map/all_to_all | solution.py:17
  46.3 6.9 %all-to-all-done.2 = f32[16,4,4,128]{3,2,1,0:T(4,128)S(1)} async-done(((f32[16,4,4,128]{3,2,1,0:T(4,128)}), f32[16,4,4,128]{3,2,1,0:T(4,128)S(1)}, u32[]{:S(2)}, u32[]{:S(2)}) %all-to-all-start.2) | async-done | bytes 131104 | tf_op jit(solution)/shard_map/all_to_all | solution.py:17
  53.2 0.2 fusion.14
  53.4 0.7 broadcast_in_dim.8
  54.0 4.8 %all-to-all-start.3 = ((f32[16,4,4,128]{3,2,1,0:T(4,128)}), f32[16,4,4,128]{3,2,1,0:T(4,128)S(1)}, u32[]{:S(2)}, u32[]{:S(2)}) async-start(f32[16,4,4,128]{3,2,1,0:T(4,128)} %broadcast_in_dim.8), calls=%async_computation.3 | async-start | bytes 262144 | tf_op jit(solution)/shard_map/all_to_all | solution.py:23
  58.8 3.4 %collective-permute-start = (bf16[64,4,128]{2,1,0:T(4,128)(2,1)S(1)}, bf16[64,4,128]{2,1,0:T(4,128)(2,1)S(1)}, u32[]{:S(2)}, u32[]{:S(2)}) collective-permute-start(bf16[64,4,128]{2,1,0:T(4,128)(2,1)S(1)} %bitcast.97), channel_id=1, source_target_pairs={{0,1},{1,2},{2,3},{3,4},{4,5},{5,6},{6,7},{7,8},{8,9},{9,10},{10,1... | collective-permute-start | bytes 196616 | tf_op jit(solution)/shard_map/ppermute | solution.py:40
  62.2 2.8 %collective-permute-done = bf16[64,4,128]{2,1,0:T(4,128)(2,1)S(1)} collective-permute-done((bf16[64,4,128]{2,1,0:T(4,128)(2,1)S(1)}, bf16[64,4,128]{2,1,0:T(4,128)(2,1)S(1)}, u32[]{:S(2)}, u32[]{:S(2)}) %collective-permute-start) | collective-permute-done | bytes 65568 | tf_op jit(solution)/shard_map/ppermute | solution.py:40
  65.0 0.6 all-to-all-done.3
  65.6 0.7 gather_fusion.2
  66.3 11.2 %all_to_all.72 = bf16[16,8,4,128]{3,2,1,0:T(4,128)(2,1)S(1)} all-to-all(bf16[16,8,4,128]{3,2,1,0:T(4,128)(2,1)S(1)} %bitcast.93), channel_id=1, replica_groups=mesh['rows'=16,'delay'=16] {'rows'}, dimensions={0} | all-to-all | bytes 262144 | tf_op jit(solution)/shard_map/all_to_all | solution.py:55
  77.5 1.0 gather_fusion.3
  78.5 4.7 %fusion.4 = f32[64,4,128,1]{2,1,3,0:T(4,128)S(1)} fusion(bf16[64,4,4,128]{3,2,1,0:T(4,128)(2,1)S(1)} %bitcast.80, bf16[1,64,4,128,128]{4,3,2,1,0:T(8,128)(2,1)} %param.6), kind=kOutput, calls=%fused_computation.12 | convolution fusion | flops 33554432 | bytes 8781824 | tf_op jit(solution)/shard_map/nleb,nlbc->nec/dot_general | solution.py:59
  83.2 13.2 %all_to_all.73 = f32[16,4,4,128]{3,2,1,0:T(4,128)S(1)} all-to-all(f32[16,4,4,128]{3,2,1,0:T(4,128)S(1)} %bitcast.89), channel_id=1, replica_groups=mesh['rows'=16,'delay'=16] {'delay'}, dimensions={0} | all-to-all | bytes 262144 | tf_op jit(solution)/shard_map/all_to_all | solution.py:17
  96.4 0.1 fusion.12
  96.6 0.7 broadcast_in_dim.9
  97.3 4.8 %all-to-all-start.6 = ((f32[16,4,4,128]{3,2,1,0:T(4,128)}), f32[16,4,4,128]{3,2,1,0:T(4,128)S(1)}, u32[]{:S(2)}, u32[]{:S(2)}) async-start(f32[16,4,4,128]{3,2,1,0:T(4,128)} %broadcast_in_dim.9), calls=%async_computation.6 | async-start | bytes 262144 | tf_op jit(solution)/shard_map/all_to_all | solution.py:23
  102.0 3.4 %collective-permute-start.1 = (bf16[64,4,128]{2,1,0:T(4,128)(2,1)S(1)}, bf16[64,4,128]{2,1,0:T(4,128)(2,1)S(1)}, u32[]{:S(2)}, u32[]{:S(2)}) collective-permute-start(bf16[64,4,128]{2,1,0:T(4,128)(2,1)S(1)} %bitcast_select_fusion.2), channel_id=1, source_target_pairs={{0,1},{1,2},{2,3},{3,4},{4,5},{5,6},{6,7},{7,8},{8,9},{9,10},{10,1... | collective-permute-start | bytes 196616 | tf_op jit(solution)/shard_map/ppermute | solution.py:40
  105.4 2.8 %collective-permute-done.1 = bf16[64,4,128]{2,1,0:T(4,128)(2,1)S(1)} collective-permute-done((bf16[64,4,128]{2,1,0:T(4,128)(2,1)S(1)}, bf16[64,4,128]{2,1,0:T(4,128)(2,1)S(1)}, u32[]{:S(2)}, u32[]{:S(2)}) %collective-permute-start.1) | collective-permute-done | bytes 65568 | tf_op jit(solution)/shard_map/ppermute | solution.py:40
  108.2 0.6 all-to-all-done.6
  108.8 0.7 gather_fusion.4
  109.5 11.5 %all_to_all.74 = bf16[16,8,4,128]{3,2,1,0:T(4,128)(2,1)S(1)} all-to-all(bf16[16,8,4,128]{3,2,1,0:T(4,128)(2,1)S(1)} %bitcast.94), channel_id=1, replica_groups=mesh['rows'=16,'delay'=16] {'rows'}, dimensions={0} | all-to-all | bytes 262144 | tf_op jit(solution)/shard_map/all_to_all | solution.py:55
  121.0 1.0 gather_fusion.5
  122.0 4.7 %fusion.2 = f32[64,4,128,1]{2,1,3,0:T(4,128)S(1)} fusion(bf16[64,4,4,128]{3,2,1,0:T(4,128)(2,1)S(1)} %bitcast.81, bf16[1,64,4,128,128]{4,3,2,1,0:T(8,128)(2,1)} %param.6), kind=kOutput, calls=%fused_computation.10 | convolution fusion | flops 33554432 | bytes 8781824 | tf_op jit(solution)/shard_map/nleb,nlbc->nec/dot_general | solution.py:59
  126.7 13.2 %all_to_all.75 = f32[16,4,4,128]{3,2,1,0:T(4,128)S(1)} all-to-all(f32[16,4,4,128]{3,2,1,0:T(4,128)S(1)} %bitcast.90), channel_id=1, replica_groups=mesh['rows'=16,'delay'=16] {'delay'}, dimensions={0} | all-to-all | bytes 262144 | tf_op jit(solution)/shard_map/all_to_all | solution.py:17
  139.9 0.1 fusion.10
  140.1 0.7 broadcast_in_dim.10
  140.8 4.8 %all-to-all-start.9 = ((f32[16,4,4,128]{3,2,1,0:T(4,128)}), f32[16,4,4,128]{3,2,1,0:T(4,128)S(1)}, u32[]{:S(2)}, u32[]{:S(2)}) async-start(f32[16,4,4,128]{3,2,1,0:T(4,128)} %broadcast_in_dim.10), calls=%async_computation.9 | async-start | bytes 262144 | tf_op jit(solution)/shard_map/all_to_all | solution.py:23
  145.5 3.4 %collective-permute-start.2 = (bf16[64,4,128]{2,1,0:T(4,128)(2,1)S(1)}, bf16[64,4,128]{2,1,0:T(4,128)(2,1)S(1)}, u32[]{:S(2)}, u32[]{:S(2)}) collective-permute-start(bf16[64,4,128]{2,1,0:T(4,128)(2,1)S(1)} %bitcast_select_fusion.1), channel_id=1, source_target_pairs={{0,1},{1,2},{2,3},{3,4},{4,5},{5,6},{6,7},{7,8},{8,9},{9,10},{10,1... | collective-permute-start | bytes 196616 | tf_op jit(solution)/shard_map/ppermute | solution.py:40
  148.9 2.8 %collective-permute-done.2 = bf16[64,4,128]{2,1,0:T(4,128)(2,1)S(1)} collective-permute-done((bf16[64,4,128]{2,1,0:T(4,128)(2,1)S(1)}, bf16[64,4,128]{2,1,0:T(4,128)(2,1)S(1)}, u32[]{:S(2)}, u32[]{:S(2)}) %collective-permute-start.2) | collective-permute-done | bytes 65568 | tf_op jit(solution)/shard_map/ppermute | solution.py:40
  151.7 0.6 all-to-all-done.9
  152.3 0.7 gather_fusion.6
  153.0 11.5 %all_to_all.76 = bf16[16,8,4,128]{3,2,1,0:T(4,128)(2,1)S(1)} all-to-all(bf16[16,8,4,128]{3,2,1,0:T(4,128)(2,1)S(1)} %bitcast.92), channel_id=1, replica_groups=mesh['rows'=16,'delay'=16] {'rows'}, dimensions={0} | all-to-all | bytes 262144 | tf_op jit(solution)/shard_map/all_to_all | solution.py:55
  164.5 1.0 gather_fusion.7
  165.5 4.7 %fusion = f32[64,4,128,1]{2,1,3,0:T(4,128)S(1)} fusion(bf16[64,4,4,128]{3,2,1,0:T(4,128)(2,1)S(1)} %bitcast.78, bf16[1,64,4,128,128]{4,3,2,1,0:T(8,128)(2,1)} %param.6), kind=kOutput, calls=%fused_computation.8 | convolution fusion | flops 33554432 | bytes 8781824 | tf_op jit(solution)/shard_map/nleb,nlbc->nec/dot_general | solution.py:59
  170.2 13.2 %all_to_all.77 = f32[16,4,4,128]{3,2,1,0:T(4,128)S(1)} all-to-all(f32[16,4,4,128]{3,2,1,0:T(4,128)S(1)} %bitcast.91), channel_id=1, replica_groups=mesh['rows'=16,'delay'=16] {'delay'}, dimensions={0} | all-to-all | bytes 262144 | tf_op jit(solution)/shard_map/all_to_all | solution.py:17
  183.4 0.1 fusion.8
  183.6 11.1 %all_to_all.78 = f32[16,4,4,128]{3,2,1,0:T(4,128)S(1)} all-to-all(f32[16,4,4,128]{3,2,1,0:T(4,128)S(1)} %broadcast_in_dim.11), channel_id=1, replica_groups=mesh['rows'=16,'delay'=16] {'delay'}, dimensions={0} | all-to-all | bytes 262144 | tf_op jit(solution)/shard_map/all_to_all | solution.py:23
  194.7 0.9 pad_maximum_fusion
  (22 shorter events, 0.6 us)
Async XLA Ops:
  0.0 53.2 %copy-start = (bf16[64,128,128]{2,1,0:T(8,128)(2,1)S(1)}, bf16[64,128,128]{2,1,0:T(8,128)(2,1)}, u32[]{:S(2)}) copy-start(bf16[64,128,128]{2,1,0:T(8,128)(2,1)} %param.9) | copy-start | bytes 6291460
  1.5 16.1 %all-to-all-start = ((s32[16,1,8]{2,1,0:T(1,128)}), s32[16,1,8]{2,1,0:T(1,128)S(1)}, u32[]{:S(2)}, u32[]{:S(2)}) async-start(s32[16,1,8]{2,1,0:T(1,128)} %copy.10), calls=%async_computation | async-start | bytes 16384 | tf_op jit(solution)/shard_map/all_to_all | solution.py:50
  20.1 26.1 %copy-start.1 = (f32[4,64,4,128]{3,2,1,0:T(4,128)S(1)}, f32[4,64,4,128]{3,2,1,0:T(4,128)}, u32[]{:S(2)}) copy-start(f32[4,64,4,128]{3,2,1,0:T(4,128)} %param.10) | copy-start | bytes 1572868
  20.1 12.3 %all-to-all-start.1 = ((bf16[16,8,4,128]{3,2,1,0:T(4,128)(2,1)}), bf16[16,8,4,128]{3,2,1,0:T(4,128)(2,1)S(1)}, u32[]{:S(2)}, u32[]{:S(2)}) async-start(bf16[16,8,4,128]{3,2,1,0:T(4,128)(2,1)} %bitcast.4), calls=%async_computation.1 | async-start | bytes 262144 | tf_op jit(solution)/shard_map/all_to_all | solution.py:55
  33.4 25.4 %copy-start.2 = (bf16[1,64,4,128]{3,2,1,0:T(4,128)(2,1)S(1)}, bf16[1,64,4,128]{3,2,1,0:T(4,128)(2,1)}, u32[]{:S(2)}) copy-start(bf16[1,64,4,128]{3,2,1,0:T(4,128)(2,1)} %param.11) | copy-start | bytes 196612
  38.7 14.4 %all-to-all-start.2 = ((f32[16,4,4,128]{3,2,1,0:T(4,128)}), f32[16,4,4,128]{3,2,1,0:T(4,128)S(1)}, u32[]{:S(2)}, u32[]{:S(2)}) async-start(f32[16,4,4,128]{3,2,1,0:T(4,128)} %bitcast.11), calls=%async_computation.2 | async-start | bytes 262144 | tf_op jit(solution)/shard_map/all_to_all | solution.py:17
  54.0 11.5 %all-to-all-start.3 = ((f32[16,4,4,128]{3,2,1,0:T(4,128)}), f32[16,4,4,128]{3,2,1,0:T(4,128)S(1)}, u32[]{:S(2)}, u32[]{:S(2)}) async-start(f32[16,4,4,128]{3,2,1,0:T(4,128)} %broadcast_in_dim.8), calls=%async_computation.3 | async-start | bytes 262144 | tf_op jit(solution)/shard_map/all_to_all | solution.py:23
  58.8 6.2 %collective-permute-start = (bf16[64,4,128]{2,1,0:T(4,128)(2,1)S(1)}, bf16[64,4,128]{2,1,0:T(4,128)(2,1)S(1)}, u32[]{:S(2)}, u32[]{:S(2)}) collective-permute-start(bf16[64,4,128]{2,1,0:T(4,128)(2,1)S(1)} %bitcast.97), channel_id=1, source_target_pairs={{0,1},{1,2},{2,3},{3,4},{4,5},{5,6},{6,7},{7,8},{8,9},{9,10},{10,1... | collective-permute-start | bytes 196616 | tf_op jit(solution)/shard_map/ppermute | solution.py:40
  97.3 11.5 %all-to-all-start.6 = ((f32[16,4,4,128]{3,2,1,0:T(4,128)}), f32[16,4,4,128]{3,2,1,0:T(4,128)S(1)}, u32[]{:S(2)}, u32[]{:S(2)}) async-start(f32[16,4,4,128]{3,2,1,0:T(4,128)} %broadcast_in_dim.9), calls=%async_computation.6 | async-start | bytes 262144 | tf_op jit(solution)/shard_map/all_to_all | solution.py:23
  102.0 6.1 %collective-permute-start.1 = (bf16[64,4,128]{2,1,0:T(4,128)(2,1)S(1)}, bf16[64,4,128]{2,1,0:T(4,128)(2,1)S(1)}, u32[]{:S(2)}, u32[]{:S(2)}) collective-permute-start(bf16[64,4,128]{2,1,0:T(4,128)(2,1)S(1)} %bitcast_select_fusion.2), channel_id=1, source_target_pairs={{0,1},{1,2},{2,3},{3,4},{4,5},{5,6},{6,7},{7,8},{8,9},{9,10},{10,1... | collective-permute-start | bytes 196616 | tf_op jit(solution)/shard_map/ppermute | solution.py:40
  140.8 11.5 %all-to-all-start.9 = ((f32[16,4,4,128]{3,2,1,0:T(4,128)}), f32[16,4,4,128]{3,2,1,0:T(4,128)S(1)}, u32[]{:S(2)}, u32[]{:S(2)}) async-start(f32[16,4,4,128]{3,2,1,0:T(4,128)} %broadcast_in_dim.10), calls=%async_computation.9 | async-start | bytes 262144 | tf_op jit(solution)/shard_map/all_to_all | solution.py:23
  145.5 6.1 %collective-permute-start.2 = (bf16[64,4,128]{2,1,0:T(4,128)(2,1)S(1)}, bf16[64,4,128]{2,1,0:T(4,128)(2,1)S(1)}, u32[]{:S(2)}, u32[]{:S(2)}) collective-permute-start(bf16[64,4,128]{2,1,0:T(4,128)(2,1)S(1)} %bitcast_select_fusion.1), channel_id=1, source_target_pairs={{0,1},{1,2},{2,3},{3,4},{4,5},{5,6},{6,7},{7,8},{8,9},{9,10},{10,1... | collective-permute-start | bytes 196616 | tf_op jit(solution)/shard_map/ppermute | solution.py:40
where the time goes:
time: 197 us; the launch traced here: 196 us
  blocking collectives  84.9 us (43%)
  starting transfers between devices  44.1 us (22%)
  waiting for transfers between devices  32.1 us (16%)
  matrix products  20 us (10%)
  local copies, waits for them, and re-layouts  13.1 us (7%)
    all_to_all x3, blocking collectives, sent_and_summed(): lax.all_to_all(tiles, axis, split_axis=0, concat_axis=0, tiled=True)  39.7 us
    all_to_all x3, blocking collectives, body(): lax.all_to_all(looked_up, 'rows', split_axis=0, concat_axis=0, tiled=True)  34.2 us
    dot_general x4, matrix products, body(): jnp.einsum('nleb,nlbc->nec', blocks, tile_block, preferred_element_type=j...  19.4 us
    all_to_all x3, starting transfers between devices, copy_for_each(): return lax.all_to_all(copies, axis, split_axis=0, concat_axis=0, tiled=True)  14.3 us
    all_to_all x1, blocking collectives, copy_for_each(): return lax.all_to_all(copies, axis, split_axis=0, concat_axis=0, tiled=True)  11.1 us
    ppermute x3, starting transfers between devices, from_behind(): return lax.ppermute(array, axis, pairs)  10.1 us
    all_to_all x1, waiting for transfers between devices, body(): lax.all_to_all(looked_up, 'rows', split_axis=0, concat_axis=0, tiled=True)  8.59 us
    all_to_all x1, starting transfers between devices, body(): lax.all_to_all(requests, 'rows', split_axis=0, concat_axis=0, tiled=True)  8.57 us
  transfers between devices with their start and end apart: 9, of which 9 were waited for; matrix products, arithmetic and copies ran while one was open for 0% of the time, Pallas kernels for 0%

commit v1 on v0

v1 whole, which is shorter than its diff:
```python
import jax
import jax.numpy as jnp
from jax import lax
from jax.experimental import pallas as pl
from jax.experimental.pallas import tpu as pltpu
from jax.sharding import PartitionSpec as P

STEPS = 4
LANES = 16
ROWS = 16
CAP = 8
NB = 64
EXC = 4
B = 128
L = 4
TAKEN = ROWS * CAP
FLAT = NB * EXC
SPARE = (4, 5, 6)
GROUP = 8

bf16 = jnp.bfloat16
f32 = jnp.float32
VMEM = pl.BlockSpec(memory_space=pltpu.VMEM)
SMEM = pl.BlockSpec(memory_space=pltpu.SMEM)
LIMIT = 24 * 1024 * 1024


def call(kernel, out_shape, scratch, operands, in_smem, name):
    specs = [SMEM if i in in_smem else VMEM for i in range(len(operands))]
    many = isinstance(out_shape, (tuple, list))
    return pl.pallas_call(
        kernel,
        out_shape=out_shape,
        in_specs=specs,
        out_specs=[VMEM] * len(out_shape) if many else VMEM,
        scratch_shapes=scratch,
        compiler_params=pltpu.CompilerParams(vmem_limit_bytes=LIMIT),
        name=name,
    )(*operands)


def pick_initial(asked, h0, h1, h2, h3, out, wide, packed):
    for t, h in enumerate((h0, h1, h2, h3)):
        wide[:, EXC * t : EXC * (t + 1), :] = h[...].astype(f32)
    packed[...] = wide[...].astype(bf16)

    @pl.loop(0, ROWS)
    def _(r):
        for p in range(CAP):
            out[r * CAP + p] = packed[asked[r, p]]


def initial_terms(slots, tiles, arrived, out, total):
    @pl.loop(0, NB // GROUP)
    def _(g):
        for j in range(GROUP):
            i = g * GROUP + j
            row = jnp.concatenate([arrived[slots[s, i]] for s in range(L)], axis=1)
            tile = tiles[i].reshape(L * B, B)
            term = jnp.dot(row, tile, preferred_element_type=f32)
            at = pl.multiple_of(g * GROUP * EXC, GROUP * EXC)
            for t in range(STEPS):
                total[t, pl.ds(at + EXC * j, EXC), :] = term[EXC * t : EXC * (t + 1)]

    for t in range(STEPS):
        value = total[t].astype(bf16)
        if t == 0:
            for lane in range(LANES):
                if lane not in SPARE:
                    out[lane] = value
        else:
            out[SPARE[t - 1]] = value


def solve_and_pick(asked, driven, diag, solved, send):
    for i in range(NB):
        row = driven[EXC * i : EXC * (i + 1), :].astype(bf16)
        solved[i] = jnp.dot(row, diag[i], preferred_element_type=f32)

    @pl.loop(0, ROWS)
    def _(r):
        for p in range(CAP):
            send[r * CAP + p] = solved[asked[r, p]].astype(bf16)


def first_step(lane, asked, terms, excite, diag, item, send, driven, solved):
    total = terms[0].astype(f32)
    for k in range(1, LANES):
        total = total + terms[k].astype(f32)
    value = excite[...] - total
    driven[...] = value
    me = lane[0]
    spare = (me >= SPARE[0]) & (me <= SPARE[-1])
    item[...] = jnp.where(spare, total, value).astype(bf16)
    solve_and_pick(asked, driven, diag, solved, send)


def tile_terms(slots, tiles, arrived, total):
    @pl.loop(0, NB // GROUP)
    def _(g):
        for j in range(GROUP):
            i = g * GROUP + j
            row = jnp.concatenate([arrived[slots[s, i]] for s in range(L)], axis=1)
            tile = tiles[i].reshape(L * B, B)
            at = pl.multiple_of(g * GROUP * EXC, GROUP * EXC)
            total[pl.ds(at + EXC * j, EXC), :] = jnp.dot(row, tile, preferred_element_type=f32)


def second_step(lane, asked, slots, tiles, arrived, extra, excite, diag, item, send, total, driven, solved):
    tile_terms(slots, tiles, arrived, total)
    value = total[...] + extra[...].astype(f32)
    rest = excite[...] - value
    driven[...] = rest
    item[...] = jnp.where(lane[0] == 0, rest, value).astype(bf16)
    solve_and_pick(asked, driven, diag, solved, send)


def third_step(lane, asked, slots, tiles, arrived, extra, held, excite, diag, item, send, total, driven, solved):
    tile_terms(slots, tiles, arrived, total)
    me = lane[0]
    came = extra[...].astype(f32)
    rest = jnp.where(me == 0, excite[...] - (total[...] + came), came)
    driven[...] = rest
    item[...] = jnp.where(me == 2, held[...].astype(f32), rest).astype(bf16)
    solve_and_pick(asked, driven, diag, solved, send)


def fourth_step(lane, slots, tiles, arrived, extra, out, total):
    tile_terms(slots, tiles, arrived, total)
    me = lane[0]
    came = extra[...].astype(f32)
    value = jnp.where(me == 0, total[...], jnp.where(me == 1, total[...] + came, came)).astype(bf16)
    for y in range(4):
        out[y] = value


def last_solve(item0, items, excite, diag, out, driven):
    driven[0] = item0[...].astype(f32)
    driven[1] = items[2].astype(f32)
    driven[2] = items[3].astype(f32)
    driven[3] = excite[...] - (items[0].astype(f32) + items[1].astype(f32))
    for i in range(NB):
        rows = [driven[t, EXC * i : EXC * (i + 1), :] for t in range(STEPS)]
        both = jnp.concatenate(rows, axis=0).astype(bf16)
        value = jnp.dot(both, diag[i], preferred_element_type=f32)
        for t in range(STEPS):
            out[t, i] = value[EXC * t : EXC * (t + 1)]


def shifted(array, axis, by):
    peers = lax.axis_size(axis)
    return lax.ppermute(array, axis, [(i, i + by) for i in range(peers - by)])


def exchange(array, axis, groups=None):
    return lax.all_to_all(array, axis, split_axis=0, concat_axis=0, tiled=True, axis_index_groups=groups)


def body(retarded_tiles, wanted_blocks, tile_slots, diag_inverse, excitation, history_init):
    sds = jax.ShapeDtypeStruct
    tiles = retarded_tiles[0]
    slots = tile_slots[0].T
    lane = lax.axis_index("delay").astype(jnp.int32).reshape(1)
    excite = excitation.reshape(STEPS, FLAT, B)

    asked = exchange(wanted_blocks[0, 0], "rows")
    h0 = history_init[0]
    later = [shifted(h0, "delay", t) for t in range(1, STEPS)]

    picked = call(
        pick_initial,
        sds((TAKEN, EXC * STEPS, B), bf16),
        [pltpu.VMEM((NB, EXC * STEPS, B), f32), pltpu.VMEM((NB, EXC * STEPS, B), bf16)],
        (asked, h0, *later),
        (0,),
        "pick_initial",
    )
    arrived = exchange(picked.reshape(ROWS, CAP, EXC * STEPS, B), "rows").reshape(TAKEN, EXC * STEPS, B)
    terms = call(
        initial_terms,
        sds((LANES, FLAT, B), bf16),
        [pltpu.VMEM((STEPS, FLAT, B), f32)],
        (slots, tiles, arrived),
        (0,),
        "initial_terms",
    )
    terms = exchange(terms, "delay")

    flat = pltpu.VMEM((FLAT, B), f32)
    block = pltpu.VMEM((NB, EXC, B), f32)
    outs = (sds((FLAT, B), bf16), sds((TAKEN, EXC, B), bf16))

    item, send = call(
        first_step, outs, [flat, block], (lane, asked, terms, excite[0], diag_inverse), (0, 1), "first_step"
    )
    came = lax.ppermute(item, "delay", [(4, 0), (5, 1), (6, 2), (0, 4), (1, 5), (2, 6)])
    arrived = exchange(send.reshape(ROWS, CAP, EXC, B), "rows").reshape(TAKEN, EXC, B)
    me = lane[0]
    item0 = jnp.where((me >= SPARE[0]) & (me <= SPARE[-1]), came, item)

    item1, send = call(
        second_step,
        outs,
        [flat, flat, block],
        (lane, asked, slots, tiles, arrived, came, excite[1], diag_inverse),
        (0, 1, 2),
        "second_step",
    )
    came = lax.ppermute(item1, "delay", [(0, 1), (1, 0)])
    arrived = exchange(send.reshape(ROWS, CAP, EXC, B), "rows").reshape(TAKEN, EXC, B)

    item2, send = call(
        third_step,
        outs,
        [flat, flat, block],
        (lane, asked, slots, tiles, arrived, came, item1, excite[2], diag_inverse),
        (0, 1, 2),
        "third_step",
    )
    came = lax.ppermute(item2, "delay", [(0, 3), (1, 2), (2, 1)])
    arrived = exchange(send.reshape(ROWS, CAP, EXC, B), "rows").reshape(TAKEN, EXC, B)

    item3 = call(
        fourth_step,
        sds((4, FLAT, B), bf16),
        [flat],
        (lane, slots, tiles, arrived, came),
        (0, 1),
        "fourth_step",
    )
    along_y = [[4 * y + x for y in range(4)] for x in range(4)]
    along_x = [[4 * y + x for x in range(4)] for y in range(4)]
    column = exchange(item3, "delay", along_y)[0]
    items = exchange(jnp.broadcast_to(column, (4, FLAT, B)), "delay", along_x)
    return call(
        last_solve,
        sds((STEPS, NB, EXC, B), f32),
        [pltpu.VMEM((STEPS, FLAT, B), f32)],
        (item0, items, excite[3], diag_inverse),
        (),
        "last_solve",
    )


def solution(mesh):
    return jax.shard_map(
        body,
        mesh=mesh,
        in_specs=(
            P("delay", "rows", None, None, None),
            P("delay", "rows", None, None),
            P("delay", "rows", None),
            P("rows", None, None),
            P(None, "rows", None, None),
            P("delay", "rows", None, None),
        ),
        out_specs=P(None, "rows", None, None),
        check_vma=False,
    )
```

time: 197 us -> 170 us (0.86)
  blocking collectives: 84.9 us -> 34.5 us
  matrix products: 20 us -> 0 us
  Pallas kernels: 0 us -> 18.6 us
  waiting for transfers between devices: 32.1 us -> 45 us
  local copies, waits for them, and re-layouts: 13.1 us -> 21.5 us
  starting transfers between devices: 44.1 us -> 49.1 us
    all_to_all x7 -> x2, blocking collectives: 84.9 us -> 34.5 us  [exchange(): lax.all_to_all(array, axis, split_axis=0, concat_axis=0, tiled=True, axis...]
    dot_general x8 -> x0, matrix products: 20 us -> none  [the longest x4 19.4 us: body(): jnp.einsum('nleb,nlbc->nec', blocks, tile_block, preferred_element_type=j...]
    pallas_call x0 -> x7, Pallas kernels: none -> 18.6 us  [call(): pl.pallas_call(kernel, out_shape=out_shape, in_specs=specs, out_specs=[VM...]
    unnamed x7 -> x26, local copies, waits for them, and re-layouts: 0.79 us -> 18.2 us
    ppermute x3 -> x6, starting transfers between devices: 10.1 us -> 20.6 us  [the longest x3 11.5 us: shifted(): return lax.ppermute(array, axis, [(i, i + by) for i in range(peers - by)])]
    all_to_all x6, waiting for transfers between devices: 23.8 us -> 33.8 us  [exchange(): lax.all_to_all(array, axis, split_axis=0, concat_axis=0, tiled=True, axis...]
    gather x8 -> x0, local copies, waits for them, and re-layouts: 8.4 us -> none  [the longest x4 4.48 us: body(): looked_up = current[asked]]
    all_to_all x6, starting transfers between devices: 34 us -> 28.6 us  [exchange(): lax.all_to_all(array, axis, split_axis=0, concat_axis=0, tiled=True, axis...]
  transfers between devices with their start and end apart: 9 -> 12, of which waited for: 9 -> 9; matrix products, arithmetic and copies ran while one was open for 0% -> 2% of each run, Pallas kernels for 0% -> 0%
where the time goes in v1:
time: 170 us; the launch traced here: 169 us
  starting transfers between devices  49.1 us (29%)
  waiting for transfers between devices  45 us (26%)
  blocking collectives  34.5 us (20%)
  local copies, waits for them, and re-layouts  21.5 us (13%)
  Pallas kernels  18.6 us (11%)
    all_to_all x2, blocking collectives, exchange(): lax.all_to_all(array, axis, split_axis=0, concat_axis=0, tiled=True, axis...  34.5 us
    all_to_all x6, waiting for transfers between devices, exchange(): lax.all_to_all(array, axis, split_axis=0, concat_axis=0, tiled=True, axis...  33.8 us
    all_to_all x6, starting transfers between devices, exchange(): lax.all_to_all(array, axis, split_axis=0, concat_axis=0, tiled=True, axis...  28.6 us
    pallas_call x7, Pallas kernels, call(): pl.pallas_call(kernel, out_shape=out_shape, in_specs=specs, out_specs=[VM...  18.6 us
    unnamed x26, local copies, waits for them, and re-layouts  18.2 us
    ppermute x3, starting transfers between devices, shifted(): return lax.ppermute(array, axis, [(i, i + by) for i in range(peers - by)])  11.5 us
    ppermute x1, starting transfers between devices, body(): came = lax.ppermute(item1, 'delay', [(0, 1), (1, 0)])  4.89 us
    ppermute x1, waiting for transfers between devices, body(): came = lax.ppermute(item2, 'delay', [(0, 3), (1, 2), (2, 1)])  4.36 us
  transfers between devices with their start and end apart: 12, of which 9 were waited for; matrix products, arithmetic and copies ran while one was open for 2% of the time, Pallas kernels for 0%

profile of v1, /device:TPU:2, one launch (start us, length us, event | category | flops | bytes accessed | tf_op | source)
XLA Modules:
  0.0 168.9 jit_solution(16326669231738138764)
XLA Ops:
  0.0 3.4 %collective-permute-start = (bf16[64,4,128]{2,1,0:T(4,128)(2,1)}, bf16[64,4,128]{2,1,0:T(4,128)(2,1)S(1)}, u32[]{:S(2)}, u32[]{:S(2)}) collective-permute-start(bf16[64,4,128]{2,1,0:T(4,128)(2,1)} %bitcast.40), channel_id=1, source_target_pairs={{0,1},{1,2},{2,3},{3,4},{4,5},{5,6},{6,7},{7,8},{8,9},{9,10},{10,1... | collective-permute-start | bytes 196616 | tf_op jit(solution)/shard_map/ppermute | solution.py:152
  3.4 4.0 %collective-permute-start.1 = (bf16[64,4,128]{2,1,0:T(4,128)(2,1)}, bf16[64,4,128]{2,1,0:T(4,128)(2,1)S(1)}, u32[]{:S(2)}, u32[]{:S(2)}) collective-permute-start(bf16[64,4,128]{2,1,0:T(4,128)(2,1)} %bitcast.41), channel_id=1, source_target_pairs={{0,2},{1,3},{2,4},{3,5},{4,6},{5,7},{6,8},{7,9},{8,10},{9,11},{10,... | collective-permute-start | bytes 196616 | tf_op jit(solution)/shard_map/ppermute | solution.py:152
  7.4 4.1 %collective-permute-start.2 = (bf16[64,4,128]{2,1,0:T(4,128)(2,1)}, bf16[64,4,128]{2,1,0:T(4,128)(2,1)S(1)}, u32[]{:S(2)}, u32[]{:S(2)}) collective-permute-start(bf16[64,4,128]{2,1,0:T(4,128)(2,1)} %bitcast.42), channel_id=1, source_target_pairs={{0,3},{1,4},{2,5},{3,6},{4,7},{5,8},{6,9},{7,10},{8,11},{9,12},{10... | collective-permute-start | bytes 196616 | tf_op jit(solution)/shard_map/ppermute | solution.py:152
  11.5 0.8 copy.11
  12.3 16.0 %all_to_all.46 = s32[16,1,8]{2,1,0:T(1,128)S(1)} all-to-all(s32[16,1,8]{2,1,0:T(1,128)S(1)} %copy.11), channel_id=1, replica_groups=mesh['rows'=16,'delay'=16] {'rows'}, dimensions={0} | all-to-all | bytes 1024 | tf_op jit(solution)/shard_map/all_to_all | solution.py:156
  28.2 0.0 collective-permute-done.h1
  28.2 0.0 collective-permute-done.1.h2
  28.2 0.0 collective-permute-done.2.h3
  28.2 0.0 copy-start.8
  28.3 0.8 copy-done.8
  29.1 1.0 pick_initial.1
  30.1 18.6 %all_to_all.47 = bf16[16,8,16,128]{3,2,1,0:T(8,128)(2,1)S(1)} all-to-all(bf16[16,8,16,128]{3,2,1,0:T(8,128)(2,1)S(1)} %bitcast.26), channel_id=1, replica_groups=mesh['rows'=16,'delay'=16] {'rows'}, dimensions={0} | all-to-all | bytes 1048576 | tf_op jit(solution)/shard_map/all_to_all | solution.py:156
  48.6 3.4 %copy-done = bf16[1,64,4,128,128]{4,3,2,1,0:T(8,128)(2,1)S(1)} copy-done((bf16[1,64,4,128,128]{4,3,2,1,0:T(8,128)(2,1)S(1)}, bf16[1,64,4,128,128]{4,3,2,1,0:T(8,128)(2,1)}, u32[]{:S(2)}) %copy-start) | copy-done | bytes 8388632
  52.0 0.7 copy-done.11
  52.7 2.7 %initial_terms.1 = bf16[16,256,128]{2,1,0:T(8,128)(2,1)S(1)} custom-call(s32[4,64]{1,0:T(4,128)S(1)} %bitcast.44, bf16[64,4,128,128]{3,2,1,0:T(8,128)(2,1)S(1)} %bitcast.22, bf16[128,16,128]{2,1,0:T(8,128)(2,1)S(1)} %bitcast.27), custom_call_target="tpu_custom_call" | custom-call | tf_op jit(solution)/shard_map/initial_terms/pallas_call | solution.py:31
  55.4 1.0 copy-done.5
  56.4 5.7 %all-to-all-start.2 = ((bf16[16,256,128]{2,1,0:T(8,128)(2,1)}), bf16[16,256,128]{2,1,0:T(8,128)(2,1)S(1)}, u32[]{:S(2)}, u32[]{:S(2)}) async-start(bf16[16,256,128]{2,1,0:T(8,128)(2,1)} %copy-done.5), calls=%async_computation.2 | async-start | bytes 2097152 | tf_op jit(solution)/shard_map/all_to_all | solution.py:156
  62.1 1.8 %fusion = (f32[1,64,4,128]{3,2,1,0:T(4,128)S(1)}, f32[1,64,4,128]{3,2,1,0:T(4,128)S(1)}, f32[1,64,4,128]{3,2,1,0:T(4,128)}, f32[1,64,4,128]{3,2,1,0:T(4,128)S(1)}) fusion(f32[4,64,4,128]{3,2,1,0:T(4,128)} %param.10), kind=kLoop, calls=%fused_computation.2 | loop fusion | bytes 1048576 | tf_op jit(solution)/shard_map/slice | solution.py:239
  63.8 15.0 %all-to-all-done.2.terms = bf16[16,256,128]{2,1,0:T(8,128)(2,1)S(1)} async-done(((bf16[16,256,128]{2,1,0:T(8,128)(2,1)}), bf16[16,256,128]{2,1,0:T(8,128)(2,1)S(1)}, u32[]{:S(2)}, u32[]{:S(2)}) %all-to-all-start.2) | async-done | bytes 1048608 | tf_op jit(solution)/shard_map/all_to_all | solution.py:156
  78.9 0.9 copy-done.6
  79.8 1.5 first_step.1
  81.3 0.6 copy-done.9
  82.0 0.7 copy-done.7
  82.6 3.5 %all-to-all-start.3 = ((bf16[16,8,4,128]{3,2,1,0:T(4,128)(2,1)}), bf16[16,8,4,128]{3,2,1,0:T(4,128)(2,1)S(1)}, u32[]{:S(2)}, u32[]{:S(2)}) async-start(bf16[16,8,4,128]{3,2,1,0:T(4,128)(2,1)} %bitcast.39), calls=%async_computation.3 | async-start | bytes 262144 | tf_op jit(solution)/shard_map/all_to_all | solution.py:156
  86.1 2.3 %collective-permute-start.3 = (bf16[256,128]{1,0:T(8,128)(2,1)}, bf16[256,128]{1,0:T(8,128)(2,1)S(1)}, u32[]{:S(2)}, u32[]{:S(2)}) collective-permute-start(bf16[256,128]{1,0:T(8,128)(2,1)} %copy-done.9), channel_id=1, source_target_pairs={{4,0},{5,1},{6,2},{0,4},{1,5},{2,6},{20,16},{21,17},{22,18},{16,20... | collective-permute-start | bytes 196616 | tf_op jit(solution)/shard_map/ppermute | solution.py:196
  88.4 4.2 %collective-permute-done.3.extra = bf16[256,128]{1,0:T(8,128)(2,1)S(1)} collective-permute-done((bf16[256,128]{1,0:T(8,128)(2,1)}, bf16[256,128]{1,0:T(8,128)(2,1)S(1)}, u32[]{:S(2)}, u32[]{:S(2)}) %collective-permute-start.3) | collective-permute-done | bytes 65568 | tf_op jit(solution)/shard_map/ppermute | solution.py:196
  92.6 2.2 %all-to-all-done.3 = bf16[16,8,4,128]{3,2,1,0:T(4,128)(2,1)S(1)} async-done(((bf16[16,8,4,128]{3,2,1,0:T(4,128)(2,1)}), bf16[16,8,4,128]{3,2,1,0:T(4,128)(2,1)S(1)}, u32[]{:S(2)}, u32[]{:S(2)}) %all-to-all-start.3) | async-done | bytes 131104 | tf_op jit(solution)/shard_map/all_to_all | solution.py:156
  94.7 3.4 %copy-done.1 = bf16[1,64,4,128,128]{4,3,2,1,0:T(8,128)(2,1)S(1)} copy-done((bf16[1,64,4,128,128]{4,3,2,1,0:T(8,128)(2,1)S(1)}, bf16[1,64,4,128,128]{4,3,2,1,0:T(8,128)(2,1)}, u32[]{:S(2)}) %copy-start.1) | copy-done | bytes 8388632
  98.1 4.3 %second_step.1 = (bf16[256,128]{1,0:T(8,128)(2,1)S(1)}, bf16[128,4,128]{2,1,0:T(4,128)(2,1)}) custom-call(s32[1]{0:T(128)} %bitcast.lane, s32[16,8]{1,0:T(8,128)S(1)} %bitcast.37, s32[4,64]{1,0:T(4,128)S(1)} %bitcast.45, bf16[64,4,128,128]{3,2,1,0:T(8,128)(2,1)S(1)} %bitcast.23, bf16[128,4,128]{2,1,0:T(4,128)(2,1)S(1)} %bitcast.29, ...), custom_call_target="tpu_custom_call" | custom-call | tf_op jit(solution)/shard_map/second_step/pallas_call | solution.py:31
  102.4 4.9 %all-to-all-start.4 = ((bf16[16,8,4,128]{3,2,1,0:T(4,128)(2,1)}), bf16[16,8,4,128]{3,2,1,0:T(4,128)(2,1)S(1)}, u32[]{:S(2)}, u32[]{:S(2)}) async-start(bf16[16,8,4,128]{3,2,1,0:T(4,128)(2,1)} %bitcast.14), calls=%async_computation.4 | async-start | bytes 262144 | tf_op jit(solution)/shard_map/all_to_all | solution.py:156
  107.3 4.9 %collective-permute-start.4 = (bf16[256,128]{1,0:T(8,128)(2,1)S(1)}, bf16[256,128]{1,0:T(8,128)(2,1)S(1)}, u32[]{:S(2)}, u32[]{:S(2)}) collective-permute-start(bf16[256,128]{1,0:T(8,128)(2,1)S(1)} %get-tuple-element.14.held), channel_id=1, source_target_pairs={{0,1},{1,0},{16,17},{17,16},{32,33},{33,32},{48,49},{49,48},{64,65... | collective-permute-start | bytes 196616 | tf_op jit(solution)/shard_map/ppermute | solution.py:209
  112.2 2.6 %collective-permute-done.4.extra = bf16[256,128]{1,0:T(8,128)(2,1)S(1)} collective-permute-done((bf16[256,128]{1,0:T(8,128)(2,1)S(1)}, bf16[256,128]{1,0:T(8,128)(2,1)S(1)}, u32[]{:S(2)}, u32[]{:S(2)}) %collective-permute-start.4) | collective-permute-done | bytes 65568 | tf_op jit(solution)/shard_map/ppermute | solution.py:209
  114.9 1.1 all-to-all-done.4
  116.0 3.4 %copy-done.2 = bf16[1,64,4,128,128]{4,3,2,1,0:T(8,128)(2,1)S(1)} copy-done((bf16[1,64,4,128,128]{4,3,2,1,0:T(8,128)(2,1)S(1)}, bf16[1,64,4,128,128]{4,3,2,1,0:T(8,128)(2,1)}, u32[]{:S(2)}) %copy-start.2) | copy-done | bytes 8388632
  119.4 4.3 %third_step.1 = (bf16[256,128]{1,0:T(8,128)(2,1)S(1)}, bf16[128,4,128]{2,1,0:T(4,128)(2,1)}) custom-call(s32[1]{0:T(128)} %bitcast.lane, s32[16,8]{1,0:T(8,128)S(1)} %bitcast.38, s32[4,64]{1,0:T(4,128)S(1)} %bitcast.46, bf16[64,4,128,128]{3,2,1,0:T(8,128)(2,1)S(1)} %bitcast.24, bf16[128,4,128]{2,1,0:T(4,128)(2,1)S(1)} %bitcast.28, ...), custom_call_target="tpu_custom_call" | custom-call | tf_op jit(solution)/shard_map/third_step/pallas_call | solution.py:31
  123.6 5.8 %all-to-all-start.5 = ((bf16[16,8,4,128]{3,2,1,0:T(4,128)(2,1)}), bf16[16,8,4,128]{3,2,1,0:T(4,128)(2,1)S(1)}, u32[]{:S(2)}, u32[]{:S(2)}) async-start(bf16[16,8,4,128]{3,2,1,0:T(4,128)(2,1)} %bitcast.17), calls=%async_computation.5 | async-start | bytes 262144 | tf_op jit(solution)/shard_map/all_to_all | solution.py:156
  129.5 1.9 %collective-permute-start.5 = (bf16[256,128]{1,0:T(8,128)(2,1)S(1)}, bf16[256,128]{1,0:T(8,128)(2,1)S(1)}, u32[]{:S(2)}, u32[]{:S(2)}) collective-permute-start(bf16[256,128]{1,0:T(8,128)(2,1)S(1)} %get-tuple-element.16), channel_id=1, source_target_pairs={{0,3},{1,2},{2,1},{16,19},{17,18},{18,17},{32,35},{33,34},{34,33},... | collective-permute-start | bytes 196616 | tf_op jit(solution)/shard_map/ppermute | solution.py:220
  131.4 4.4 %collective-permute-done.5.extra = bf16[256,128]{1,0:T(8,128)(2,1)S(1)} collective-permute-done((bf16[256,128]{1,0:T(8,128)(2,1)S(1)}, bf16[256,128]{1,0:T(8,128)(2,1)S(1)}, u32[]{:S(2)}, u32[]{:S(2)}) %collective-permute-start.5) | collective-permute-done | bytes 65568 | tf_op jit(solution)/shard_map/ppermute | solution.py:220
  135.7 2.4 %all-to-all-done.5 = bf16[16,8,4,128]{3,2,1,0:T(4,128)(2,1)S(1)} async-done(((bf16[16,8,4,128]{3,2,1,0:T(4,128)(2,1)}), bf16[16,8,4,128]{3,2,1,0:T(4,128)(2,1)S(1)}, u32[]{:S(2)}, u32[]{:S(2)}) %all-to-all-start.5) | async-done | bytes 131104 | tf_op jit(solution)/shard_map/all_to_all | solution.py:156
  138.1 3.4 %copy-done.3 = bf16[1,64,4,128,128]{4,3,2,1,0:T(8,128)(2,1)S(1)} copy-done((bf16[1,64,4,128,128]{4,3,2,1,0:T(8,128)(2,1)S(1)}, bf16[1,64,4,128,128]{4,3,2,1,0:T(8,128)(2,1)}, u32[]{:S(2)}) %copy-start.3) | copy-done | bytes 8388632
  141.5 3.3 %fourth_step.1 = bf16[4,256,128]{2,1,0:T(8,128)(2,1)} custom-call(s32[1]{0:T(128)} %bitcast.lane, s32[4,64]{1,0:T(4,128)S(1)} %bitcast.47, bf16[64,4,128,128]{3,2,1,0:T(8,128)(2,1)S(1)} %bitcast.25, bf16[128,4,128]{2,1,0:T(4,128)(2,1)S(1)} %bitcast.30, bf16[256,128]{1,0:T(8,128)(2,1)S(1)} %collective-permute-done.5.extra), custom_call_target="tpu_custom_call" | custom-call | tf_op jit(solution)/shard_map/fourth_step/pallas_call | solution.py:31
  144.8 3.4 %all-to-all-start.6 = ((bf16[4,256,128]{2,1,0:T(8,128)(2,1)}), bf16[4,256,128]{2,1,0:T(8,128)(2,1)S(1)}, u32[]{:S(2)}, u32[]{:S(2)}) async-start(bf16[4,256,128]{2,1,0:T(8,128)(2,1)} %fourth_step.1), calls=%async_computation.6 | async-start | bytes 524288 | tf_op jit(solution)/shard_map/all_to_all | solution.py:156
  148.3 7.7 %all-to-all-done.6 = bf16[4,256,128]{2,1,0:T(8,128)(2,1)S(1)} async-done(((bf16[4,256,128]{2,1,0:T(8,128)(2,1)}), bf16[4,256,128]{2,1,0:T(8,128)(2,1)S(1)}, u32[]{:S(2)}, u32[]{:S(2)}) %all-to-all-start.6) | async-done | bytes 262176 | tf_op jit(solution)/shard_map/all_to_all | solution.py:156
  156.0 0.7 broadcast_in_dim.3
  156.7 5.3 %all-to-all-start.7 = ((bf16[4,256,128]{2,1,0:T(8,128)(2,1)}), bf16[4,256,128]{2,1,0:T(8,128)(2,1)S(1)}, u32[]{:S(2)}, u32[]{:S(2)}) async-start(bf16[4,256,128]{2,1,0:T(8,128)(2,1)} %broadcast_in_dim.3), calls=%async_computation.7 | async-start | bytes 524288 | tf_op jit(solution)/shard_map/all_to_all | solution.py:156
  162.0 0.0 copy-done.10
  162.0 5.4 %all-to-all-done.7.items = bf16[4,256,128]{2,1,0:T(8,128)(2,1)S(1)} async-done(((bf16[4,256,128]{2,1,0:T(8,128)(2,1)}), bf16[4,256,128]{2,1,0:T(8,128)(2,1)S(1)}, u32[]{:S(2)}, u32[]{:S(2)}) %all-to-all-start.7) | async-done | bytes 262176 | tf_op jit(solution)/shard_map/all_to_all | solution.py:156
  167.4 1.5 last_solve.1
  (16 shorter events, 0.0 us)
Async XLA Ops:
  0.0 28.2 %collective-permute-start = (bf16[64,4,128]{2,1,0:T(4,128)(2,1)}, bf16[64,4,128]{2,1,0:T(4,128)(2,1)S(1)}, u32[]{:S(2)}, u32[]{:S(2)}) collective-permute-start(bf16[64,4,128]{2,1,0:T(4,128)(2,1)} %bitcast.40), channel_id=1, source_target_pairs={{0,1},{1,2},{2,3},{3,4},{4,5},{5,6},{6,7},{7,8},{8,9},{9,10},{10,1... | collective-permute-start | bytes 196616 | tf_op jit(solution)/shard_map/ppermute | solution.py:152
  3.4 24.8 %collective-permute-start.1 = (bf16[64,4,128]{2,1,0:T(4,128)(2,1)}, bf16[64,4,128]{2,1,0:T(4,128)(2,1)S(1)}, u32[]{:S(2)}, u32[]{:S(2)}) collective-permute-start(bf16[64,4,128]{2,1,0:T(4,128)(2,1)} %bitcast.41), channel_id=1, source_target_pairs={{0,2},{1,3},{2,4},{3,5},{4,6},{5,7},{6,8},{7,9},{8,10},{9,11},{10,... | collective-permute-start | bytes 196616 | tf_op jit(solution)/shard_map/ppermute | solution.py:152
  7.4 20.8 %collective-permute-start.2 = (bf16[64,4,128]{2,1,0:T(4,128)(2,1)}, bf16[64,4,128]{2,1,0:T(4,128)(2,1)S(1)}, u32[]{:S(2)}, u32[]{:S(2)}) collective-permute-start(bf16[64,4,128]{2,1,0:T(4,128)(2,1)} %bitcast.42), channel_id=1, source_target_pairs={{0,3},{1,4},{2,5},{3,6},{4,7},{5,8},{6,9},{7,10},{8,11},{9,12},{10... | collective-permute-start | bytes 196616 | tf_op jit(solution)/shard_map/ppermute | solution.py:152
  28.2 0.8 copy-start.8
  48.6 46.1 %copy-start.12 = (s32[1,64,4]{1,2,0:T(4,128)S(1)}, s32[1,64,4]{1,2,0:T(4,128)}, u32[]{:S(2)}) copy-start(s32[1,64,4]{1,2,0:T(4,128)} %param.8) | copy-start | bytes 3076
  48.6 3.4 %copy-start = (bf16[1,64,4,128,128]{4,3,2,1,0:T(8,128)(2,1)S(1)}, bf16[1,64,4,128,128]{4,3,2,1,0:T(8,128)(2,1)}, u32[]{:S(2)}) copy-start(bf16[1,64,4,128,128]{4,3,2,1,0:T(8,128)(2,1)} %param.6) | copy-start | bytes 25165828
  52.0 0.7 copy-start.11
  52.7 26.2 %copy-start.4 = (bf16[64,128,128]{2,1,0:T(8,128)(2,1)S(1)}, bf16[64,128,128]{2,1,0:T(8,128)(2,1)}, u32[]{:S(2)}) copy-start(bf16[64,128,128]{2,1,0:T(8,128)(2,1)} %diag.7) | copy-start | bytes 6291460
  55.4 1.0 copy-start.5
  56.4 22.5 %all-to-all-start.2 = ((bf16[16,256,128]{2,1,0:T(8,128)(2,1)}), bf16[16,256,128]{2,1,0:T(8,128)(2,1)S(1)}, u32[]{:S(2)}, u32[]{:S(2)}) async-start(bf16[16,256,128]{2,1,0:T(8,128)(2,1)} %copy-done.5), calls=%async_computation.2 | async-start | bytes 2097152 | tf_op jit(solution)/shard_map/all_to_all | solution.py:156
  78.9 0.9 copy-start.6
  81.3 0.6 copy-start.9
  82.0 0.7 copy-start.7
  82.6 12.1 %all-to-all-start.3 = ((bf16[16,8,4,128]{3,2,1,0:T(4,128)(2,1)}), bf16[16,8,4,128]{3,2,1,0:T(4,128)(2,1)S(1)}, u32[]{:S(2)}, u32[]{:S(2)}) async-start(bf16[16,8,4,128]{3,2,1,0:T(4,128)(2,1)} %bitcast.39), calls=%async_computation.3 | async-start | bytes 262144 | tf_op jit(solution)/shard_map/all_to_all | solution.py:156
  86.1 6.4 %collective-permute-start.3 = (bf16[256,128]{1,0:T(8,128)(2,1)}, bf16[256,128]{1,0:T(8,128)(2,1)S(1)}, u32[]{:S(2)}, u32[]{:S(2)}) collective-permute-start(bf16[256,128]{1,0:T(8,128)(2,1)} %copy-done.9), channel_id=1, source_target_pairs={{4,0},{5,1},{6,2},{0,4},{1,5},{2,6},{20,16},{21,17},{22,18},{16,20... | collective-permute-start | bytes 196616 | tf_op jit(solution)/shard_map/ppermute | solution.py:196
  94.7 3.4 %copy-start.1 = (bf16[1,64,4,128,128]{4,3,2,1,0:T(8,128)(2,1)S(1)}, bf16[1,64,4,128,128]{4,3,2,1,0:T(8,128)(2,1)}, u32[]{:S(2)}) copy-start(bf16[1,64,4,128,128]{4,3,2,1,0:T(8,128)(2,1)} %param.6) | copy-start | bytes 25165828
  102.4 13.6 %all-to-all-start.4 = ((bf16[16,8,4,128]{3,2,1,0:T(4,128)(2,1)}), bf16[16,8,4,128]{3,2,1,0:T(4,128)(2,1)S(1)}, u32[]{:S(2)}, u32[]{:S(2)}) async-start(bf16[16,8,4,128]{3,2,1,0:T(4,128)(2,1)} %bitcast.14), calls=%async_computation.4 | async-start | bytes 262144 | tf_op jit(solution)/shard_map/all_to_all | solution.py:156
  107.3 7.5 %collective-permute-start.4 = (bf16[256,128]{1,0:T(8,128)(2,1)S(1)}, bf16[256,128]{1,0:T(8,128)(2,1)S(1)}, u32[]{:S(2)}, u32[]{:S(2)}) collective-permute-start(bf16[256,128]{1,0:T(8,128)(2,1)S(1)} %get-tuple-element.14.held), channel_id=1, source_target_pairs={{0,1},{1,0},{16,17},{17,16},{32,33},{33,32},{48,49},{49,48},{64,65... | collective-permute-start | bytes 196616 | tf_op jit(solution)/shard_map/ppermute | solution.py:209
  116.0 3.4 %copy-start.2 = (bf16[1,64,4,128,128]{4,3,2,1,0:T(8,128)(2,1)S(1)}, bf16[1,64,4,128,128]{4,3,2,1,0:T(8,128)(2,1)}, u32[]{:S(2)}) copy-start(bf16[1,64,4,128,128]{4,3,2,1,0:T(8,128)(2,1)} %param.6) | copy-start | bytes 25165828
  119.4 42.6 %copy-start.10 = (bf16[256,128]{1,0:T(8,128)(2,1)S(1)}, bf16[256,128]{1,0:T(8,128)(2,1)}, u32[]{:S(2)}) copy-start(bf16[256,128]{1,0:T(8,128)(2,1)} %copy-done.9) | copy-start | bytes 196612
  123.6 14.5 %all-to-all-start.5 = ((bf16[16,8,4,128]{3,2,1,0:T(4,128)(2,1)}), bf16[16,8,4,128]{3,2,1,0:T(4,128)(2,1)S(1)}, u32[]{:S(2)}, u32[]{:S(2)}) async-start(bf16[16,8,4,128]{3,2,1,0:T(4,128)(2,1)} %bitcast.17), calls=%async_computation.5 | async-start | bytes 262144 | tf_op jit(solution)/shard_map/all_to_all | solution.py:156
  129.5 6.3 %collective-permute-start.5 = (bf16[256,128]{1,0:T(8,128)(2,1)S(1)}, bf16[256,128]{1,0:T(8,128)(2,1)S(1)}, u32[]{:S(2)}, u32[]{:S(2)}) collective-permute-start(bf16[256,128]{1,0:T(8,128)(2,1)S(1)} %get-tuple-element.16), channel_id=1, source_target_pairs={{0,3},{1,2},{2,1},{16,19},{17,18},{18,17},{32,35},{33,34},{34,33},... | collective-permute-start | bytes 196616 | tf_op jit(solution)/shard_map/ppermute | solution.py:220
  138.1 3.4 %copy-start.3 = (bf16[1,64,4,128,128]{4,3,2,1,0:T(8,128)(2,1)S(1)}, bf16[1,64,4,128,128]{4,3,2,1,0:T(8,128)(2,1)}, u32[]{:S(2)}) copy-start(bf16[1,64,4,128,128]{4,3,2,1,0:T(8,128)(2,1)} %param.6) | copy-start | bytes 25165828
  144.8 11.1 %all-to-all-start.6 = ((bf16[4,256,128]{2,1,0:T(8,128)(2,1)}), bf16[4,256,128]{2,1,0:T(8,128)(2,1)S(1)}, u32[]{:S(2)}, u32[]{:S(2)}) async-start(bf16[4,256,128]{2,1,0:T(8,128)(2,1)} %fourth_step.1), calls=%async_computation.6 | async-start | bytes 524288 | tf_op jit(solution)/shard_map/all_to_all | solution.py:156
  156.7 10.7 %all-to-all-start.7 = ((bf16[4,256,128]{2,1,0:T(8,128)(2,1)}), bf16[4,256,128]{2,1,0:T(8,128)(2,1)S(1)}, u32[]{:S(2)}, u32[]{:S(2)}) async-start(bf16[4,256,128]{2,1,0:T(8,128)(2,1)} %broadcast_in_dim.3), calls=%async_computation.7 | async-start | bytes 524288 | tf_op jit(solution)/shard_map/all_to_all | solution.py:156

commit v2 on v1

--- a/solution.py
+++ b/solution.py
@@ -4,6 +4,7 @@
 from jax.experimental import pallas as pl
 from jax.experimental.pallas import tpu as pltpu
 from jax.sharding import PartitionSpec as P
+
 
 STEPS = 4
 LANES = 16
@@ -25,7 +26,7 @@
 LIMIT = 24 * 1024 * 1024
 
 
-def call(kernel, out_shape, scratch, operands, in_smem, name):
+def call(kernel, out_shape, scratch, operands, in_smem):
     specs = [SMEM if i in in_smem else VMEM for i in range(len(operands))]
     many = isinstance(out_shape, (tuple, list))
     return pl.pallas_call(
@@ -35,11 +36,10 @@
         out_specs=[VMEM] * len(out_shape) if many else VMEM,
         scratch_shapes=scratch,
         compiler_params=pltpu.CompilerParams(vmem_limit_bytes=LIMIT),
-        name=name,
     )(*operands)
 
 
-def pick_initial(asked, h0, h1, h2, h3, out, wide, packed):
+def pick_initial(lane, asked, h0, h1, h2, h3, out, wide, packed):
     for t, h in enumerate((h0, h1, h2, h3)):
         wide[:, EXC * t : EXC * (t + 1), :] = h[...].astype(f32)
     packed[...] = wide[...].astype(bf16)
@@ -87,7 +87,7 @@
     total = terms[0].astype(f32)
     for k in range(1, LANES):
         total = total + terms[k].astype(f32)
-    value = excite[...] - total
+    value = excite[0] - total
     driven[...] = value
     me = lane[0]
     spare = (me >= SPARE[0]) & (me <= SPARE[-1])
@@ -106,27 +106,24 @@
             total[pl.ds(at + EXC * j, EXC), :] = jnp.dot(row, tile, preferred_element_type=f32)
 
 
-def second_step(lane, asked, slots, tiles, arrived, extra, excite, diag, item, send, total, driven, solved):
-    tile_terms(slots, tiles, arrived, total)
+def second_step(lane, asked, total, extra, excite, diag, item, send, driven, solved):
     value = total[...] + extra[...].astype(f32)
-    rest = excite[...] - value
+    rest = excite[1] - value
     driven[...] = rest
     item[...] = jnp.where(lane[0] == 0, rest, value).astype(bf16)
     solve_and_pick(asked, driven, diag, solved, send)
 
 
-def third_step(lane, asked, slots, tiles, arrived, extra, held, excite, diag, item, send, total, driven, solved):
-    tile_terms(slots, tiles, arrived, total)
+def third_step(lane, asked, total, extra, held, excite, diag, item, send, driven, solved):
     me = lane[0]
     came = extra[...].astype(f32)
-    rest = jnp.where(me == 0, excite[...] - (total[...] + came), came)
+    rest = jnp.where(me == 0, excite[2] - (total[...] + came), came)
     driven[...] = rest
     item[...] = jnp.where(me == 2, held[...].astype(f32), rest).astype(bf16)
     solve_and_pick(asked, driven, diag, solved, send)
 
 
-def fourth_step(lane, slots, tiles, arrived, extra, out, total):
-    tile_terms(slots, tiles, arrived, total)
+def fourth_step(lane, total, extra, out):
     me = lane[0]
     came = extra[...].astype(f32)
     value = jnp.where(me == 0, total[...], jnp.where(me == 1, total[...] + came, came)).astype(bf16)
@@ -134,11 +131,18 @@
         out[y] = value
 
 
-def last_solve(item0, items, excite, diag, out, driven):
-    driven[0] = item0[...].astype(f32)
+def repeat(column, out):
+    for x in range(4):
+        out[x] = column[0]
+
+
+def last_solve(lane, item0, came, items, excite, diag, out, driven):
+    me = lane[0]
+    spare = (me >= SPARE[0]) & (me <= SPARE[-1])
+    driven[0] = jnp.where(spare, came[...].astype(f32), item0[...].astype(f32))
     driven[1] = items[2].astype(f32)
     driven[2] = items[3].astype(f32)
-    driven[3] = excite[...] - (items[0].astype(f32) + items[1].astype(f32))
+    driven[3] = excite[3] - (items[0].astype(f32) + items[1].astype(f32))
     for i in range(NB):
         rows = [driven[t, EXC * i : EXC * (i + 1), :] for t in range(STEPS)]
         both = jnp.concatenate(rows, axis=0).astype(bf16)
@@ -165,15 +169,16 @@
 
     asked = exchange(wanted_blocks[0, 0], "rows")
     h0 = history_init[0]
-    later = [shifted(h0, "delay", t) for t in range(1, STEPS)]
+    later = []
+    for t in range(1, STEPS):
+        later.append(shifted(h0, "delay", t))
 
     picked = call(
         pick_initial,
         sds((TAKEN, EXC * STEPS, B), bf16),
         [pltpu.VMEM((NB, EXC * STEPS, B), f32), pltpu.VMEM((NB, EXC * STEPS, B), bf16)],
-        (asked, h0, *later),
-        (0,),
-        "pick_initial",
+        (lane, asked, h0, *later),
+        (0, 1),
     )
     arrived = exchange(picked.reshape(ROWS, CAP, EXC * STEPS, B), "rows").reshape(TAKEN, EXC * STEPS, B)
     terms = call(
@@ -182,7 +187,6 @@
         [pltpu.VMEM((STEPS, FLAT, B), f32)],
         (slots, tiles, arrived),
         (0,),
-        "initial_terms",
     )
     terms = exchange(terms, "delay")
 
@@ -190,55 +194,43 @@
     block = pltpu.VMEM((NB, EXC, B), f32)
     outs = (sds((FLAT, B), bf16), sds((TAKEN, EXC, B), bf16))
 
-    item, send = call(
-        first_step, outs, [flat, block], (lane, asked, terms, excite[0], diag_inverse), (0, 1), "first_step"
-    )
-    came = lax.ppermute(item, "delay", [(4, 0), (5, 1), (6, 2), (0, 4), (1, 5), (2, 6)])
+    item0, send = call(
+        first_step, outs, [flat, block], (lane, asked, terms, excite, diag_inverse), (0, 1)
+    )
+    came0 = lax.ppermute(item0, "delay", [(4, 0), (5, 1), (6, 2), (0, 4), (1, 5), (2, 6)])
     arrived = exchange(send.reshape(ROWS, CAP, EXC, B), "rows").reshape(TAKEN, EXC, B)
-    me = lane[0]
-    item0 = jnp.where((me >= SPARE[0]) & (me <= SPARE[-1]), came, item)
+    total = call(tile_terms, sds((FLAT, B), f32), [], (slots, tiles, arrived), (0,))
 
     item1, send = call(
-        second_step,
-        outs,
-        [flat, flat, block],
-        (lane, asked, slots, tiles, arrived, came, excite[1], diag_inverse),
-        (0, 1, 2),
-        "second_step",
+        second_step, outs, [flat, block], (lane, asked, total, came0, excite, diag_inverse), (0, 1)
     )
     came = lax.ppermute(item1, "delay", [(0, 1), (1, 0)])
     arrived = exchange(send.reshape(ROWS, CAP, EXC, B), "rows").reshape(TAKEN, EXC, B)
+    total = call(tile_terms, sds((FLAT, B), f32), [], (slots, tiles, arrived), (0,))
 
     item2, send = call(
         third_step,
         outs,
-        [flat, flat, block],
-        (lane, asked, slots, tiles, arrived, came, item1, excite[2], diag_inverse),
-        (0, 1, 2),
-        "third_step",
+        [flat, block],
+        (lane, asked, total, came, item1, excite, diag_inverse),
+        (0, 1),
     )
     came = lax.ppermute(item2, "delay", [(0, 3), (1, 2), (2, 1)])
     arrived = exchange(send.reshape(ROWS, CAP, EXC, B), "rows").reshape(TAKEN, EXC, B)
-
-    item3 = call(
-        fourth_step,
-        sds((4, FLAT, B), bf16),
-        [flat],
-        (lane, slots, tiles, arrived, came),
-        (0, 1),
-        "fourth_step",
-    )
+    total = call(tile_terms, sds((FLAT, B), f32), [], (slots, tiles, arrived), (0,))
+
+    item3 = call(fourth_step, sds((4, FLAT, B), bf16), [], (lane, total, came), (0,))
     along_y = [[4 * y + x for y in range(4)] for x in range(4)]
     along_x = [[4 * y + x for x in range(4)] for y in range(4)]
-    column = exchange(item3, "delay", along_y)[0]
-    items = exchange(jnp.broadcast_to(column, (4, FLAT, B)), "delay", along_x)
+    column = exchange(item3, "delay", along_y)
+    column = call(repeat, sds((4, FLAT, B), bf16), [], (column,), ())
+    items = exchange(column, "delay", along_x)
     return call(
         last_solve,
         sds((STEPS, NB, EXC, B), f32),
         [pltpu.VMEM((STEPS, FLAT, B), f32)],
-        (item0, items, excite[3], diag_inverse),
-        (),
-        "last_solve",
+        (lane, item0, came0, items, excite, diag_inverse),
+        (0,),
     )
 
 

time: 170 us -> 161 us (0.947)
  blocking collectives: 34.5 us -> 60 us
  waiting for transfers between devices: 45 us -> 25.5 us
  starting transfers between devices: 49.1 us -> 38.5 us
  local copies, waits for them, and re-layouts: 21.5 us -> 16.4 us
    all_to_all x2 -> x4, blocking collectives: 34.5 us -> 60 us  [exchange(): lax.all_to_all(array, axis, split_axis=0, concat_axis=0, tiled=True, axis...]
    all_to_all x6 -> x4, starting transfers between devices: 28.6 us -> 19.1 us  [exchange(): lax.all_to_all(array, axis, split_axis=0, concat_axis=0, tiled=True, axis...]
    all_to_all x6 -> x4, waiting for transfers between devices: 33.8 us -> 25.5 us  [exchange(): lax.all_to_all(array, axis, split_axis=0, concat_axis=0, tiled=True, axis...]
    ppermute x1, waiting for transfers between devices: 4.36 us -> 0.01 us  [body(): came = lax.ppermute(item2, 'delay', [(0, 3), (1, 2), (2, 1)])]
    ppermute x1, waiting for transfers between devices: 4.15 us -> 0.01 us  [body(): lax.ppermute(item0, 'delay', [(4, 0), (5, 1), (6, 2), (0, 4), (1, 5), (2,...]
    unnamed x26 -> x18, local copies, waits for them, and re-layouts: 18.2 us -> 15.1 us
    ppermute x1, waiting for transfers between devices: 2.64 us -> 0.01 us  [body(): came = lax.ppermute(item1, 'delay', [(0, 1), (1, 0)])]
    slice x1 -> x0, local copies, waits for them, and re-layouts: 1.79 us -> none  [body(): excite[3]]
  transfers between devices with their start and end apart: 12 -> 10, of which waited for: 9 -> 4; matrix products, arithmetic and copies ran while one was open for 2% -> 1% of each run, Pallas kernels for 0% -> 5%
where the time goes in v2:
time: 161 us; the launch traced here: 160 us
  blocking collectives  60 us (37%)
  starting transfers between devices  38.5 us (24%)
  waiting for transfers between devices  25.5 us (16%)
  Pallas kernels  19.7 us (12%)
  local copies, waits for them, and re-layouts  16.4 us (10%)
    all_to_all x4, blocking collectives, exchange(): lax.all_to_all(array, axis, split_axis=0, concat_axis=0, tiled=True, axis...  60 us
    all_to_all x4, waiting for transfers between devices, exchange(): lax.all_to_all(array, axis, split_axis=0, concat_axis=0, tiled=True, axis...  25.5 us
    pallas_call x11, Pallas kernels, call(): pl.pallas_call(kernel, out_shape=out_shape, in_specs=specs, out_specs=[VM...  19.7 us
    all_to_all x4, starting transfers between devices, exchange(): lax.all_to_all(array, axis, split_axis=0, concat_axis=0, tiled=True, axis...  19.1 us
    unnamed x18, local copies, waits for them, and re-layouts  15.1 us
    ppermute x3, starting transfers between devices, shifted(): return lax.ppermute(array, axis, [(i, i + by) for i in range(peers - by)])  11.6 us
    ppermute x1, starting transfers between devices, body(): came = lax.ppermute(item1, 'delay', [(0, 1), (1, 0)])  3.37 us
  transfers between devices with their start and end apart: 10, of which 4 were waited for; matrix products, arithmetic and copies ran while one was open for 1% of the time, Pallas kernels for 5%

profile of v2, /device:TPU:2, one launch (start us, length us, event | category | flops | bytes accessed | tf_op | source)
XLA Modules:
  0.0 160.4 jit_solution(16821177925482115488)
XLA Ops:
  0.0 3.6 %collective-permute-start.2 = (bf16[64,4,128]{2,1,0:T(4,128)(2,1)}, bf16[64,4,128]{2,1,0:T(4,128)(2,1)S(1)}, u32[]{:S(2)}, u32[]{:S(2)}) collective-permute-start(bf16[64,4,128]{2,1,0:T(4,128)(2,1)} %bitcast.34), channel_id=1, source_target_pairs={{0,3},{1,4},{2,5},{3,6},{4,7},{5,8},{6,9},{7,10},{8,11},{9,12},{10... | collective-permute-start | bytes 196616 | tf_op jit(solution)/shard_map/ppermute | solution.py:156
  3.6 4.3 %collective-permute-start.1 = (bf16[64,4,128]{2,1,0:T(4,128)(2,1)}, bf16[64,4,128]{2,1,0:T(4,128)(2,1)S(1)}, u32[]{:S(2)}, u32[]{:S(2)}) collective-permute-start(bf16[64,4,128]{2,1,0:T(4,128)(2,1)} %bitcast.35), channel_id=1, source_target_pairs={{0,2},{1,3},{2,4},{3,5},{4,6},{5,7},{6,8},{7,9},{8,10},{9,11},{10,... | collective-permute-start | bytes 196616 | tf_op jit(solution)/shard_map/ppermute | solution.py:156
  7.9 3.7 %collective-permute-start = (bf16[64,4,128]{2,1,0:T(4,128)(2,1)}, bf16[64,4,128]{2,1,0:T(4,128)(2,1)S(1)}, u32[]{:S(2)}, u32[]{:S(2)}) collective-permute-start(bf16[64,4,128]{2,1,0:T(4,128)(2,1)} %bitcast.36), channel_id=1, source_target_pairs={{0,1},{1,2},{2,3},{3,4},{4,5},{5,6},{6,7},{7,8},{8,9},{9,10},{10,1... | collective-permute-start | bytes 196616 | tf_op jit(solution)/shard_map/ppermute | solution.py:156
  11.6 1.4 copy.11
  13.0 8.6 %all-to-all-start = ((s32[16,1,8]{2,1,0:T(1,128)}), s32[16,1,8]{2,1,0:T(1,128)S(1)}, u32[]{:S(2)}, u32[]{:S(2)}) async-start(s32[16,1,8]{2,1,0:T(1,128)} %copy.11), calls=%async_computation | async-start | bytes 16384 | tf_op jit(solution)/shard_map/all_to_all | solution.py:160
  21.6 7.5 %all-to-all-done = s32[16,1,8]{2,1,0:T(1,128)S(1)} async-done(((s32[16,1,8]{2,1,0:T(1,128)}), s32[16,1,8]{2,1,0:T(1,128)S(1)}, u32[]{:S(2)}, u32[]{:S(2)}) %all-to-all-start) | async-done | bytes 544 | tf_op jit(solution)/shard_map/all_to_all | solution.py:160
  29.1 0.0 collective-permute-done.2.h3
  29.1 0.0 collective-permute-done.1.h2
  29.1 0.0 collective-permute-done.h1
  29.1 0.0 copy-start.6
  29.1 0.8 copy-done.6
  30.0 1.0 shard_map.64
  30.9 0.0 copy-start.8
  31.0 18.6 %all_to_all.46 = bf16[16,8,16,128]{3,2,1,0:T(8,128)(2,1)S(1)} all-to-all(bf16[16,8,16,128]{3,2,1,0:T(8,128)(2,1)S(1)} %bitcast.25), channel_id=1, replica_groups=mesh['rows'=16,'delay'=16] {'rows'}, dimensions={0} | all-to-all | bytes 1048576 | tf_op jit(solution)/shard_map/all_to_all | solution.py:160
  49.5 0.0 copy-start
  49.5 3.4 %copy-done = bf16[1,64,4,128,128]{4,3,2,1,0:T(8,128)(2,1)S(1)} copy-done((bf16[1,64,4,128,128]{4,3,2,1,0:T(8,128)(2,1)S(1)}, bf16[1,64,4,128,128]{4,3,2,1,0:T(8,128)(2,1)}, u32[]{:S(2)}) %copy-start) | copy-done | bytes 8388632
  52.9 0.0 copy-start.7
  52.9 0.7 copy-done.7
  53.6 0.0 copy-start.4
  53.6 2.7 %shard_map.65 = bf16[16,256,128]{2,1,0:T(8,128)(2,1)S(1)} custom-call(s32[4,64]{1,0:T(4,128)S(1)} %bitcast.38, bf16[64,4,128,128]{3,2,1,0:T(8,128)(2,1)S(1)} %bitcast.17, bf16[128,16,128]{2,1,0:T(8,128)(2,1)S(1)} %bitcast.26), custom_call_target="tpu_custom_call" | custom-call | tf_op jit(solution)/shard_map/pallas_call | solution.py:32
  56.3 22.3 %all_to_all.47.terms = bf16[16,256,128]{2,1,0:T(8,128)(2,1)S(1)} all-to-all(bf16[16,256,128]{2,1,0:T(8,128)(2,1)S(1)} %shard_map.65), channel_id=1, replica_groups=mesh['rows'=16,'delay'=16] {'delay'}, dimensions={0} | all-to-all | bytes 2097152 | tf_op jit(solution)/shard_map/all_to_all | solution.py:160
  78.6 0.0 copy-done.5
  78.6 0.0 copy-done.4
  78.6 2.2 %shard_map.66 = (bf16[256,128]{1,0:T(8,128)(2,1)S(1)}, bf16[128,4,128]{2,1,0:T(4,128)(2,1)}) custom-call(s32[1]{0:T(128)} %bitcast.lane, s32[16,8]{1,0:T(8,128)S(1)} %bitcast.31, bf16[16,256,128]{2,1,0:T(8,128)(2,1)S(1)} %all_to_all.47.terms, f32[4,256,128]{2,1,0:T(8,128)S(1)} %bitcast.21, bf16[64,128,128]{2,1,0:T(8,128)(2,1)S(1)} %copy-done.4), custom_call_target="tpu_custom_call" | custom-call | tf_op jit(solution)/shard_map/pallas_call | solution.py:32
  80.8 3.5 %all-to-all-start.3 = ((bf16[16,8,4,128]{3,2,1,0:T(4,128)(2,1)}), bf16[16,8,4,128]{3,2,1,0:T(4,128)(2,1)S(1)}, u32[]{:S(2)}, u32[]{:S(2)}) async-start(bf16[16,8,4,128]{3,2,1,0:T(4,128)(2,1)} %bitcast.11), calls=%async_computation.3 | async-start | bytes 262144 | tf_op jit(solution)/shard_map/all_to_all | solution.py:160
  84.3 1.9 %collective-permute-start.3 = (bf16[256,128]{1,0:T(8,128)(2,1)S(1)}, bf16[256,128]{1,0:T(8,128)(2,1)S(1)}, u32[]{:S(2)}, u32[]{:S(2)}) collective-permute-start(bf16[256,128]{1,0:T(8,128)(2,1)S(1)} %get-tuple-element.11.item0), channel_id=1, source_target_pairs={{4,0},{5,1},{6,2},{0,4},{1,5},{2,6},{20,16},{21,17},{22,18},{16,20... | collective-permute-start | bytes 196616 | tf_op jit(solution)/shard_map/ppermute | solution.py:200
  86.3 6.7 %all-to-all-done.3 = bf16[16,8,4,128]{3,2,1,0:T(4,128)(2,1)S(1)} async-done(((bf16[16,8,4,128]{3,2,1,0:T(4,128)(2,1)}), bf16[16,8,4,128]{3,2,1,0:T(4,128)(2,1)S(1)}, u32[]{:S(2)}, u32[]{:S(2)}) %all-to-all-start.3) | async-done | bytes 131104 | tf_op jit(solution)/shard_map/all_to_all | solution.py:160
  93.0 0.0 copy-done.8
  93.0 3.4 %copy-done.1 = bf16[1,64,4,128,128]{4,3,2,1,0:T(8,128)(2,1)S(1)} copy-done((bf16[1,64,4,128,128]{4,3,2,1,0:T(8,128)(2,1)S(1)}, bf16[1,64,4,128,128]{4,3,2,1,0:T(8,128)(2,1)}, u32[]{:S(2)}) %copy-start.1) | copy-done | bytes 8388632
  96.3 2.6 %shard_map.67.total = f32[256,128]{1,0:T(8,128)S(1)} custom-call(s32[4,64]{1,0:T(4,128)S(1)} %bitcast.39, bf16[64,4,128,128]{3,2,1,0:T(8,128)(2,1)S(1)} %bitcast.18, bf16[128,4,128]{2,1,0:T(4,128)(2,1)S(1)} %bitcast.27), custom_call_target="tpu_custom_call" | custom-call | tf_op jit(solution)/shard_map/pallas_call | solution.py:32
  98.9 0.0 collective-permute-done.3.extra.came
  98.9 2.2 %shard_map.68 = (bf16[256,128]{1,0:T(8,128)(2,1)S(1)}, bf16[128,4,128]{2,1,0:T(4,128)(2,1)}) custom-call(s32[1]{0:T(128)} %bitcast.lane, s32[16,8]{1,0:T(8,128)S(1)} %bitcast.32, f32[256,128]{1,0:T(8,128)S(1)} %shard_map.67.total, bf16[256,128]{1,0:T(8,128)(2,1)S(1)} %collective-permute-done.3.extra.came, f32[4,256,128]{2,1,0:T(8,128)S(1)} %bitcast.22, ...), custom_call_target="tpu_custom_call" | custom-call | tf_op jit(solution)/shard_map/pallas_call | solution.py:32
  101.2 3.5 %all-to-all-start.4 = ((bf16[16,8,4,128]{3,2,1,0:T(4,128)(2,1)}), bf16[16,8,4,128]{3,2,1,0:T(4,128)(2,1)S(1)}, u32[]{:S(2)}, u32[]{:S(2)}) async-start(bf16[16,8,4,128]{3,2,1,0:T(4,128)(2,1)} %bitcast.13), calls=%async_computation.4 | async-start | bytes 262144 | tf_op jit(solution)/shard_map/all_to_all | solution.py:160
  104.7 3.4 %collective-permute-start.4 = (bf16[256,128]{1,0:T(8,128)(2,1)S(1)}, bf16[256,128]{1,0:T(8,128)(2,1)S(1)}, u32[]{:S(2)}, u32[]{:S(2)}) collective-permute-start(bf16[256,128]{1,0:T(8,128)(2,1)S(1)} %get-tuple-element.14.held), channel_id=1, source_target_pairs={{0,1},{1,0},{16,17},{17,16},{32,33},{33,32},{48,49},{49,48},{64,65... | collective-permute-start | bytes 196616 | tf_op jit(solution)/shard_map/ppermute | solution.py:207
  108.1 5.2 %all-to-all-done.4 = bf16[16,8,4,128]{3,2,1,0:T(4,128)(2,1)S(1)} async-done(((bf16[16,8,4,128]{3,2,1,0:T(4,128)(2,1)}), bf16[16,8,4,128]{3,2,1,0:T(4,128)(2,1)S(1)}, u32[]{:S(2)}, u32[]{:S(2)}) %all-to-all-start.4) | async-done | bytes 131104 | tf_op jit(solution)/shard_map/all_to_all | solution.py:160
  113.3 3.4 %copy-done.2 = bf16[1,64,4,128,128]{4,3,2,1,0:T(8,128)(2,1)S(1)} copy-done((bf16[1,64,4,128,128]{4,3,2,1,0:T(8,128)(2,1)S(1)}, bf16[1,64,4,128,128]{4,3,2,1,0:T(8,128)(2,1)}, u32[]{:S(2)}) %copy-start.2) | copy-done | bytes 8388632
  116.7 2.6 %shard_map.69.total = f32[256,128]{1,0:T(8,128)S(1)} custom-call(s32[4,64]{1,0:T(4,128)S(1)} %bitcast.40, bf16[64,4,128,128]{3,2,1,0:T(8,128)(2,1)S(1)} %bitcast.19, bf16[128,4,128]{2,1,0:T(4,128)(2,1)S(1)} %bitcast.28), custom_call_target="tpu_custom_call" | custom-call | tf_op jit(solution)/shard_map/pallas_call | solution.py:32
  119.3 0.0 collective-permute-done.4.extra
  119.3 2.2 %shard_map.70 = (bf16[256,128]{1,0:T(8,128)(2,1)S(1)}, bf16[128,4,128]{2,1,0:T(4,128)(2,1)}) custom-call(s32[1]{0:T(128)} %bitcast.lane, s32[16,8]{1,0:T(8,128)S(1)} %bitcast.33, f32[256,128]{1,0:T(8,128)S(1)} %shard_map.69.total, bf16[256,128]{1,0:T(8,128)(2,1)S(1)} %collective-permute-done.4.extra, bf16[256,128]{1,0:T(8,128)(2,1)S(1)} %get-tuple-element.14.held, ...), custom_call_target="tpu_custom_call" | custom-call | tf_op jit(solution)/shard_map/pallas_call | solution.py:32
  121.5 3.5 %all-to-all-start.5 = ((bf16[16,8,4,128]{3,2,1,0:T(4,128)(2,1)}), bf16[16,8,4,128]{3,2,1,0:T(4,128)(2,1)S(1)}, u32[]{:S(2)}, u32[]{:S(2)}) async-start(bf16[16,8,4,128]{3,2,1,0:T(4,128)(2,1)} %bitcast.15), calls=%async_computation.5 | async-start | bytes 262144 | tf_op jit(solution)/shard_map/all_to_all | solution.py:160
  125.0 2.5 %collective-permute-start.5 = (bf16[256,128]{1,0:T(8,128)(2,1)S(1)}, bf16[256,128]{1,0:T(8,128)(2,1)S(1)}, u32[]{:S(2)}, u32[]{:S(2)}) collective-permute-start(bf16[256,128]{1,0:T(8,128)(2,1)S(1)} %get-tuple-element.16), channel_id=1, source_target_pairs={{0,3},{1,2},{2,1},{16,19},{17,18},{18,17},{32,35},{33,34},{34,33},... | collective-permute-start | bytes 196616 | tf_op jit(solution)/shard_map/ppermute | solution.py:218
  127.5 6.1 %all-to-all-done.5 = bf16[16,8,4,128]{3,2,1,0:T(4,128)(2,1)S(1)} async-done(((bf16[16,8,4,128]{3,2,1,0:T(4,128)(2,1)}), bf16[16,8,4,128]{3,2,1,0:T(4,128)(2,1)S(1)}, u32[]{:S(2)}, u32[]{:S(2)}) %all-to-all-start.5) | async-done | bytes 131104 | tf_op jit(solution)/shard_map/all_to_all | solution.py:160
  133.6 3.4 %copy-done.3 = bf16[1,64,4,128,128]{4,3,2,1,0:T(8,128)(2,1)S(1)} copy-done((bf16[1,64,4,128,128]{4,3,2,1,0:T(8,128)(2,1)S(1)}, bf16[1,64,4,128,128]{4,3,2,1,0:T(8,128)(2,1)}, u32[]{:S(2)}) %copy-start.3) | copy-done | bytes 8388632
  137.0 2.6 %shard_map.71.total = f32[256,128]{1,0:T(8,128)S(1)} custom-call(s32[4,64]{1,0:T(4,128)S(1)} %bitcast.41, bf16[64,4,128,128]{3,2,1,0:T(8,128)(2,1)S(1)} %bitcast.20, bf16[128,4,128]{2,1,0:T(4,128)(2,1)S(1)} %bitcast.29), custom_call_target="tpu_custom_call" | custom-call | tf_op jit(solution)/shard_map/pallas_call | solution.py:32
  139.6 0.0 collective-permute-done.5.extra
  139.7 10.1 %all_to_all.48.column = bf16[4,256,128]{2,1,0:T(8,128)(2,1)S(1)} all-to-all(bf16[4,256,128]{2,1,0:T(8,128)(2,1)S(1)} %shard_map.72), channel_id=1, replica_groups={{0,4,8,12},{1,5,9,13},{2,6,10,14},{3,7,11,15},{16,20,24,28},{17,21,25,2..., dimensions={0} | all-to-all | bytes 524288 | tf_op jit(solution)/shard_map/all_to_all | solution.py:160
  149.8 9.1 %all_to_all.49.items = bf16[4,256,128]{2,1,0:T(8,128)(2,1)S(1)} all-to-all(bf16[4,256,128]{2,1,0:T(8,128)(2,1)S(1)} %shard_map.73), channel_id=1, replica_groups={{0,1,2,3},{4,5,6,7},{8,9,10,11},{12,13,14,15},{16,17,18,19},{20,21,22,2..., dimensions={0} | all-to-all | bytes 524288 | tf_op jit(solution)/shard_map/all_to_all | solution.py:160
  158.9 1.5 shard_map.74
  (6 shorter events, 0.1 us)
Async XLA Ops:
  0.0 78.6 %copy-start.5 = (f32[4,64,4,128]{3,2,1,0:T(4,128)S(1)}, f32[4,64,4,128]{3,2,1,0:T(4,128)}, u32[]{:S(2)}) copy-start(f32[4,64,4,128]{3,2,1,0:T(4,128)} %param.10) | copy-start | bytes 1572868
  0.0 29.1 %collective-permute-start.2 = (bf16[64,4,128]{2,1,0:T(4,128)(2,1)}, bf16[64,4,128]{2,1,0:T(4,128)(2,1)S(1)}, u32[]{:S(2)}, u32[]{:S(2)}) collective-permute-start(bf16[64,4,128]{2,1,0:T(4,128)(2,1)} %bitcast.34), channel_id=1, source_target_pairs={{0,3},{1,4},{2,5},{3,6},{4,7},{5,8},{6,9},{7,10},{8,11},{9,12},{10... | collective-permute-start | bytes 196616 | tf_op jit(solution)/shard_map/ppermute | solution.py:156
  3.6 25.5 %collective-permute-start.1 = (bf16[64,4,128]{2,1,0:T(4,128)(2,1)}, bf16[64,4,128]{2,1,0:T(4,128)(2,1)S(1)}, u32[]{:S(2)}, u32[]{:S(2)}) collective-permute-start(bf16[64,4,128]{2,1,0:T(4,128)(2,1)} %bitcast.35), channel_id=1, source_target_pairs={{0,2},{1,3},{2,4},{3,5},{4,6},{5,7},{6,8},{7,9},{8,10},{9,11},{10,... | collective-permute-start | bytes 196616 | tf_op jit(solution)/shard_map/ppermute | solution.py:156
  7.9 21.2 %collective-permute-start = (bf16[64,4,128]{2,1,0:T(4,128)(2,1)}, bf16[64,4,128]{2,1,0:T(4,128)(2,1)S(1)}, u32[]{:S(2)}, u32[]{:S(2)}) collective-permute-start(bf16[64,4,128]{2,1,0:T(4,128)(2,1)} %bitcast.36), channel_id=1, source_target_pairs={{0,1},{1,2},{2,3},{3,4},{4,5},{5,6},{6,7},{7,8},{8,9},{9,10},{10,1... | collective-permute-start | bytes 196616 | tf_op jit(solution)/shard_map/ppermute | solution.py:156
  13.0 16.1 %all-to-all-start = ((s32[16,1,8]{2,1,0:T(1,128)}), s32[16,1,8]{2,1,0:T(1,128)S(1)}, u32[]{:S(2)}, u32[]{:S(2)}) async-start(s32[16,1,8]{2,1,0:T(1,128)} %copy.11), calls=%async_computation | async-start | bytes 16384 | tf_op jit(solution)/shard_map/all_to_all | solution.py:160
  29.1 0.8 copy-start.6
  30.9 62.0 %copy-start.8 = (s32[1,64,4]{1,2,0:T(4,128)S(1)}, s32[1,64,4]{1,2,0:T(4,128)}, u32[]{:S(2)}) copy-start(s32[1,64,4]{1,2,0:T(4,128)} %param.8) | copy-start | bytes 3076
  49.5 3.4 %copy-start = (bf16[1,64,4,128,128]{4,3,2,1,0:T(8,128)(2,1)S(1)}, bf16[1,64,4,128,128]{4,3,2,1,0:T(8,128)(2,1)}, u32[]{:S(2)}) copy-start(bf16[1,64,4,128,128]{4,3,2,1,0:T(8,128)(2,1)} %param.6) | copy-start | bytes 25165828
  52.9 0.7 copy-start.7
  53.6 25.0 %copy-start.4 = (bf16[64,128,128]{2,1,0:T(8,128)(2,1)S(1)}, bf16[64,128,128]{2,1,0:T(8,128)(2,1)}, u32[]{:S(2)}) copy-start(bf16[64,128,128]{2,1,0:T(8,128)(2,1)} %diag.7) | copy-start | bytes 6291460
  80.8 12.1 %all-to-all-start.3 = ((bf16[16,8,4,128]{3,2,1,0:T(4,128)(2,1)}), bf16[16,8,4,128]{3,2,1,0:T(4,128)(2,1)S(1)}, u32[]{:S(2)}, u32[]{:S(2)}) async-start(bf16[16,8,4,128]{3,2,1,0:T(4,128)(2,1)} %bitcast.11), calls=%async_computation.3 | async-start | bytes 262144 | tf_op jit(solution)/shard_map/all_to_all | solution.py:160
  84.3 14.6 %collective-permute-start.3 = (bf16[256,128]{1,0:T(8,128)(2,1)S(1)}, bf16[256,128]{1,0:T(8,128)(2,1)S(1)}, u32[]{:S(2)}, u32[]{:S(2)}) collective-permute-start(bf16[256,128]{1,0:T(8,128)(2,1)S(1)} %get-tuple-element.11.item0), channel_id=1, source_target_pairs={{4,0},{5,1},{6,2},{0,4},{1,5},{2,6},{20,16},{21,17},{22,18},{16,20... | collective-permute-start | bytes 196616 | tf_op jit(solution)/shard_map/ppermute | solution.py:200
  93.0 3.4 %copy-start.1 = (bf16[1,64,4,128,128]{4,3,2,1,0:T(8,128)(2,1)S(1)}, bf16[1,64,4,128,128]{4,3,2,1,0:T(8,128)(2,1)}, u32[]{:S(2)}) copy-start(bf16[1,64,4,128,128]{4,3,2,1,0:T(8,128)(2,1)} %param.6) | copy-start | bytes 25165828
  101.2 12.1 %all-to-all-start.4 = ((bf16[16,8,4,128]{3,2,1,0:T(4,128)(2,1)}), bf16[16,8,4,128]{3,2,1,0:T(4,128)(2,1)S(1)}, u32[]{:S(2)}, u32[]{:S(2)}) async-start(bf16[16,8,4,128]{3,2,1,0:T(4,128)(2,1)} %bitcast.13), calls=%async_computation.4 | async-start | bytes 262144 | tf_op jit(solution)/shard_map/all_to_all | solution.py:160
  104.7 14.6 %collective-permute-start.4 = (bf16[256,128]{1,0:T(8,128)(2,1)S(1)}, bf16[256,128]{1,0:T(8,128)(2,1)S(1)}, u32[]{:S(2)}, u32[]{:S(2)}) collective-permute-start(bf16[256,128]{1,0:T(8,128)(2,1)S(1)} %get-tuple-element.14.held), channel_id=1, source_target_pairs={{0,1},{1,0},{16,17},{17,16},{32,33},{33,32},{48,49},{49,48},{64,65... | collective-permute-start | bytes 196616 | tf_op jit(solution)/shard_map/ppermute | solution.py:207
  113.3 3.4 %copy-start.2 = (bf16[1,64,4,128,128]{4,3,2,1,0:T(8,128)(2,1)S(1)}, bf16[1,64,4,128,128]{4,3,2,1,0:T(8,128)(2,1)}, u32[]{:S(2)}) copy-start(bf16[1,64,4,128,128]{4,3,2,1,0:T(8,128)(2,1)} %param.6) | copy-start | bytes 25165828
  121.5 12.1 %all-to-all-start.5 = ((bf16[16,8,4,128]{3,2,1,0:T(4,128)(2,1)}), bf16[16,8,4,128]{3,2,1,0:T(4,128)(2,1)S(1)}, u32[]{:S(2)}, u32[]{:S(2)}) async-start(bf16[16,8,4,128]{3,2,1,0:T(4,128)(2,1)} %bitcast.15), calls=%async_computation.5 | async-start | bytes 262144 | tf_op jit(solution)/shard_map/all_to_all | solution.py:160
  125.0 14.6 %collective-permute-start.5 = (bf16[256,128]{1,0:T(8,128)(2,1)S(1)}, bf16[256,128]{1,0:T(8,128)(2,1)S(1)}, u32[]{:S(2)}, u32[]{:S(2)}) collective-permute-start(bf16[256,128]{1,0:T(8,128)(2,1)S(1)} %get-tuple-element.16), channel_id=1, source_target_pairs={{0,3},{1,2},{2,1},{16,19},{17,18},{18,17},{32,35},{33,34},{34,33},... | collective-permute-start | bytes 196616 | tf_op jit(solution)/shard_map/ppermute | solution.py:218
  133.6 3.4 %copy-start.3 = (bf16[1,64,4,128,128]{4,3,2,1,0:T(8,128)(2,1)S(1)}, bf16[1,64,4,128,128]{4,3,2,1,0:T(8,128)(2,1)}, u32[]{:S(2)}) copy-start(bf16[1,64,4,128,128]{4,3,2,1,0:T(8,128)(2,1)} %param.6) | copy-start | bytes 25165828

commit v3 on v2

v3 whole, which is shorter than its diff:
```python
import jax
import jax.numpy as jnp
from jax import lax
from jax.experimental import pallas as pl
from jax.experimental.pallas import tpu as pltpu
from jax.sharding import PartitionSpec as P


STEPS = 4
LANES = 16
ROWS = 16
CAP = 8
NB = 64
EXC = 4
B = 128
L = 4
TAKEN = ROWS * CAP
FLAT = NB * EXC
KNOWN = 3
SHARE = FLAT // LANES
PART = FLAT // 4
GROUP = 8

bf16 = jnp.bfloat16
f32 = jnp.float32
VMEM = pl.BlockSpec(memory_space=pltpu.VMEM)
SMEM = pl.BlockSpec(memory_space=pltpu.SMEM)
HBM = pl.BlockSpec(memory_space=pltpu.HBM)
LIMIT = 24 * 1024 * 1024


def call(kernel, out_shape, scratch, operands, in_smem, in_place=()):
    specs = [SMEM if i in in_smem else HBM if i in in_place else VMEM for i in range(len(operands))]
    many = isinstance(out_shape, (tuple, list))
    operands = [pltpu.with_memory_space_constraint(x, pltpu.HBM) if i in in_place else x for i, x in enumerate(operands)]
    return pl.pallas_call(
        kernel,
        out_shape=out_shape,
        in_specs=specs,
        out_specs=[VMEM] * len(out_shape) if many else VMEM,
        scratch_shapes=scratch,
        compiler_params=pltpu.CompilerParams(vmem_limit_bytes=LIMIT),
    )(*operands)


def pick_initial(lane, asked, stored, h1, h2, out, h0, sem):
    copy = pltpu.make_async_copy(stored, h0, sem)
    copy.start()

    @pl.loop(0, ROWS)
    def _(r):
        for t, h in enumerate((h1, h2)):
            for p in range(CAP):
                out[r, (t + 1) * CAP + p] = h[asked[r, p]]

    copy.wait()

    @pl.loop(0, ROWS)
    def _(r):
        for p in range(CAP):
            out[r, p] = h0[asked[r, p]]


def initial_terms(listed, stored, arrived, out, tiles, slots, wide, packed, total, sem, sems):
    lists = pltpu.make_async_copy(listed, slots, sem)
    lists.start()
    copies = []
    for g in range(NB // GROUP):
        part = pl.ds(g * GROUP, GROUP)
        copies.append(pltpu.make_async_copy(stored.at[part], tiles.at[part], sems.at[g]))
        copies[-1].start()
    for o in range(ROWS):
        for t in range(KNOWN):
            here = arrived[o, CAP * t : CAP * (t + 1)]
            wide[CAP * o : CAP * (o + 1), EXC * t : EXC * (t + 1), :] = here.astype(f32)
    packed[...] = wide[...].astype(bf16)
    lists.wait()

    for g in range(NB // GROUP):
        copies[g].wait()
        for j in range(GROUP):
            i = g * GROUP + j
            row = jnp.concatenate([packed[slots[s, i]] for s in range(L)], axis=1)
            tile = tiles[i].reshape(L * B, B)
            term = jnp.dot(row, tile, preferred_element_type=f32)
            for t in range(KNOWN):
                total[t, EXC * i : EXC * (i + 1), :] = term[EXC * t : EXC * (t + 1)]

    for y in range(4):
        for x in range(4):
            out[4 * y + x] = total[y % KNOWN, PART * x : PART * (x + 1), :].astype(bf16)


def add_terms(terms, out):
    total = terms[0].astype(f32)
    for k in range(1, LANES):
        total = total + terms[k].astype(f32)
    for x in range(4):
        out[x] = total


def solve(driven, diag, solved):
    for i in range(NB):
        row = driven[EXC * i : EXC * (i + 1), :].astype(bf16)
        solved[i] = jnp.dot(row, diag[i], preferred_element_type=f32)


def pick(asked, solved, send):
    @pl.loop(0, ROWS)
    def _(r):
        for p in range(CAP):
            send[r, p] = solved[asked[r, p]].astype(bf16)


def first_step(lane, asked, total, excite, diag, item, send, driven, solved):
    driven[...] = excite[0] - total[...]
    item[...] = driven[...].astype(bf16)
    solve(driven, diag, solved)
    pick(asked, solved, send)


def tile_terms(slots, tiles, arrived, total):
    @pl.loop(0, NB // GROUP)
    def _(g):
        for j in range(GROUP):
            i = g * GROUP + j
            row = jnp.concatenate([arrived[slots[s, i]] for s in range(L)], axis=1)
            tile = tiles[i].reshape(L * B, B)
            at = pl.multiple_of(g * GROUP * EXC, GROUP * EXC)
            total[pl.ds(at + EXC * j, EXC), :] = jnp.dot(row, tile, preferred_element_type=f32)


def second_step(lane, asked, total, came, h2, excite, diag, item, send, driven, solved):
    me = lane[0]
    value = total[...] + came[...]
    driven[...] = excite[1] - value

    @pl.when(me == 0)
    def _():
        item[...] = driven[...].astype(bf16).astype(f32)
        solve(driven, diag, solved)
        pick(asked, solved, send)

    @pl.when(me == 1)
    def _():
        item[...] = value

    @pl.when(me > 1)
    def _():
        for i in range(NB):
            item[EXC * i : EXC * (i + 1), :] = h2[i].astype(f32)


def third_step(lane, asked, total, came, first, excite, diag, item, send, driven, solved):
    me = lane[0]
    other = jnp.where(me == 2, first[...].astype(f32), came[...])
    driven[...] = jnp.where(me == 0, excite[2] - (total[...] + came[...]), other)
    item[...] = driven[...].astype(bf16)

    @pl.when(me < KNOWN)
    def _():
        solve(driven, diag, solved)

    @pl.when(me >= KNOWN)
    def _():
        for i in range(NB):
            solved[i] = driven[EXC * i : EXC * (i + 1), :]

    pick(asked, solved, send)


def fourth_step(slots, tiles, arrived, item, out, total):
    tile_terms(slots, tiles, arrived, total)
    for k in range(LANES):
        mine = slice(SHARE * k, SHARE * (k + 1))
        out[k, :SHARE] = total[mine, :].astype(bf16)
        out[k, SHARE:] = item[mine, :]


def share_driven(lane, parts, excite, out):
    total = parts[0, :SHARE].astype(f32)
    for k in range(1, LANES):
        total = total + parts[k, :SHARE].astype(f32)
    start = pl.multiple_of(lane[0] * SHARE, SHARE)
    last = (excite[STEPS - 1, pl.ds(start, SHARE), :] - total).astype(bf16)
    for k in range(LANES):
        for t in range(STEPS - 1):
            out[k, SHARE * t : SHARE * (t + 1)] = parts[STEPS - 2 - t, SHARE:]
        out[k, SHARE * (STEPS - 1) :] = last


def last_solve(driven, diag, out):
    each = SHARE // EXC
    for i in range(NB):
        value = jnp.dot(driven[i // each], diag[i], preferred_element_type=f32)
        for t in range(STEPS):
            at = SHARE * t + EXC * (i % each)
            out[t, i] = value[at : at + EXC]


def shifted(array, axis, by):
    peers = lax.axis_size(axis)
    return lax.ppermute(array, axis, [(i, i + by) for i in range(peers - by)])


def exchange(array, axis, groups=None):
    return lax.all_to_all(array, axis, split_axis=0, concat_axis=0, tiled=True, axis_index_groups=groups)


def body(retarded_tiles, wanted_blocks, tile_slots, diag_inverse, excitation, history_init):
    sds = jax.ShapeDtypeStruct
    stored = retarded_tiles[0]
    slots = tile_slots[0].T
    lane = lax.axis_index("delay").astype(jnp.int32).reshape(1)
    excite = excitation.reshape(STEPS, FLAT, B)

    asked = exchange(wanted_blocks[0, 0], "rows")
    h0 = history_init[0]
    later = []
    for t in range(1, KNOWN):
        later.append(shifted(h0, "delay", t))

    picked = call(
        pick_initial,
        sds((ROWS, KNOWN * CAP, EXC, B), bf16),
        [pltpu.VMEM(h0.shape, bf16), pltpu.SemaphoreType.DMA],
        (lane, asked, h0, *later),
        (0, 1),
        (2,),
    )
    arrived = exchange(picked, "rows")
    wide = (TAKEN, EXC * STEPS, B)
    terms, tiles = call(
        initial_terms,
        (sds((LANES, PART, B), bf16), sds(stored.shape, bf16)),
        [
            pltpu.SMEM(slots.shape, jnp.int32),
            pltpu.VMEM(wide, f32),
            pltpu.VMEM(wide, bf16),
            pltpu.VMEM((KNOWN, FLAT, B), f32),
            pltpu.SemaphoreType.DMA,
            pltpu.SemaphoreType.DMA((NB // GROUP,)),
        ],
        (slots, stored, arrived),
        (),
        (0, 1),
    )
    terms = exchange(terms, "delay")
    part = call(add_terms, sds((4, PART, B), f32), [], (terms,), ())
    along_x = [[4 * y + x for x in range(4)] for y in range(4)]
    whole = exchange(part, "delay", along_x).reshape(FLAT, B)

    flat = pltpu.VMEM((FLAT, B), f32)
    block = pltpu.VMEM((NB, EXC, B), f32)
    send_shape = sds((ROWS, CAP, EXC, B), bf16)

    came = lax.ppermute(whole, "delay", [(4, 0), (9, 1)])
    item0, send = call(
        first_step,
        (sds((FLAT, B), bf16), send_shape),
        [flat, block],
        (lane, asked, whole, excite, diag_inverse),
        (0, 1),
    )
    arrived = exchange(send, "rows").reshape(TAKEN, EXC, B)
    total = call(tile_terms, sds((FLAT, B), f32), [], (slots, tiles, arrived), (0,))

    item1, send = call(
        second_step,
        (sds((FLAT, B), f32), send_shape),
        [flat, block],
        (lane, asked, total, came, later[1], excite, diag_inverse),
        (0, 1),
    )
    came = lax.ppermute(item1, "delay", [(0, 1), (1, 0)] + [(k, k + 1) for k in range(2, LANES - 1)])
    arrived = exchange(send, "rows").reshape(TAKEN, EXC, B)
    total = call(tile_terms, sds((FLAT, B), f32), [], (slots, tiles, arrived), (0,))

    item2, send = call(
        third_step,
        (sds((FLAT, B), bf16), send_shape),
        [flat, block],
        (lane, asked, total, came, item0, excite, diag_inverse),
        (0, 1),
    )
    arrived = exchange(send, "rows").reshape(TAKEN, EXC, B)
    parts = call(
        fourth_step, sds((LANES, 2 * SHARE, B), bf16), [flat], (slots, tiles, arrived, item2), (0,)
    )
    parts = exchange(parts, "delay")
    shares = call(
        share_driven, sds((LANES, STEPS * SHARE, B), bf16), [], (lane, parts, excite), (0,)
    )
    driven = exchange(shares, "delay")
    return call(last_solve, sds((STEPS, NB, EXC, B), f32), [], (driven, diag_inverse), ())


def solution(mesh):
    return jax.shard_map(
        body,
        mesh=mesh,
        in_specs=(
            P("delay", "rows", None, None, None),
            P("delay", "rows", None, None),
            P("delay", "rows", None),
            P("rows", None, None),
            P(None, "rows", None, None),
            P("delay", "rows", None, None),
        ),
        out_specs=P(None, "rows", None, None),
        check_vma=False,
    )
```

time: 161 us -> 160 us (level)
  blocking collectives: 60 us -> 76.6 us
  starting transfers between devices: 38.5 us -> 28.2 us
  waiting for transfers between devices: 25.5 us -> 19.2 us
  local copies, waits for them, and re-layouts: 16.4 us -> 14.7 us
    all_to_all x4 -> x6, blocking collectives: 60 us -> 76.6 us  [exchange(): lax.all_to_all(array, axis, split_axis=0, concat_axis=0, tiled=True, axis...]
    all_to_all x4 -> x3, waiting for transfers between devices: 25.5 us -> 19.2 us  [exchange(): lax.all_to_all(array, axis, split_axis=0, concat_axis=0, tiled=True, axis...]
    ppermute x3 -> x2, starting transfers between devices: 11.6 us -> 7.09 us  [shifted(): return lax.ppermute(array, axis, [(i, i + by) for i in range(peers - by)])]
    all_to_all x4 -> x3, starting transfers between devices: 19.1 us -> 15.6 us  [exchange(): lax.all_to_all(array, axis, split_axis=0, concat_axis=0, tiled=True, axis...]
    ppermute x3 -> x2, starting transfers between devices: 7.8 us -> 5.54 us  [the longest x1 4.25 us: body(): lax.ppermute(item1, 'delay', [(0, 1), (1, 0)] + [(k, k + 1) for k in rang...]
    unnamed x18 -> x14, local copies, waits for them, and re-layouts: 15.1 us -> 13.4 us
  transfers between devices with their start and end apart: 10 -> 7, of which waited for: 4 -> 3; matrix products, arithmetic and copies ran while one was open for 1% -> 1% of each run, Pallas kernels for 5% -> 3%
where the time goes in v3:
time: 160 us; the launch traced here: 159 us
  blocking collectives  76.6 us (48%)
  starting transfers between devices  28.2 us (18%)
  Pallas kernels  20 us (12%)
  waiting for transfers between devices  19.2 us (12%)
  local copies, waits for them, and re-layouts  14.7 us (9%)
    all_to_all x6, blocking collectives, exchange(): lax.all_to_all(array, axis, split_axis=0, concat_axis=0, tiled=True, axis...  76.6 us
    pallas_call x11, Pallas kernels, call(): pl.pallas_call(kernel, out_shape=out_shape, in_specs=specs, out_specs=[VM...  20 us
    all_to_all x3, waiting for transfers between devices, exchange(): lax.all_to_all(array, axis, split_axis=0, concat_axis=0, tiled=True, axis...  19.2 us
    all_to_all x3, starting transfers between devices, exchange(): lax.all_to_all(array, axis, split_axis=0, concat_axis=0, tiled=True, axis...  15.6 us
    unnamed x14, local copies, waits for them, and re-layouts  13.4 us
    ppermute x2, starting transfers between devices, shifted(): return lax.ppermute(array, axis, [(i, i + by) for i in range(peers - by)])  7.09 us
    ppermute x1, starting transfers between devices, body(): lax.ppermute(item1, 'delay', [(0, 1), (1, 0)] + [(k, k + 1) for k in rang...  4.25 us
  transfers between devices with their start and end apart: 7, of which 3 were waited for; matrix products, arithmetic and copies ran while one was open for 1% of the time, Pallas kernels for 3%

profile of v3, /device:TPU:2, one launch (start us, length us, event | category | flops | bytes accessed | tf_op | source)
XLA Modules:
  0.0 158.9 jit_solution(2460855888542237758)
XLA Ops:
  0.0 0.0 copy-start.6
  0.0 0.0 copy-start.4
  0.0 0.0 copy-start.5
  0.0 4.3 %collective-permute-start.1 = (bf16[64,4,128]{2,1,0:T(4,128)(2,1)}, bf16[64,4,128]{2,1,0:T(4,128)(2,1)S(1)}, u32[]{:S(2)}, u32[]{:S(2)}) collective-permute-start(bf16[64,4,128]{2,1,0:T(4,128)(2,1)} %bitcast.31), channel_id=1, source_target_pairs={{0,2},{1,3},{2,4},{3,5},{4,6},{5,7},{6,8},{7,9},{8,10},{9,11},{10,... | collective-permute-start | bytes 196616 | tf_op jit(solution)/shard_map/ppermute | solution.py:203
  4.3 2.8 %collective-permute-start = (bf16[64,4,128]{2,1,0:T(4,128)(2,1)}, bf16[64,4,128]{2,1,0:T(4,128)(2,1)S(1)}, u32[]{:S(2)}, u32[]{:S(2)}) collective-permute-start(bf16[64,4,128]{2,1,0:T(4,128)(2,1)} %bitcast.32), channel_id=1, source_target_pairs={{0,1},{1,2},{2,3},{3,4},{4,5},{5,6},{6,7},{7,8},{8,9},{9,10},{10,1... | collective-permute-start | bytes 196616 | tf_op jit(solution)/shard_map/ppermute | solution.py:203
  7.1 1.4 copy.11
  8.5 8.6 %all-to-all-start = ((s32[16,1,8]{2,1,0:T(1,128)}), s32[16,1,8]{2,1,0:T(1,128)S(1)}, u32[]{:S(2)}, u32[]{:S(2)}) async-start(s32[16,1,8]{2,1,0:T(1,128)} %copy.11), calls=%async_computation | async-start | bytes 16384 | tf_op jit(solution)/shard_map/all_to_all | solution.py:207
  17.1 7.5 %all-to-all-done = s32[16,1,8]{2,1,0:T(1,128)S(1)} async-done(((s32[16,1,8]{2,1,0:T(1,128)}), s32[16,1,8]{2,1,0:T(1,128)S(1)}, u32[]{:S(2)}, u32[]{:S(2)}) %all-to-all-start) | async-done | bytes 544 | tf_op jit(solution)/shard_map/all_to_all | solution.py:207
  24.6 0.0 collective-permute-done.1.h2
  24.6 0.0 collective-permute-done.h1
  24.6 1.7 %shard_map.64 = bf16[16,24,4,128]{3,2,1,0:T(4,128)(2,1)S(1)} custom-call(s32[1]{0:T(128)} %bitcast.lane, s32[16,8]{1,0:T(8,128)S(1)} %bitcast.22, bf16[64,4,128]{2,1,0:T(4,128)(2,1)} %bitcast.33, bf16[64,4,128]{2,1,0:T(4,128)(2,1)S(1)} %collective-permute-done.h1, bf16[64,4,128]{2,1,0:T(4,128)(2,1)S(1)} %collective-permute-done.1.h2), custom_call_target="tpu_custom_call" | custom-call | tf_op jit(solution)/shard_map/pallas_call | solution.py:36
  26.3 16.2 %all_to_all.51.arrived = bf16[16,24,4,128]{3,2,1,0:T(4,128)(2,1)S(1)} all-to-all(bf16[16,24,4,128]{3,2,1,0:T(4,128)(2,1)S(1)} %shard_map.64), channel_id=1, replica_groups=mesh['rows'=16,'delay'=16] {'rows'}, dimensions={0} | all-to-all | bytes 786432 | tf_op jit(solution)/shard_map/all_to_all | solution.py:207
  42.5 3.8 %shard_map.65 = (bf16[16,64,128]{2,1,0:T(8,128)(2,1)S(1)}, bf16[64,4,128,128]{3,2,1,0:T(8,128)(2,1)S(1)}) custom-call(s32[4,64]{1,0:T(4,128)} %bitcast.26, bf16[64,4,128,128]{3,2,1,0:T(8,128)(2,1)} %bitcast.30, bf16[16,24,4,128]{3,2,1,0:T(4,128)(2,1)S(1)} %all_to_all.51.arrived), custom_call_target="tpu_custom_call" | custom-call | tf_op jit(solution)/shard_map/pallas_call | solution.py:36
  46.2 0.0 copy-start
  46.3 3.2 %copy-done = bf16[64,4,128,128]{3,2,1,0:T(8,128)(2,1)} copy-done((bf16[64,4,128,128]{3,2,1,0:T(8,128)(2,1)}, bf16[64,4,128,128]{3,2,1,0:T(8,128)(2,1)S(1)}, u32[]{:S(2)}) %copy-start) | copy-done | bytes 8388632
  49.5 16.9 %all_to_all.52.terms = bf16[16,64,128]{2,1,0:T(8,128)(2,1)S(1)} all-to-all(bf16[16,64,128]{2,1,0:T(8,128)(2,1)S(1)} %get-tuple-element.14), channel_id=1, replica_groups=mesh['rows'=16,'delay'=16] {'delay'}, dimensions={0} | all-to-all | bytes 524288 | tf_op jit(solution)/shard_map/all_to_all | solution.py:207
  66.5 8.4 %all_to_all.53 = f32[4,64,128]{2,1,0:T(8,128)S(1)} all-to-all(f32[4,64,128]{2,1,0:T(8,128)S(1)} %shard_map.66), channel_id=1, replica_groups={{0,1,2,3},{4,5,6,7},{8,9,10,11},{12,13,14,15},{16,17,18,19},{20,21,22,2..., dimensions={0} | all-to-all | bytes 262144 | tf_op jit(solution)/shard_map/all_to_all | solution.py:207
  74.8 0.0 copy-done.4
  74.8 0.0 copy-done.5
  74.8 2.2 %shard_map.67 = (bf16[256,128]{1,0:T(8,128)(2,1)S(1)}, bf16[16,8,4,128]{3,2,1,0:T(4,128)(2,1)}) custom-call(s32[1]{0:T(128)} %bitcast.lane, s32[16,8]{1,0:T(8,128)S(1)} %bitcast.23, f32[256,128]{1,0:T(8,128)S(1)} %bitcast.20, f32[4,256,128]{2,1,0:T(8,128)S(1)} %bitcast.13, bf16[64,128,128]{2,1,0:T(8,128)(2,1)S(1)} %copy-done.4), custom_call_target="tpu_custom_call" | custom-call | tf_op jit(solution)/shard_map/pallas_call | solution.py:36
  77.0 3.5 %all-to-all-start.4 = ((bf16[16,8,4,128]{3,2,1,0:T(4,128)(2,1)}), bf16[16,8,4,128]{3,2,1,0:T(4,128)(2,1)S(1)}, u32[]{:S(2)}, u32[]{:S(2)}) async-start(bf16[16,8,4,128]{3,2,1,0:T(4,128)(2,1)} %get-tuple-element.15), calls=%async_computation.4 | async-start | bytes 262144 | tf_op jit(solution)/shard_map/all_to_all | solution.py:207
  80.5 1.3 collective-permute-start.2
  81.8 7.3 %all-to-all-done.4 = bf16[16,8,4,128]{3,2,1,0:T(4,128)(2,1)S(1)} async-done(((bf16[16,8,4,128]{3,2,1,0:T(4,128)(2,1)}), bf16[16,8,4,128]{3,2,1,0:T(4,128)(2,1)S(1)}, u32[]{:S(2)}, u32[]{:S(2)}) %all-to-all-start.4) | async-done | bytes 131104 | tf_op jit(solution)/shard_map/all_to_all | solution.py:207
  89.2 0.0 copy-done.6
  89.2 0.0 copy-start.1
  89.2 3.4 %copy-done.1 = bf16[64,4,128,128]{3,2,1,0:T(8,128)(2,1)S(1)} copy-done((bf16[64,4,128,128]{3,2,1,0:T(8,128)(2,1)S(1)}, bf16[64,4,128,128]{3,2,1,0:T(8,128)(2,1)}, u32[]{:S(2)}) %copy-start.1) | copy-done | bytes 8388632
  92.6 2.6 %shard_map.68.total = f32[256,128]{1,0:T(8,128)S(1)} custom-call(s32[4,64]{1,0:T(4,128)S(1)} %bitcast.27, bf16[64,4,128,128]{3,2,1,0:T(8,128)(2,1)S(1)} %copy-done.1, bf16[128,4,128]{2,1,0:T(4,128)(2,1)S(1)} %bitcast.17), custom_call_target="tpu_custom_call" | custom-call | tf_op jit(solution)/shard_map/pallas_call | solution.py:36
  95.2 0.0 collective-permute-done.2.came
  95.2 1.4 shard_map.69
  96.5 3.5 %all-to-all-start.5 = ((bf16[16,8,4,128]{3,2,1,0:T(4,128)(2,1)}), bf16[16,8,4,128]{3,2,1,0:T(4,128)(2,1)S(1)}, u32[]{:S(2)}, u32[]{:S(2)}) async-start(bf16[16,8,4,128]{3,2,1,0:T(4,128)(2,1)} %get-tuple-element.16), calls=%async_computation.5 | async-start | bytes 262144 | tf_op jit(solution)/shard_map/all_to_all | solution.py:207
  100.1 4.2 %collective-permute-start.3 = (f32[256,128]{1,0:T(8,128)S(1)}, f32[256,128]{1,0:T(8,128)S(1)}, u32[]{:S(2)}, u32[]{:S(2)}) collective-permute-start(f32[256,128]{1,0:T(8,128)S(1)} %get-tuple-element.17), channel_id=1, source_target_pairs={{0,1},{1,0},{2,3},{3,4},{4,5},{5,6},{6,7},{7,8},{8,9},{9,10},{10,1... | collective-permute-start | bytes 393224 | tf_op jit(solution)/shard_map/ppermute | solution.py:275
  104.3 4.4 %all-to-all-done.5 = bf16[16,8,4,128]{3,2,1,0:T(4,128)(2,1)S(1)} async-done(((bf16[16,8,4,128]{3,2,1,0:T(4,128)(2,1)}), bf16[16,8,4,128]{3,2,1,0:T(4,128)(2,1)S(1)}, u32[]{:S(2)}, u32[]{:S(2)}) %all-to-all-start.5) | async-done | bytes 131104 | tf_op jit(solution)/shard_map/all_to_all | solution.py:207
  108.7 0.0 copy-start.2
  108.7 3.4 %copy-done.2 = bf16[64,4,128,128]{3,2,1,0:T(8,128)(2,1)S(1)} copy-done((bf16[64,4,128,128]{3,2,1,0:T(8,128)(2,1)S(1)}, bf16[64,4,128,128]{3,2,1,0:T(8,128)(2,1)}, u32[]{:S(2)}) %copy-start.2) | copy-done | bytes 8388632
  112.1 2.6 %shard_map.70.total = f32[256,128]{1,0:T(8,128)S(1)} custom-call(s32[4,64]{1,0:T(4,128)S(1)} %bitcast.28, bf16[64,4,128,128]{3,2,1,0:T(8,128)(2,1)S(1)} %copy-done.2, bf16[128,4,128]{2,1,0:T(4,128)(2,1)S(1)} %bitcast.18), custom_call_target="tpu_custom_call" | custom-call | tf_op jit(solution)/shard_map/pallas_call | solution.py:36
  114.7 0.0 collective-permute-done.3.came
  114.7 1.6 %shard_map.71 = (bf16[256,128]{1,0:T(8,128)(2,1)S(1)}, bf16[16,8,4,128]{3,2,1,0:T(4,128)(2,1)S(1)}) custom-call(s32[1]{0:T(128)} %bitcast.lane, s32[16,8]{1,0:T(8,128)S(1)} %bitcast.25, f32[256,128]{1,0:T(8,128)S(1)} %shard_map.70.total, f32[256,128]{1,0:T(8,128)S(1)} %collective-permute-done.3.came, bf16[256,128]{1,0:T(8,128)(2,1)S(1)} %get-tuple-element.18.first, ...), custom_call_target="tpu_custom_call" | custom-call | tf_op jit(solution)/shard_map/pallas_call | solution.py:36
  116.3 11.5 %all_to_all.54 = bf16[16,8,4,128]{3,2,1,0:T(4,128)(2,1)S(1)} all-to-all(bf16[16,8,4,128]{3,2,1,0:T(4,128)(2,1)S(1)} %get-tuple-element.19), channel_id=1, replica_groups=mesh['rows'=16,'delay'=16] {'rows'}, dimensions={0} | all-to-all | bytes 262144 | tf_op jit(solution)/shard_map/all_to_all | solution.py:207
  127.8 0.0 copy-start.3
  127.8 3.4 %copy-done.3 = bf16[64,4,128,128]{3,2,1,0:T(8,128)(2,1)S(1)} copy-done((bf16[64,4,128,128]{3,2,1,0:T(8,128)(2,1)S(1)}, bf16[64,4,128,128]{3,2,1,0:T(8,128)(2,1)}, u32[]{:S(2)}) %copy-start.3) | copy-done | bytes 8388632
  131.2 2.6 %shard_map.72 = bf16[16,32,128]{2,1,0:T(8,128)(2,1)S(1)} custom-call(s32[4,64]{1,0:T(4,128)S(1)} %bitcast.29, bf16[64,4,128,128]{3,2,1,0:T(8,128)(2,1)S(1)} %copy-done.3, bf16[128,4,128]{2,1,0:T(4,128)(2,1)S(1)} %bitcast.19, bf16[256,128]{1,0:T(8,128)(2,1)S(1)} %get-tuple-element.20.item), custom_call_target="tpu_custom_call" | custom-call | tf_op jit(solution)/shard_map/pallas_call | solution.py:36
  133.8 11.8 %all_to_all.55.parts = bf16[16,32,128]{2,1,0:T(8,128)(2,1)S(1)} all-to-all(bf16[16,32,128]{2,1,0:T(8,128)(2,1)S(1)} %shard_map.72), channel_id=1, replica_groups=mesh['rows'=16,'delay'=16] {'delay'}, dimensions={0} | all-to-all | bytes 262144 | tf_op jit(solution)/shard_map/all_to_all | solution.py:207
  145.7 11.8 %all_to_all.56.driven = bf16[16,64,128]{2,1,0:T(8,128)(2,1)S(1)} all-to-all(bf16[16,64,128]{2,1,0:T(8,128)(2,1)S(1)} %shard_map.73), channel_id=1, replica_groups=mesh['rows'=16,'delay'=16] {'delay'}, dimensions={0} | all-to-all | bytes 524288 | tf_op jit(solution)/shard_map/all_to_all | solution.py:207
  157.4 1.5 shard_map.74
  (2 shorter events, 0.1 us)
Async XLA Ops:
  0.0 89.2 %copy-start.6 = (s32[1,64,4]{1,2,0:T(4,128)S(1)}, s32[1,64,4]{1,2,0:T(4,128)}, u32[]{:S(2)}) copy-start(s32[1,64,4]{1,2,0:T(4,128)} %param.8) | copy-start | bytes 3076
  0.0 74.8 %copy-start.4 = (bf16[64,128,128]{2,1,0:T(8,128)(2,1)S(1)}, bf16[64,128,128]{2,1,0:T(8,128)(2,1)}, u32[]{:S(2)}) copy-start(bf16[64,128,128]{2,1,0:T(8,128)(2,1)} %diag.7) | copy-start | bytes 6291460
  0.0 74.8 %copy-start.5 = (f32[4,64,4,128]{3,2,1,0:T(4,128)S(1)}, f32[4,64,4,128]{3,2,1,0:T(4,128)}, u32[]{:S(2)}) copy-start(f32[4,64,4,128]{3,2,1,0:T(4,128)} %param.10) | copy-start | bytes 1572868
  0.0 24.6 %collective-permute-start.1 = (bf16[64,4,128]{2,1,0:T(4,128)(2,1)}, bf16[64,4,128]{2,1,0:T(4,128)(2,1)S(1)}, u32[]{:S(2)}, u32[]{:S(2)}) collective-permute-start(bf16[64,4,128]{2,1,0:T(4,128)(2,1)} %bitcast.31), channel_id=1, source_target_pairs={{0,2},{1,3},{2,4},{3,5},{4,6},{5,7},{6,8},{7,9},{8,10},{9,11},{10,... | collective-permute-start | bytes 196616 | tf_op jit(solution)/shard_map/ppermute | solution.py:203
  4.3 20.3 %collective-permute-start = (bf16[64,4,128]{2,1,0:T(4,128)(2,1)}, bf16[64,4,128]{2,1,0:T(4,128)(2,1)S(1)}, u32[]{:S(2)}, u32[]{:S(2)}) collective-permute-start(bf16[64,4,128]{2,1,0:T(4,128)(2,1)} %bitcast.32), channel_id=1, source_target_pairs={{0,1},{1,2},{2,3},{3,4},{4,5},{5,6},{6,7},{7,8},{8,9},{9,10},{10,1... | collective-permute-start | bytes 196616 | tf_op jit(solution)/shard_map/ppermute | solution.py:203
  8.5 16.1 %all-to-all-start = ((s32[16,1,8]{2,1,0:T(1,128)}), s32[16,1,8]{2,1,0:T(1,128)S(1)}, u32[]{:S(2)}, u32[]{:S(2)}) async-start(s32[16,1,8]{2,1,0:T(1,128)} %copy.11), calls=%async_computation | async-start | bytes 16384 | tf_op jit(solution)/shard_map/all_to_all | solution.py:207
  46.2 3.2 %copy-start = (bf16[64,4,128,128]{3,2,1,0:T(8,128)(2,1)}, bf16[64,4,128,128]{3,2,1,0:T(8,128)(2,1)S(1)}, u32[]{:S(2)}) copy-start(bf16[64,4,128,128]{3,2,1,0:T(8,128)(2,1)S(1)} %get-tuple-element.13.tiles) | copy-start | bytes 25165828
  77.0 12.1 %all-to-all-start.4 = ((bf16[16,8,4,128]{3,2,1,0:T(4,128)(2,1)}), bf16[16,8,4,128]{3,2,1,0:T(4,128)(2,1)S(1)}, u32[]{:S(2)}, u32[]{:S(2)}) async-start(bf16[16,8,4,128]{3,2,1,0:T(4,128)(2,1)} %get-tuple-element.15), calls=%async_computation.4 | async-start | bytes 262144 | tf_op jit(solution)/shard_map/all_to_all | solution.py:207
  80.5 14.6 %collective-permute-start.2 = (f32[256,128]{1,0:T(8,128)S(1)}, f32[256,128]{1,0:T(8,128)S(1)}, u32[]{:S(2)}, u32[]{:S(2)}) collective-permute-start(f32[256,128]{1,0:T(8,128)S(1)} %bitcast.21), channel_id=1, source_target_pairs={{4,0},{9,1},{20,16},{25,17},{36,32},{41,33},{52,48},{57,49},{68,64... | collective-permute-start | bytes 393224 | tf_op jit(solution)/shard_map/ppermute | solution.py:257
  89.2 3.4 %copy-start.1 = (bf16[64,4,128,128]{3,2,1,0:T(8,128)(2,1)S(1)}, bf16[64,4,128,128]{3,2,1,0:T(8,128)(2,1)}, u32[]{:S(2)}) copy-start(bf16[64,4,128,128]{3,2,1,0:T(8,128)(2,1)} %copy-done) | copy-start | bytes 25165828
  96.5 12.1 %all-to-all-start.5 = ((bf16[16,8,4,128]{3,2,1,0:T(4,128)(2,1)}), bf16[16,8,4,128]{3,2,1,0:T(4,128)(2,1)S(1)}, u32[]{:S(2)}, u32[]{:S(2)}) async-start(bf16[16,8,4,128]{3,2,1,0:T(4,128)(2,1)} %get-tuple-element.16), calls=%async_computation.5 | async-start | bytes 262144 | tf_op jit(solution)/shard_map/all_to_all | solution.py:207
  100.1 14.6 %collective-permute-start.3 = (f32[256,128]{1,0:T(8,128)S(1)}, f32[256,128]{1,0:T(8,128)S(1)}, u32[]{:S(2)}, u32[]{:S(2)}) collective-permute-start(f32[256,128]{1,0:T(8,128)S(1)} %get-tuple-element.17), channel_id=1, source_target_pairs={{0,1},{1,0},{2,3},{3,4},{4,5},{5,6},{6,7},{7,8},{8,9},{9,10},{10,1... | collective-permute-start | bytes 393224 | tf_op jit(solution)/shard_map/ppermute | solution.py:275
  108.7 3.4 %copy-start.2 = (bf16[64,4,128,128]{3,2,1,0:T(8,128)(2,1)S(1)}, bf16[64,4,128,128]{3,2,1,0:T(8,128)(2,1)}, u32[]{:S(2)}) copy-start(bf16[64,4,128,128]{3,2,1,0:T(8,128)(2,1)} %copy-done) | copy-start | bytes 25165828
  127.8 3.4 %copy-start.3 = (bf16[64,4,128,128]{3,2,1,0:T(8,128)(2,1)S(1)}, bf16[64,4,128,128]{3,2,1,0:T(8,128)(2,1)}, u32[]{:S(2)}) copy-start(bf16[64,4,128,128]{3,2,1,0:T(8,128)(2,1)} %copy-done) | copy-start | bytes 25165828

commit v4 on v3

--- a/solution.py
+++ b/solution.py
@@ -43,20 +43,17 @@
     )(*operands)
 
 
-def pick_initial(lane, asked, stored, h1, h2, out, h0, sem):
+def pick_initial(asked, stored, h1, h2, out, h0, sem):
     copy = pltpu.make_async_copy(stored, h0, sem)
     copy.start()
 
-    @pl.loop(0, ROWS)
-    def _(r):
-        for t, h in enumerate((h1, h2)):
-            for p in range(CAP):
-                out[r, (t + 1) * CAP + p] = h[asked[r, p]]
-
+    for r in range(ROWS):
+        for p in range(CAP):
+            at = asked[r, p]
+            out[r, CAP + p] = h1[at]
+            out[r, 2 * CAP + p] = h2[at]
     copy.wait()
-
-    @pl.loop(0, ROWS)
-    def _(r):
+    for r in range(ROWS):
         for p in range(CAP):
             out[r, p] = h0[asked[r, p]]
 
@@ -106,13 +103,12 @@
 
 
 def pick(asked, solved, send):
-    @pl.loop(0, ROWS)
-    def _(r):
+    for r in range(ROWS):
         for p in range(CAP):
             send[r, p] = solved[asked[r, p]].astype(bf16)
 
 
-def first_step(lane, asked, total, excite, diag, item, send, driven, solved):
+def first_step(asked, total, excite, diag, item, send, driven, solved):
     driven[...] = excite[0] - total[...]
     item[...] = driven[...].astype(bf16)
     solve(driven, diag, solved)
@@ -120,18 +116,14 @@
 
 
 def tile_terms(slots, tiles, arrived, total):
-    @pl.loop(0, NB // GROUP)
-    def _(g):
-        for j in range(GROUP):
-            i = g * GROUP + j
-            row = jnp.concatenate([arrived[slots[s, i]] for s in range(L)], axis=1)
-            tile = tiles[i].reshape(L * B, B)
-            at = pl.multiple_of(g * GROUP * EXC, GROUP * EXC)
-            total[pl.ds(at + EXC * j, EXC), :] = jnp.dot(row, tile, preferred_element_type=f32)
-
-
-def second_step(lane, asked, total, came, h2, excite, diag, item, send, driven, solved):
-    me = lane[0]
+    for i in range(NB):
+        row = jnp.concatenate([arrived[slots[s, i]] for s in range(L)], axis=1)
+        tile = tiles[i].reshape(L * B, B)
+        total[EXC * i : EXC * (i + 1), :] = jnp.dot(row, tile, preferred_element_type=f32)
+
+
+def second_step(asked, total, came, h2, excite, diag, item, send, driven, solved):
+    me = lax.axis_index("delay")
     value = total[...] + came[...]
     driven[...] = excite[1] - value
 
@@ -151,8 +143,8 @@
             item[EXC * i : EXC * (i + 1), :] = h2[i].astype(f32)
 
 
-def third_step(lane, asked, total, came, first, excite, diag, item, send, driven, solved):
-    me = lane[0]
+def third_step(asked, total, came, first, excite, diag, item, send, driven, solved):
+    me = lax.axis_index("delay")
     other = jnp.where(me == 2, first[...].astype(f32), came[...])
     driven[...] = jnp.where(me == 0, excite[2] - (total[...] + came[...]), other)
     item[...] = driven[...].astype(bf16)
@@ -177,11 +169,11 @@
         out[k, SHARE:] = item[mine, :]
 
 
-def share_driven(lane, parts, excite, out):
+def share_driven(parts, excite, out):
     total = parts[0, :SHARE].astype(f32)
     for k in range(1, LANES):
         total = total + parts[k, :SHARE].astype(f32)
-    start = pl.multiple_of(lane[0] * SHARE, SHARE)
+    start = pl.multiple_of(lax.axis_index("delay") * SHARE, SHARE)
     last = (excite[STEPS - 1, pl.ds(start, SHARE), :] - total).astype(bf16)
     for k in range(LANES):
         for t in range(STEPS - 1):
@@ -211,7 +203,6 @@
     sds = jax.ShapeDtypeStruct
     stored = retarded_tiles[0]
     slots = tile_slots[0].T
-    lane = lax.axis_index("delay").astype(jnp.int32).reshape(1)
     excite = excitation.reshape(STEPS, FLAT, B)
 
     asked = exchange(wanted_blocks[0, 0], "rows")
@@ -224,9 +215,9 @@
         pick_initial,
         sds((ROWS, KNOWN * CAP, EXC, B), bf16),
         [pltpu.VMEM(h0.shape, bf16), pltpu.SemaphoreType.DMA],
-        (lane, asked, h0, *later),
-        (0, 1),
-        (2,),
+        (asked, h0, *later),
+        (0,),
+        (1,),
     )
     arrived = exchange(picked, "rows")
     wide = (TAKEN, EXC * STEPS, B)
@@ -259,8 +250,8 @@
         first_step,
         (sds((FLAT, B), bf16), send_shape),
         [flat, block],
-        (lane, asked, whole, excite, diag_inverse),
-        (0, 1),
+        (asked, whole, excite, diag_inverse),
+        (0,),
     )
     arrived = exchange(send, "rows").reshape(TAKEN, EXC, B)
     total = call(tile_terms, sds((FLAT, B), f32), [], (slots, tiles, arrived), (0,))
@@ -269,8 +260,8 @@
         second_step,
         (sds((FLAT, B), f32), send_shape),
         [flat, block],
-        (lane, asked, total, came, later[1], excite, diag_inverse),
-        (0, 1),
+        (asked, total, came, later[1], excite, diag_inverse),
+        (0,),
     )
     came = lax.ppermute(item1, "delay", [(0, 1), (1, 0)] + [(k, k + 1) for k in range(2, LANES - 1)])
     arrived = exchange(send, "rows").reshape(TAKEN, EXC, B)
@@ -280,17 +271,15 @@
         third_step,
         (sds((FLAT, B), bf16), send_shape),
         [flat, block],
-        (lane, asked, total, came, item0, excite, diag_inverse),
-        (0, 1),
+        (asked, total, came, item0, excite, diag_inverse),
+        (0,),
     )
     arrived = exchange(send, "rows").reshape(TAKEN, EXC, B)
     parts = call(
         fourth_step, sds((LANES, 2 * SHARE, B), bf16), [flat], (slots, tiles, arrived, item2), (0,)
     )
     parts = exchange(parts, "delay")
-    shares = call(
-        share_driven, sds((LANES, STEPS * SHARE, B), bf16), [], (lane, parts, excite), (0,)
-    )
+    shares = call(share_driven, sds((LANES, STEPS * SHARE, B), bf16), [], (parts, excite), ())
     driven = exchange(shares, "delay")
     return call(last_solve, sds((STEPS, NB, EXC, B), f32), [], (driven, diag_inverse), ())
 

time: 160 us -> 156 us (0.975)
  blocking collectives: 76.6 us -> 92.4 us
  starting transfers between devices: 28.2 us -> 19.5 us
  waiting for transfers between devices: 19.2 us -> 11.8 us
  Pallas kernels: 20 us -> 17.3 us
    all_to_all x6 -> x7, blocking collectives: 76.6 us -> 92.4 us  [exchange(): lax.all_to_all(array, axis, split_axis=0, concat_axis=0, tiled=True, axis...]
    all_to_all x3 -> x2, starting transfers between devices: 15.6 us -> 7.03 us  [exchange(): lax.all_to_all(array, axis, split_axis=0, concat_axis=0, tiled=True, axis...]
    all_to_all x3 -> x2, waiting for transfers between devices: 19.2 us -> 11.8 us  [exchange(): lax.all_to_all(array, axis, split_axis=0, concat_axis=0, tiled=True, axis...]
    pallas_call x11, Pallas kernels: 20 us -> 17.3 us  [call(): pl.pallas_call(kernel, out_shape=out_shape, in_specs=specs, out_specs=[VM...]
  transfers between devices with their start and end apart: 7 -> 6, of which waited for: 3 -> 2; matrix products, arithmetic and copies ran while one was open for 1% -> 0% of each run, Pallas kernels for 3% -> 2%
where the time goes in v4:
time: 156 us; the launch traced here: 155 us
  blocking collectives  92.4 us (59%)
  starting transfers between devices  19.5 us (12%)
  Pallas kernels  17.3 us (11%)
  local copies, waits for them, and re-layouts  14.1 us (9%)
  waiting for transfers between devices  11.8 us (8%)
    all_to_all x7, blocking collectives, exchange(): lax.all_to_all(array, axis, split_axis=0, concat_axis=0, tiled=True, axis...  92.4 us
    pallas_call x11, Pallas kernels, call(): pl.pallas_call(kernel, out_shape=out_shape, in_specs=specs, out_specs=[VM...  17.3 us
    unnamed x14, local copies, waits for them, and re-layouts  13.4 us
    all_to_all x2, waiting for transfers between devices, exchange(): lax.all_to_all(array, axis, split_axis=0, concat_axis=0, tiled=True, axis...  11.8 us
    ppermute x2, starting transfers between devices, shifted(): return lax.ppermute(array, axis, [(i, i + by) for i in range(peers - by)])  7.09 us
    all_to_all x2, starting transfers between devices, exchange(): lax.all_to_all(array, axis, split_axis=0, concat_axis=0, tiled=True, axis...  7.03 us
    ppermute x1, starting transfers between devices, body(): lax.ppermute(item1, 'delay', [(0, 1), (1, 0)] + [(k, k + 1) for k in rang...  4.12 us
  transfers between devices with their start and end apart: 6, of which 2 were waited for; matrix products, arithmetic and copies ran while one was open for 0% of the time, Pallas kernels for 2%

profile of v4, /device:TPU:2, one launch (start us, length us, event | category | flops | bytes accessed | tf_op | source)
XLA Modules:
  0.0 155.3 jit_solution(16397263608258868682)
XLA Ops:
  0.0 0.0 copy-start.6
  0.0 0.0 copy-start.4
  0.0 0.0 copy-start.5
  0.0 4.3 %collective-permute-start.1 = (bf16[64,4,128]{2,1,0:T(4,128)(2,1)}, bf16[64,4,128]{2,1,0:T(4,128)(2,1)S(1)}, u32[]{:S(2)}, u32[]{:S(2)}) collective-permute-start(bf16[64,4,128]{2,1,0:T(4,128)(2,1)} %bitcast.30), channel_id=1, source_target_pairs={{0,2},{1,3},{2,4},{3,5},{4,6},{5,7},{6,8},{7,9},{8,10},{9,11},{10,... | collective-permute-start | bytes 196616 | tf_op jit(solution)/shard_map/ppermute | solution.py:195
  4.3 2.8 %collective-permute-start = (bf16[64,4,128]{2,1,0:T(4,128)(2,1)}, bf16[64,4,128]{2,1,0:T(4,128)(2,1)S(1)}, u32[]{:S(2)}, u32[]{:S(2)}) collective-permute-start(bf16[64,4,128]{2,1,0:T(4,128)(2,1)} %bitcast.31), channel_id=1, source_target_pairs={{0,1},{1,2},{2,3},{3,4},{4,5},{5,6},{6,7},{7,8},{8,9},{9,10},{10,1... | collective-permute-start | bytes 196616 | tf_op jit(solution)/shard_map/ppermute | solution.py:195
  7.1 0.8 copy.11
  7.9 16.0 %all_to_all.51 = s32[16,1,8]{2,1,0:T(1,128)S(1)} all-to-all(s32[16,1,8]{2,1,0:T(1,128)S(1)} %copy.11), channel_id=1, replica_groups=mesh['rows'=16,'delay'=16] {'rows'}, dimensions={0} | all-to-all | bytes 1024 | tf_op jit(solution)/shard_map/all_to_all | solution.py:199
  23.8 0.0 collective-permute-done.1.h2
  23.8 0.0 collective-permute-done.h1
  23.8 1.6 %shard_map.64 = bf16[16,24,4,128]{3,2,1,0:T(4,128)(2,1)S(1)} custom-call(s32[16,8]{1,0:T(8,128)S(1)} %bitcast.21, bf16[64,4,128]{2,1,0:T(4,128)(2,1)} %bitcast.32, bf16[64,4,128]{2,1,0:T(4,128)(2,1)S(1)} %collective-permute-done.h1, bf16[64,4,128]{2,1,0:T(4,128)(2,1)S(1)} %collective-permute-done.1.h2), custom_call_target="tpu_custom_call" | custom-call | tf_op jit(solution)/shard_map/pallas_call | solution.py:36
  25.5 16.2 %all_to_all.52.arrived = bf16[16,24,4,128]{3,2,1,0:T(4,128)(2,1)S(1)} all-to-all(bf16[16,24,4,128]{3,2,1,0:T(4,128)(2,1)S(1)} %shard_map.64), channel_id=1, replica_groups=mesh['rows'=16,'delay'=16] {'rows'}, dimensions={0} | all-to-all | bytes 786432 | tf_op jit(solution)/shard_map/all_to_all | solution.py:199
  41.6 3.8 %shard_map.65 = (bf16[16,64,128]{2,1,0:T(8,128)(2,1)S(1)}, bf16[64,4,128,128]{3,2,1,0:T(8,128)(2,1)S(1)}) custom-call(s32[4,64]{1,0:T(4,128)} %bitcast.25, bf16[64,4,128,128]{3,2,1,0:T(8,128)(2,1)} %bitcast.29, bf16[16,24,4,128]{3,2,1,0:T(4,128)(2,1)S(1)} %all_to_all.52.arrived), custom_call_target="tpu_custom_call" | custom-call | tf_op jit(solution)/shard_map/pallas_call | solution.py:36
  45.4 0.0 copy-start
  45.4 3.2 %copy-done = bf16[64,4,128,128]{3,2,1,0:T(8,128)(2,1)} copy-done((bf16[64,4,128,128]{3,2,1,0:T(8,128)(2,1)}, bf16[64,4,128,128]{3,2,1,0:T(8,128)(2,1)S(1)}, u32[]{:S(2)}) %copy-start) | copy-done | bytes 8388632
  48.6 16.9 %all_to_all.53.terms = bf16[16,64,128]{2,1,0:T(8,128)(2,1)S(1)} all-to-all(bf16[16,64,128]{2,1,0:T(8,128)(2,1)S(1)} %get-tuple-element.14), channel_id=1, replica_groups=mesh['rows'=16,'delay'=16] {'delay'}, dimensions={0} | all-to-all | bytes 524288 | tf_op jit(solution)/shard_map/all_to_all | solution.py:199
  65.6 8.4 %all_to_all.54 = f32[4,64,128]{2,1,0:T(8,128)S(1)} all-to-all(f32[4,64,128]{2,1,0:T(8,128)S(1)} %shard_map.66), channel_id=1, replica_groups={{0,1,2,3},{4,5,6,7},{8,9,10,11},{12,13,14,15},{16,17,18,19},{20,21,22,2..., dimensions={0} | all-to-all | bytes 262144 | tf_op jit(solution)/shard_map/all_to_all | solution.py:199
  74.0 0.0 copy-done.4
  74.0 0.0 copy-done.5
  74.0 2.1 %shard_map.67 = (bf16[256,128]{1,0:T(8,128)(2,1)S(1)}, bf16[16,8,4,128]{3,2,1,0:T(4,128)(2,1)}) custom-call(s32[16,8]{1,0:T(8,128)S(1)} %bitcast.22, f32[256,128]{1,0:T(8,128)S(1)} %bitcast.19, f32[4,256,128]{2,1,0:T(8,128)S(1)} %bitcast.12, bf16[64,128,128]{2,1,0:T(8,128)(2,1)S(1)} %copy-done.4), custom_call_target="tpu_custom_call" | custom-call | tf_op jit(solution)/shard_map/pallas_call | solution.py:36
  76.1 3.5 %all-to-all-start.4 = ((bf16[16,8,4,128]{3,2,1,0:T(4,128)(2,1)}), bf16[16,8,4,128]{3,2,1,0:T(4,128)(2,1)S(1)}, u32[]{:S(2)}, u32[]{:S(2)}) async-start(bf16[16,8,4,128]{3,2,1,0:T(4,128)(2,1)} %get-tuple-element.15), calls=%async_computation.4 | async-start | bytes 262144 | tf_op jit(solution)/shard_map/all_to_all | solution.py:199
  79.6 1.3 collective-permute-start.2
  80.9 7.3 %all-to-all-done.4 = bf16[16,8,4,128]{3,2,1,0:T(4,128)(2,1)S(1)} async-done(((bf16[16,8,4,128]{3,2,1,0:T(4,128)(2,1)}), bf16[16,8,4,128]{3,2,1,0:T(4,128)(2,1)S(1)}, u32[]{:S(2)}, u32[]{:S(2)}) %all-to-all-start.4) | async-done | bytes 131104 | tf_op jit(solution)/shard_map/all_to_all | solution.py:199
  88.2 0.0 copy-done.6
  88.2 0.0 copy-start.1
  88.2 3.4 %copy-done.1 = bf16[64,4,128,128]{3,2,1,0:T(8,128)(2,1)S(1)} copy-done((bf16[64,4,128,128]{3,2,1,0:T(8,128)(2,1)S(1)}, bf16[64,4,128,128]{3,2,1,0:T(8,128)(2,1)}, u32[]{:S(2)}) %copy-start.1) | copy-done | bytes 8388632
  91.6 1.8 %shard_map.68.total = f32[256,128]{1,0:T(8,128)S(1)} custom-call(s32[4,64]{1,0:T(4,128)S(1)} %bitcast.26, bf16[64,4,128,128]{3,2,1,0:T(8,128)(2,1)S(1)} %copy-done.1, bf16[128,4,128]{2,1,0:T(4,128)(2,1)S(1)} %bitcast.16), custom_call_target="tpu_custom_call" | custom-call | tf_op jit(solution)/shard_map/pallas_call | solution.py:36
  93.4 0.0 collective-permute-done.2.came
  93.4 1.4 shard_map.69
  94.8 3.5 %all-to-all-start.5 = ((bf16[16,8,4,128]{3,2,1,0:T(4,128)(2,1)}), bf16[16,8,4,128]{3,2,1,0:T(4,128)(2,1)S(1)}, u32[]{:S(2)}, u32[]{:S(2)}) async-start(bf16[16,8,4,128]{3,2,1,0:T(4,128)(2,1)} %get-tuple-element.16), calls=%async_computation.5 | async-start | bytes 262144 | tf_op jit(solution)/shard_map/all_to_all | solution.py:199
  98.3 4.1 %collective-permute-start.3 = (f32[256,128]{1,0:T(8,128)S(1)}, f32[256,128]{1,0:T(8,128)S(1)}, u32[]{:S(2)}, u32[]{:S(2)}) collective-permute-start(f32[256,128]{1,0:T(8,128)S(1)} %get-tuple-element.17), channel_id=1, source_target_pairs={{0,1},{1,0},{2,3},{3,4},{4,5},{5,6},{6,7},{7,8},{8,9},{9,10},{10,1... | collective-permute-start | bytes 393224 | tf_op jit(solution)/shard_map/ppermute | solution.py:266
  102.4 4.5 %all-to-all-done.5 = bf16[16,8,4,128]{3,2,1,0:T(4,128)(2,1)S(1)} async-done(((bf16[16,8,4,128]{3,2,1,0:T(4,128)(2,1)}), bf16[16,8,4,128]{3,2,1,0:T(4,128)(2,1)S(1)}, u32[]{:S(2)}, u32[]{:S(2)}) %all-to-all-start.5) | async-done | bytes 131104 | tf_op jit(solution)/shard_map/all_to_all | solution.py:199
  106.9 0.0 copy-start.2
  106.9 3.4 %copy-done.2 = bf16[64,4,128,128]{3,2,1,0:T(8,128)(2,1)S(1)} copy-done((bf16[64,4,128,128]{3,2,1,0:T(8,128)(2,1)S(1)}, bf16[64,4,128,128]{3,2,1,0:T(8,128)(2,1)}, u32[]{:S(2)}) %copy-start.2) | copy-done | bytes 8388632
  110.3 1.8 %shard_map.70.total = f32[256,128]{1,0:T(8,128)S(1)} custom-call(s32[4,64]{1,0:T(4,128)S(1)} %bitcast.27, bf16[64,4,128,128]{3,2,1,0:T(8,128)(2,1)S(1)} %copy-done.2, bf16[128,4,128]{2,1,0:T(4,128)(2,1)S(1)} %bitcast.17), custom_call_target="tpu_custom_call" | custom-call | tf_op jit(solution)/shard_map/pallas_call | solution.py:36
  112.1 0.0 collective-permute-done.3.came
  112.1 1.5 shard_map.71
  113.6 11.5 %all_to_all.55 = bf16[16,8,4,128]{3,2,1,0:T(4,128)(2,1)S(1)} all-to-all(bf16[16,8,4,128]{3,2,1,0:T(4,128)(2,1)S(1)} %get-tuple-element.19), channel_id=1, replica_groups=mesh['rows'=16,'delay'=16] {'rows'}, dimensions={0} | all-to-all | bytes 262144 | tf_op jit(solution)/shard_map/all_to_all | solution.py:199
  125.1 0.0 copy-start.3
  125.1 3.4 %copy-done.3 = bf16[64,4,128,128]{3,2,1,0:T(8,128)(2,1)S(1)} copy-done((bf16[64,4,128,128]{3,2,1,0:T(8,128)(2,1)S(1)}, bf16[64,4,128,128]{3,2,1,0:T(8,128)(2,1)}, u32[]{:S(2)}) %copy-start.3) | copy-done | bytes 8388632
  128.4 1.8 %shard_map.72 = bf16[16,32,128]{2,1,0:T(8,128)(2,1)S(1)} custom-call(s32[4,64]{1,0:T(4,128)S(1)} %bitcast.28, bf16[64,4,128,128]{3,2,1,0:T(8,128)(2,1)S(1)} %copy-done.3, bf16[128,4,128]{2,1,0:T(4,128)(2,1)S(1)} %bitcast.18, bf16[256,128]{1,0:T(8,128)(2,1)S(1)} %get-tuple-element.20.item), custom_call_target="tpu_custom_call" | custom-call | tf_op jit(solution)/shard_map/pallas_call | solution.py:36
  130.3 11.7 %all_to_all.56.parts = bf16[16,32,128]{2,1,0:T(8,128)(2,1)S(1)} all-to-all(bf16[16,32,128]{2,1,0:T(8,128)(2,1)S(1)} %shard_map.72), channel_id=1, replica_groups=mesh['rows'=16,'delay'=16] {'delay'}, dimensions={0} | all-to-all | bytes 262144 | tf_op jit(solution)/shard_map/all_to_all | solution.py:199
  142.0 11.8 %all_to_all.57.driven = bf16[16,64,128]{2,1,0:T(8,128)(2,1)S(1)} all-to-all(bf16[16,64,128]{2,1,0:T(8,128)(2,1)S(1)} %shard_map.73), channel_id=1, replica_groups=mesh['rows'=16,'delay'=16] {'delay'}, dimensions={0} | all-to-all | bytes 524288 | tf_op jit(solution)/shard_map/all_to_all | solution.py:199
  153.8 1.5 shard_map.74
  (2 shorter events, 0.1 us)
Async XLA Ops:
  0.0 88.2 %copy-start.6 = (s32[1,64,4]{1,2,0:T(4,128)S(1)}, s32[1,64,4]{1,2,0:T(4,128)}, u32[]{:S(2)}) copy-start(s32[1,64,4]{1,2,0:T(4,128)} %param.8) | copy-start | bytes 3076
  0.0 74.0 %copy-start.4 = (bf16[64,128,128]{2,1,0:T(8,128)(2,1)S(1)}, bf16[64,128,128]{2,1,0:T(8,128)(2,1)}, u32[]{:S(2)}) copy-start(bf16[64,128,128]{2,1,0:T(8,128)(2,1)} %diag.7) | copy-start | bytes 6291460
  0.0 74.0 %copy-start.5 = (f32[4,64,4,128]{3,2,1,0:T(4,128)S(1)}, f32[4,64,4,128]{3,2,1,0:T(4,128)}, u32[]{:S(2)}) copy-start(f32[4,64,4,128]{3,2,1,0:T(4,128)} %param.10) | copy-start | bytes 1572868
  0.0 23.8 %collective-permute-start.1 = (bf16[64,4,128]{2,1,0:T(4,128)(2,1)}, bf16[64,4,128]{2,1,0:T(4,128)(2,1)S(1)}, u32[]{:S(2)}, u32[]{:S(2)}) collective-permute-start(bf16[64,4,128]{2,1,0:T(4,128)(2,1)} %bitcast.30), channel_id=1, source_target_pairs={{0,2},{1,3},{2,4},{3,5},{4,6},{5,7},{6,8},{7,9},{8,10},{9,11},{10,... | collective-permute-start | bytes 196616 | tf_op jit(solution)/shard_map/ppermute | solution.py:195
  4.3 19.5 %collective-permute-start = (bf16[64,4,128]{2,1,0:T(4,128)(2,1)}, bf16[64,4,128]{2,1,0:T(4,128)(2,1)S(1)}, u32[]{:S(2)}, u32[]{:S(2)}) collective-permute-start(bf16[64,4,128]{2,1,0:T(4,128)(2,1)} %bitcast.31), channel_id=1, source_target_pairs={{0,1},{1,2},{2,3},{3,4},{4,5},{5,6},{6,7},{7,8},{8,9},{9,10},{10,1... | collective-permute-start | bytes 196616 | tf_op jit(solution)/shard_map/ppermute | solution.py:195
  45.4 3.2 %copy-start = (bf16[64,4,128,128]{3,2,1,0:T(8,128)(2,1)}, bf16[64,4,128,128]{3,2,1,0:T(8,128)(2,1)S(1)}, u32[]{:S(2)}) copy-start(bf16[64,4,128,128]{3,2,1,0:T(8,128)(2,1)S(1)} %get-tuple-element.13.tiles) | copy-start | bytes 25165828
  76.1 12.1 %all-to-all-start.4 = ((bf16[16,8,4,128]{3,2,1,0:T(4,128)(2,1)}), bf16[16,8,4,128]{3,2,1,0:T(4,128)(2,1)S(1)}, u32[]{:S(2)}, u32[]{:S(2)}) async-start(bf16[16,8,4,128]{3,2,1,0:T(4,128)(2,1)} %get-tuple-element.15), calls=%async_computation.4 | async-start | bytes 262144 | tf_op jit(solution)/shard_map/all_to_all | solution.py:199
  79.6 13.8 %collective-permute-start.2 = (f32[256,128]{1,0:T(8,128)S(1)}, f32[256,128]{1,0:T(8,128)S(1)}, u32[]{:S(2)}, u32[]{:S(2)}) collective-permute-start(f32[256,128]{1,0:T(8,128)S(1)} %bitcast.20), channel_id=1, source_target_pairs={{4,0},{9,1},{20,16},{25,17},{36,32},{41,33},{52,48},{57,49},{68,64... | collective-permute-start | bytes 393224 | tf_op jit(solution)/shard_map/ppermute | solution.py:248
  88.2 3.4 %copy-start.1 = (bf16[64,4,128,128]{3,2,1,0:T(8,128)(2,1)S(1)}, bf16[64,4,128,128]{3,2,1,0:T(8,128)(2,1)}, u32[]{:S(2)}) copy-start(bf16[64,4,128,128]{3,2,1,0:T(8,128)(2,1)} %copy-done) | copy-start | bytes 25165828
  94.8 12.1 %all-to-all-start.5 = ((bf16[16,8,4,128]{3,2,1,0:T(4,128)(2,1)}), bf16[16,8,4,128]{3,2,1,0:T(4,128)(2,1)S(1)}, u32[]{:S(2)}, u32[]{:S(2)}) async-start(bf16[16,8,4,128]{3,2,1,0:T(4,128)(2,1)} %get-tuple-element.16), calls=%async_computation.5 | async-start | bytes 262144 | tf_op jit(solution)/shard_map/all_to_all | solution.py:199
  98.3 13.8 %collective-permute-start.3 = (f32[256,128]{1,0:T(8,128)S(1)}, f32[256,128]{1,0:T(8,128)S(1)}, u32[]{:S(2)}, u32[]{:S(2)}) collective-permute-start(f32[256,128]{1,0:T(8,128)S(1)} %get-tuple-element.17), channel_id=1, source_target_pairs={{0,1},{1,0},{2,3},{3,4},{4,5},{5,6},{6,7},{7,8},{8,9},{9,10},{10,1... | collective-permute-start | bytes 393224 | tf_op jit(solution)/shard_map/ppermute | solution.py:266
  106.9 3.4 %copy-start.2 = (bf16[64,4,128,128]{3,2,1,0:T(8,128)(2,1)S(1)}, bf16[64,4,128,128]{3,2,1,0:T(8,128)(2,1)}, u32[]{:S(2)}) copy-start(bf16[64,4,128,128]{3,2,1,0:T(8,128)(2,1)} %copy-done) | copy-start | bytes 25165828
  125.1 3.4 %copy-start.3 = (bf16[64,4,128,128]{3,2,1,0:T(8,128)(2,1)S(1)}, bf16[64,4,128,128]{3,2,1,0:T(8,128)(2,1)}, u32[]{:S(2)}) copy-start(bf16[64,4,128,128]{3,2,1,0:T(8,128)(2,1)} %copy-done) | copy-start | bytes 25165828

commit v5 on v4

v5 whole, which is shorter than its diff:
```python
import jax
import jax.numpy as jnp
from jax import lax
from jax.experimental import pallas as pl
from jax.experimental.pallas import tpu as pltpu
from jax.sharding import PartitionSpec as P


STEPS = 4
LANES = 16
ROWS = 16
CAP = 8
NB = 64
EXC = 4
B = 128
L = 4
TAKEN = ROWS * CAP
FLAT = NB * EXC
KNOWN = 3
GIVERS = (4, 9)
SHARE = FLAT // LANES
GROUP = 16

bf16 = jnp.bfloat16
f32 = jnp.float32
VMEM = pl.BlockSpec(memory_space=pltpu.VMEM)
SMEM = pl.BlockSpec(memory_space=pltpu.SMEM)
HBM = pl.BlockSpec(memory_space=pltpu.HBM)
LIMIT = 16 * 1024 * 1024


def call(kernel, out_shape, scratch, operands, in_smem, in_place=(), out_in_place=False):
    specs = [SMEM if i in in_smem else HBM if i in in_place else VMEM for i in range(len(operands))]
    many = isinstance(out_shape, (tuple, list))
    operands = [pltpu.with_memory_space_constraint(x, pltpu.HBM) if i in in_place else x for i, x in enumerate(operands)]
    return pl.pallas_call(
        kernel,
        out_shape=out_shape,
        in_specs=specs,
        out_specs=[VMEM] * len(out_shape) if many else (HBM if out_in_place else VMEM),
        scratch_shapes=scratch,
        compiler_params=pltpu.CompilerParams(vmem_limit_bytes=LIMIT),
    )(*operands)


def pick_initial(asked, stored, tiles, h1, h2, out, h0, sem):
    copy = pltpu.make_async_copy(stored, h0, sem)
    copy.start()
    for r in range(ROWS):
        for p in range(CAP):
            at = asked[r, p]
            out[r, CAP + p] = h1[at]
            out[r, 2 * CAP + p] = h2[at]
    copy.wait()
    for r in range(ROWS):
        for p in range(CAP):
            out[r, p] = h0[asked[r, p]]


def initial_terms(slots, tiles, arrived, out, wide, packed, total):
    for o in range(ROWS):
        for t in range(KNOWN):
            here = arrived[o, CAP * t : CAP * (t + 1)]
            wide[CAP * o : CAP * (o + 1), EXC * t : EXC * (t + 1), :] = here.astype(f32)
    packed[...] = wide[...].astype(bf16)
    for i in range(NB):
        row = jnp.concatenate([packed[slots[s, i]] for s in range(L)], axis=1)
        tile = tiles[i].reshape(L * B, B)
        term = jnp.dot(row, tile, preferred_element_type=f32)
        for t in range(KNOWN):
            total[t, EXC * i : EXC * (i + 1), :] = term[EXC * t : EXC * (t + 1)]

    for y in range(4):
        out[y] = total[y % KNOWN].astype(bf16)


def add_terms(terms, out):
    total = sum(terms[y].astype(f32) for y in range(4)).astype(bf16)
    for x in range(4):
        out[x] = total


def solve(driven, diag, solved):
    for i in range(NB):
        row = driven[EXC * i : EXC * (i + 1), :].astype(bf16)
        solved[i] = jnp.dot(row, diag[i], preferred_element_type=f32)


def pick(fetch, asked, solved, send):
    fetch.wait()
    for r in range(ROWS):
        for p in range(CAP):
            send[r, p] = solved[asked[r, p]].astype(bf16)


def older(h2, item):
    for i in range(NB):
        item[EXC * i : EXC * (i + 1), :] = h2[i].astype(f32)


def first_step(listed, terms, h2, excite, diag, moved, item, send, driven, solved, asked, sem):
    fetch = pltpu.make_async_copy(listed, asked, sem)
    fetch.start()
    me = lax.axis_index("delay")
    whole = sum(terms[x].astype(f32) for x in range(4))
    driven[...] = excite[0] - whole
    gives = (me == GIVERS[0]) | (me == GIVERS[1])

    @pl.when(gives)
    def _():
        moved[...] = whole

    @pl.when(jnp.logical_not(gives))
    def _():
        older(h2, moved)

    item[...] = driven[...].astype(bf16)
    solve(driven, diag, solved)
    pick(fetch, asked, solved, send)


def tile_terms(slots, tiles, arrived, total):
    for i in range(NB):
        row = jnp.concatenate([arrived[slots[s, i]] for s in range(L)], axis=1)
        tile = tiles[i].reshape(L * B, B)
        total[EXC * i : EXC * (i + 1), :] = jnp.dot(row, tile, preferred_element_type=f32)


def second_step(listed, total, came, h2, excite, diag, item, send, driven, solved, asked, sem):
    fetch = pltpu.make_async_copy(listed, asked, sem)
    fetch.start()
    me = lax.axis_index("delay")
    value = total[...] + came[...]
    driven[...] = excite[1] - value

    @pl.when(me == 0)
    def _():
        item[...] = driven[...].astype(bf16).astype(f32)
        solve(driven, diag, solved)
        pick(fetch, asked, solved, send)

    @pl.when(me != 0)
    def _():
        fetch.wait()

    @pl.when(me == 1)
    def _():
        item[...] = value

    @pl.when(me > 1)
    def _():
        older(h2, item)


def third_step(listed, total, came, before, first, excite, diag, item, send, driven, solved, asked, sem):
    fetch = pltpu.make_async_copy(listed, asked, sem)
    fetch.start()
    me = lax.axis_index("delay")
    late = (me == 1) | (me == GIVERS[0] + 1) | (me == GIVERS[1] + 1)
    other = jnp.where(me == 2, first[...].astype(f32), jnp.where(late, came[...], before[...]))
    driven[...] = jnp.where(me == 0, excite[2] - (total[...] + came[...]), other)
    item[...] = driven[...].astype(bf16)

    @pl.when(me < KNOWN)
    def _():
        solve(driven, diag, solved)

    @pl.when(me >= KNOWN)
    def _():
        for i in range(NB):
            solved[i] = driven[EXC * i : EXC * (i + 1), :]

    pick(fetch, asked, solved, send)


def fourth_step(slots, tiles, arrived, item, out, total):
    tile_terms(slots, tiles, arrived, total)
    for k in range(LANES):
        mine = slice(SHARE * k, SHARE * (k + 1))
        out[k, :SHARE] = total[mine, :].astype(bf16)
        out[k, SHARE:] = item[mine, :]


def share_driven(parts, excite, out):
    total = parts[0, :SHARE].astype(f32)
    for k in range(1, LANES):
        total = total + parts[k, :SHARE].astype(f32)
    start = pl.multiple_of(lax.axis_index("delay") * SHARE, SHARE)
    last = (excite[STEPS - 1, pl.ds(start, SHARE), :] - total).astype(bf16)
    for k in range(LANES):
        for t in range(STEPS - 1):
            out[k, SHARE * t : SHARE * (t + 1)] = parts[STEPS - 2 - t, SHARE:]
        out[k, SHARE * (STEPS - 1) :] = last


def last_solve(driven, diag, stored, out, sems):
    each = SHARE // EXC
    copies = []
    for i in range(NB):
        value = jnp.dot(driven[i // each], diag[i], preferred_element_type=f32)
        for t in range(STEPS):
            at = SHARE * t + EXC * (i % each)
            out[t, i] = value[at : at + EXC]
        if i % GROUP == GROUP - 1:
            for t in range(STEPS):
                part = (t, pl.ds(i - GROUP + 1, GROUP))
                copies.append(pltpu.make_async_copy(out.at[part], stored.at[part], sems.at[len(copies)]))
                copies[-1].start()
    for copy in copies:
        copy.wait()


def shifted(array, axis, by):
    peers = lax.axis_size(axis)
    return lax.ppermute(array, axis, [(i, i + by) for i in range(peers - by)])


def exchange(array, axis, groups=None):
    return lax.all_to_all(array, axis, split_axis=0, concat_axis=0, tiled=True, axis_index_groups=groups)


def body(retarded_tiles, wanted_blocks, tile_slots, diag_inverse, excitation, history_init):
    sds = jax.ShapeDtypeStruct
    tiles = retarded_tiles[0]
    slots = tile_slots[0].T
    excite = excitation.reshape(STEPS, FLAT, B)

    asked = exchange(wanted_blocks[0, 0], "rows")
    h0 = history_init[0]
    later = []
    for t in range(1, KNOWN):
        later.append(shifted(h0, "delay", t))

    picked = call(
        pick_initial,
        sds((ROWS, KNOWN * CAP, EXC, B), bf16),
        [pltpu.VMEM(h0.shape, bf16), pltpu.SemaphoreType.DMA],
        (asked, h0, tiles, *later),
        (0,),
        (1, 2),
    )
    arrived = exchange(picked, "rows")
    wide = (TAKEN, EXC * STEPS, B)
    terms = call(
        initial_terms,
        sds((4, FLAT, B), bf16),
        [pltpu.VMEM(wide, f32), pltpu.VMEM(wide, bf16), pltpu.VMEM((KNOWN, FLAT, B), f32)],
        (slots, tiles, arrived),
        (0,),
    )
    along_x = [[4 * y + x for x in range(4)] for y in range(4)]
    along_y = [[4 * y + x for y in range(4)] for x in range(4)]
    terms = exchange(terms, "delay", along_y)
    terms = call(add_terms, sds((4, FLAT, B), bf16), [], (terms,), ())
    terms = exchange(terms, "delay", along_x)

    flat = pltpu.VMEM((FLAT, B), f32)
    block = pltpu.VMEM((NB, EXC, B), f32)
    work = [flat, block, pltpu.SMEM((ROWS, CAP), jnp.int32), pltpu.SemaphoreType.DMA]
    send_shape = sds((ROWS, CAP, EXC, B), bf16)

    moved, item0, send = call(
        first_step,
        (sds((FLAT, B), f32), sds((FLAT, B), bf16), send_shape),
        work,
        (asked, terms, later[1], excite, diag_inverse),
        (),
    )
    steps = [(k, k + 1) for k in range(2, LANES - 1)]
    pairs = [(k, j) for k, j in steps if k not in GIVERS]
    before = lax.ppermute(moved, "delay", [(GIVERS[0], 0), (GIVERS[1], 1)] + pairs)
    arrived = exchange(send, "rows").reshape(TAKEN, EXC, B)
    total = call(tile_terms, sds((FLAT, B), f32), [], (slots, tiles, arrived), (0,))

    item1, send = call(
        second_step,
        (sds((FLAT, B), f32), send_shape),
        work,
        (asked, total, before, later[1], excite, diag_inverse),
        (),
    )
    came = lax.ppermute(item1, "delay", [(0, 1), (1, 0)] + [(k, j) for k, j in steps if k in GIVERS])
    arrived = exchange(send, "rows").reshape(TAKEN, EXC, B)
    total = call(tile_terms, sds((FLAT, B), f32), [], (slots, tiles, arrived), (0,))

    item2, send = call(
        third_step,
        (sds((FLAT, B), bf16), send_shape),
        work,
        (asked, total, came, before, item0, excite, diag_inverse),
        (),
    )
    arrived = exchange(send, "rows").reshape(TAKEN, EXC, B)
    parts = call(
        fourth_step, sds((LANES, 2 * SHARE, B), bf16), [flat], (slots, tiles, arrived, item2), (0,)
    )
    parts = exchange(parts, "delay")
    shares = call(share_driven, sds((LANES, STEPS * SHARE, B), bf16), [], (parts, excite), ())
    driven = exchange(shares, "delay")
    final = (STEPS, NB, EXC, B)
    return call(
        last_solve,
        sds(final, f32),
        [pltpu.VMEM(final, f32), pltpu.SemaphoreType.DMA((STEPS * NB // GROUP,))],
        (driven, diag_inverse),
        (),
        out_in_place=True,
    )


def solution(mesh):
    return jax.shard_map(
        body,
        mesh=mesh,
        in_specs=(
            P("delay", "rows", None, None, None),
            P("delay", "rows", None, None),
            P("delay", "rows", None),
            P("rows", None, None),
            P(None, "rows", None, None),
            P("delay", "rows", None, None),
        ),
        out_specs=P(None, "rows", None, None),
        check_vma=False,
    )
```

time: 156 us -> 147 us (0.942)
  local copies, waits for them, and re-layouts: 14.1 us -> 10.9 us
  Pallas kernels: 17.3 us -> 14.3 us
  blocking collectives: 92.4 us -> 90.1 us
    unnamed x14, local copies, waits for them, and re-layouts: 13.4 us -> 10.2 us
    pallas_call x11, Pallas kernels: 17.3 us -> 14.3 us  [call(): pl.pallas_call(kernel, out_shape=out_shape, in_specs=specs, out_specs=[VM...]
    all_to_all x7, blocking collectives: 92.4 us -> 90.1 us  [exchange(): lax.all_to_all(array, axis, split_axis=0, concat_axis=0, tiled=True, axis...]
  transfers between devices with their start and end apart: 6 -> 6, of which waited for: 2 -> 2; matrix products, arithmetic and copies ran while one was open for 0% -> 1% of each run, Pallas kernels for 2% -> 2%
where the time goes in v5:
time: 147 us
  blocking collectives  90.1 us (61%)
  starting transfers between devices  18.8 us (13%)
  Pallas kernels  14.3 us (10%)
  waiting for transfers between devices  12.4 us (8%)
  local copies, waits for them, and re-layouts  10.9 us (7%)
    all_to_all x7, blocking collectives, exchange(): lax.all_to_all(array, axis, split_axis=0, concat_axis=0, tiled=True, axis...  90.1 us
    pallas_call x11, Pallas kernels, call(): pl.pallas_call(kernel, out_shape=out_shape, in_specs=specs, out_specs=[VM...  14.3 us
    all_to_all x2, waiting for transfers between devices, exchange(): lax.all_to_all(array, axis, split_axis=0, concat_axis=0, tiled=True, axis...  12.4 us
    unnamed x14, local copies, waits for them, and re-layouts  10.2 us
    all_to_all x2, starting transfers between devices, exchange(): lax.all_to_all(array, axis, split_axis=0, concat_axis=0, tiled=True, axis...  7.05 us
    ppermute x2, starting transfers between devices, shifted(): return lax.ppermute(array, axis, [(i, i + by) for i in range(peers - by)])  6.95 us
    ppermute x1, starting transfers between devices, body(): lax.ppermute(item1, 'delay', [(0, 1), (1, 0)] + [(k, j) for k, j in steps...  3.5 us
  transfers between devices with their start and end apart: 6, of which 2 were waited for; matrix products, arithmetic and copies ran while one was open for 1% of the time, Pallas kernels for 2%

profile of v5, /device:TPU:2, one launch (start us, length us, event | category | flops | bytes accessed | tf_op | source)
XLA Modules:
  0.0 146.7 jit_solution(12234122322693879732)
XLA Ops:
  0.0 0.0 copy-start.6
  0.0 4.2 %collective-permute-start.1 = (bf16[64,4,128]{2,1,0:T(4,128)(2,1)}, bf16[64,4,128]{2,1,0:T(4,128)(2,1)S(1)}, u32[]{:S(2)}, u32[]{:S(2)}) collective-permute-start(bf16[64,4,128]{2,1,0:T(4,128)(2,1)} %bitcast.31), channel_id=1, source_target_pairs={{0,2},{1,3},{2,4},{3,5},{4,6},{5,7},{6,8},{7,9},{8,10},{9,11},{10,... | collective-permute-start | bytes 196616 | tf_op jit(solution)/shard_map/ppermute | solution.py:215
  4.2 2.8 %collective-permute-start = (bf16[64,4,128]{2,1,0:T(4,128)(2,1)}, bf16[64,4,128]{2,1,0:T(4,128)(2,1)S(1)}, u32[]{:S(2)}, u32[]{:S(2)}) collective-permute-start(bf16[64,4,128]{2,1,0:T(4,128)(2,1)} %bitcast.32), channel_id=1, source_target_pairs={{0,1},{1,2},{2,3},{3,4},{4,5},{5,6},{6,7},{7,8},{8,9},{9,10},{10,1... | collective-permute-start | bytes 196616 | tf_op jit(solution)/shard_map/ppermute | solution.py:215
  7.0 0.8 copy.11
  7.7 0.0 copy-start
  7.7 16.2 %all_to_all.51 = s32[16,1,8]{2,1,0:T(1,128)S(1)} all-to-all(s32[16,1,8]{2,1,0:T(1,128)S(1)} %copy.11), channel_id=1, replica_groups=mesh['rows'=16,'delay'=16] {'rows'}, dimensions={0} | all-to-all | bytes 1024 | tf_op jit(solution)/shard_map/all_to_all | solution.py:219
  24.0 0.0 collective-permute-done.1.h2
  24.0 0.0 collective-permute-done.h1
  24.0 0.0 copy-start.4
  24.0 0.0 copy-start.5
  24.0 1.7 %shard_map.64 = bf16[16,24,4,128]{3,2,1,0:T(4,128)(2,1)S(1)} custom-call(s32[16,8]{1,0:T(8,128)S(1)} %bitcast.23, bf16[64,4,128]{2,1,0:T(4,128)(2,1)} %bitcast.33, bf16[64,4,128,128]{3,2,1,0:T(8,128)(2,1)} %bitcast.11, bf16[64,4,128]{2,1,0:T(4,128)(2,1)S(1)} %collective-permute-done.h1, bf16[64,4,128]{2,1,0:T(4,128)(2,1)S(1)} %collective-permute-done.1.h2), custom_call_target="tpu_custom_call" | custom-call | tf_op jit(solution)/shard_map/pallas_call | solution.py:36
  25.7 16.2 %all_to_all.52.arrived = bf16[16,24,4,128]{3,2,1,0:T(4,128)(2,1)S(1)} all-to-all(bf16[16,24,4,128]{3,2,1,0:T(4,128)(2,1)S(1)} %shard_map.64), channel_id=1, replica_groups=mesh['rows'=16,'delay'=16] {'rows'}, dimensions={0} | all-to-all | bytes 786432 | tf_op jit(solution)/shard_map/all_to_all | solution.py:219
  41.9 0.0 copy-done.6
  41.9 0.0 copy-done
  41.9 1.9 %shard_map.65 = bf16[4,256,128]{2,1,0:T(8,128)(2,1)S(1)} custom-call(s32[4,64]{1,0:T(4,128)S(1)} %bitcast.27, bf16[64,4,128,128]{3,2,1,0:T(8,128)(2,1)S(1)} %bitcast.12, bf16[16,24,4,128]{3,2,1,0:T(4,128)(2,1)S(1)} %all_to_all.52.arrived), custom_call_target="tpu_custom_call" | custom-call | tf_op jit(solution)/shard_map/pallas_call | solution.py:36
  43.8 12.0 %all_to_all.53.terms = bf16[4,256,128]{2,1,0:T(8,128)(2,1)S(1)} all-to-all(bf16[4,256,128]{2,1,0:T(8,128)(2,1)S(1)} %shard_map.65), channel_id=1, replica_groups={{0,4,8,12},{1,5,9,13},{2,6,10,14},{3,7,11,15},{16,20,24,28},{17,21,25,2..., dimensions={0} | all-to-all | bytes 524288 | tf_op jit(solution)/shard_map/all_to_all | solution.py:219
  55.9 11.3 %all_to_all.54.terms = bf16[4,256,128]{2,1,0:T(8,128)(2,1)S(1)} all-to-all(bf16[4,256,128]{2,1,0:T(8,128)(2,1)S(1)} %shard_map.66), channel_id=1, replica_groups={{0,1,2,3},{4,5,6,7},{8,9,10,11},{12,13,14,15},{16,17,18,19},{20,21,22,2..., dimensions={0} | all-to-all | bytes 524288 | tf_op jit(solution)/shard_map/all_to_all | solution.py:219
  67.2 0.0 copy-done.4
  67.2 0.0 copy-done.5
  67.2 1.5 %shard_map.67 = (f32[256,128]{1,0:T(8,128)S(1)}, bf16[256,128]{1,0:T(8,128)(2,1)S(1)}, bf16[16,8,4,128]{3,2,1,0:T(4,128)(2,1)}) custom-call(s32[16,8]{1,0:T(8,128)S(1)} %bitcast.24, bf16[4,256,128]{2,1,0:T(8,128)(2,1)S(1)} %all_to_all.54.terms, bf16[64,4,128]{2,1,0:T(4,128)(2,1)S(1)} %collective-permute-done.1.h2, f32[4,256,128]{2,1,0:T(8,128)S(1)} %bitcast.16, ...), custom_call_target="tpu_custom_call" | custom-call | tf_op jit(solution)/shard_map/pallas_call | solution.py:36
  68.7 3.5 %all-to-all-start.4 = ((bf16[16,8,4,128]{3,2,1,0:T(4,128)(2,1)}), bf16[16,8,4,128]{3,2,1,0:T(4,128)(2,1)S(1)}, u32[]{:S(2)}, u32[]{:S(2)}) async-start(bf16[16,8,4,128]{3,2,1,0:T(4,128)(2,1)} %get-tuple-element.12), calls=%async_computation.4 | async-start | bytes 262144 | tf_op jit(solution)/shard_map/all_to_all | solution.py:219
  72.3 1.3 collective-permute-start.2
  73.6 7.3 %all-to-all-done.4 = bf16[16,8,4,128]{3,2,1,0:T(4,128)(2,1)S(1)} async-done(((bf16[16,8,4,128]{3,2,1,0:T(4,128)(2,1)}), bf16[16,8,4,128]{3,2,1,0:T(4,128)(2,1)S(1)}, u32[]{:S(2)}, u32[]{:S(2)}) %all-to-all-start.4) | async-done | bytes 131104 | tf_op jit(solution)/shard_map/all_to_all | solution.py:219
  80.9 0.0 copy-start.1
  80.9 3.4 %copy-done.1 = bf16[1,64,4,128,128]{4,3,2,1,0:T(8,128)(2,1)S(1)} copy-done((bf16[1,64,4,128,128]{4,3,2,1,0:T(8,128)(2,1)S(1)}, bf16[1,64,4,128,128]{4,3,2,1,0:T(8,128)(2,1)}, u32[]{:S(2)}) %copy-start.1) | copy-done | bytes 8388632
  84.3 1.8 %shard_map.68.total = f32[256,128]{1,0:T(8,128)S(1)} custom-call(s32[4,64]{1,0:T(4,128)S(1)} %bitcast.28, bf16[64,4,128,128]{3,2,1,0:T(8,128)(2,1)S(1)} %bitcast.13, bf16[128,4,128]{2,1,0:T(4,128)(2,1)S(1)} %bitcast.21), custom_call_target="tpu_custom_call" | custom-call | tf_op jit(solution)/shard_map/pallas_call | solution.py:36
  86.0 0.0 collective-permute-done.2.came.before
  86.1 1.4 shard_map.69
  87.4 3.5 %all-to-all-start.5 = ((bf16[16,8,4,128]{3,2,1,0:T(4,128)(2,1)}), bf16[16,8,4,128]{3,2,1,0:T(4,128)(2,1)S(1)}, u32[]{:S(2)}, u32[]{:S(2)}) async-start(bf16[16,8,4,128]{3,2,1,0:T(4,128)(2,1)} %get-tuple-element.14), calls=%async_computation.5 | async-start | bytes 262144 | tf_op jit(solution)/shard_map/all_to_all | solution.py:219
  90.9 3.5 %collective-permute-start.3 = (f32[256,128]{1,0:T(8,128)S(1)}, f32[256,128]{1,0:T(8,128)S(1)}, u32[]{:S(2)}, u32[]{:S(2)}) collective-permute-start(f32[256,128]{1,0:T(8,128)S(1)} %get-tuple-element.15), channel_id=1, source_target_pairs={{0,1},{1,0},{4,5},{9,10},{16,17},{17,16},{20,21},{25,26},{32,33},{... | collective-permute-start | bytes 393224 | tf_op jit(solution)/shard_map/ppermute | solution.py:282
  94.5 5.1 %all-to-all-done.5 = bf16[16,8,4,128]{3,2,1,0:T(4,128)(2,1)S(1)} async-done(((bf16[16,8,4,128]{3,2,1,0:T(4,128)(2,1)}), bf16[16,8,4,128]{3,2,1,0:T(4,128)(2,1)S(1)}, u32[]{:S(2)}, u32[]{:S(2)}) %all-to-all-start.5) | async-done | bytes 131104 | tf_op jit(solution)/shard_map/all_to_all | solution.py:219
  99.6 0.0 copy-start.2
  99.6 3.4 %copy-done.2 = bf16[1,64,4,128,128]{4,3,2,1,0:T(8,128)(2,1)S(1)} copy-done((bf16[1,64,4,128,128]{4,3,2,1,0:T(8,128)(2,1)S(1)}, bf16[1,64,4,128,128]{4,3,2,1,0:T(8,128)(2,1)}, u32[]{:S(2)}) %copy-start.2) | copy-done | bytes 8388632
  103.0 1.8 %shard_map.70.total = f32[256,128]{1,0:T(8,128)S(1)} custom-call(s32[4,64]{1,0:T(4,128)S(1)} %bitcast.29, bf16[64,4,128,128]{3,2,1,0:T(8,128)(2,1)S(1)} %bitcast.14, bf16[128,4,128]{2,1,0:T(4,128)(2,1)S(1)} %bitcast.20), custom_call_target="tpu_custom_call" | custom-call | tf_op jit(solution)/shard_map/pallas_call | solution.py:36
  104.7 0.0 collective-permute-done.3.came
  104.7 0.8 shard_map.71
  105.6 11.5 %all_to_all.55 = bf16[16,8,4,128]{3,2,1,0:T(4,128)(2,1)S(1)} all-to-all(bf16[16,8,4,128]{3,2,1,0:T(4,128)(2,1)S(1)} %get-tuple-element.17), channel_id=1, replica_groups=mesh['rows'=16,'delay'=16] {'rows'}, dimensions={0} | all-to-all | bytes 262144 | tf_op jit(solution)/shard_map/all_to_all | solution.py:219
  117.1 0.0 copy-start.3
  117.1 3.4 %copy-done.3 = bf16[1,64,4,128,128]{4,3,2,1,0:T(8,128)(2,1)S(1)} copy-done((bf16[1,64,4,128,128]{4,3,2,1,0:T(8,128)(2,1)S(1)}, bf16[1,64,4,128,128]{4,3,2,1,0:T(8,128)(2,1)}, u32[]{:S(2)}) %copy-start.3) | copy-done | bytes 8388632
  120.5 1.8 %shard_map.72 = bf16[16,32,128]{2,1,0:T(8,128)(2,1)S(1)} custom-call(s32[4,64]{1,0:T(4,128)S(1)} %bitcast.30, bf16[64,4,128,128]{3,2,1,0:T(8,128)(2,1)S(1)} %bitcast.15, bf16[128,4,128]{2,1,0:T(4,128)(2,1)S(1)} %bitcast.22, bf16[256,128]{1,0:T(8,128)(2,1)S(1)} %get-tuple-element.18.item), custom_call_target="tpu_custom_call" | custom-call | tf_op jit(solution)/shard_map/pallas_call | solution.py:36
  122.3 11.1 %all_to_all.56.parts = bf16[16,32,128]{2,1,0:T(8,128)(2,1)S(1)} all-to-all(bf16[16,32,128]{2,1,0:T(8,128)(2,1)S(1)} %shard_map.72), channel_id=1, replica_groups=mesh['rows'=16,'delay'=16] {'delay'}, dimensions={0} | all-to-all | bytes 262144 | tf_op jit(solution)/shard_map/all_to_all | solution.py:219
  133.4 11.8 %all_to_all.57.driven = bf16[16,64,128]{2,1,0:T(8,128)(2,1)S(1)} all-to-all(bf16[16,64,128]{2,1,0:T(8,128)(2,1)S(1)} %shard_map.73), channel_id=1, replica_groups=mesh['rows'=16,'delay'=16] {'delay'}, dimensions={0} | all-to-all | bytes 524288 | tf_op jit(solution)/shard_map/all_to_all | solution.py:219
  145.2 1.5 %shard_map.74 = f32[4,64,4,128]{3,2,1,0:T(4,128)} custom-call(bf16[16,64,128]{2,1,0:T(8,128)(2,1)S(1)} %all_to_all.57.driven, bf16[64,128,128]{2,1,0:T(8,128)(2,1)S(1)} %copy-done.4), custom_call_target="tpu_custom_call" | custom-call | tf_op jit(solution)/shard_map/pallas_call | solution.py:36
  (2 shorter events, 0.1 us)
Async XLA Ops:
  0.0 41.9 %copy-start.6 = (s32[1,64,4]{1,2,0:T(4,128)S(1)}, s32[1,64,4]{1,2,0:T(4,128)}, u32[]{:S(2)}) copy-start(s32[1,64,4]{1,2,0:T(4,128)} %param.8) | copy-start | bytes 3076
  0.0 24.0 %collective-permute-start.1 = (bf16[64,4,128]{2,1,0:T(4,128)(2,1)}, bf16[64,4,128]{2,1,0:T(4,128)(2,1)S(1)}, u32[]{:S(2)}, u32[]{:S(2)}) collective-permute-start(bf16[64,4,128]{2,1,0:T(4,128)(2,1)} %bitcast.31), channel_id=1, source_target_pairs={{0,2},{1,3},{2,4},{3,5},{4,6},{5,7},{6,8},{7,9},{8,10},{9,11},{10,... | collective-permute-start | bytes 196616 | tf_op jit(solution)/shard_map/ppermute | solution.py:215
  4.2 19.8 %collective-permute-start = (bf16[64,4,128]{2,1,0:T(4,128)(2,1)}, bf16[64,4,128]{2,1,0:T(4,128)(2,1)S(1)}, u32[]{:S(2)}, u32[]{:S(2)}) collective-permute-start(bf16[64,4,128]{2,1,0:T(4,128)(2,1)} %bitcast.32), channel_id=1, source_target_pairs={{0,1},{1,2},{2,3},{3,4},{4,5},{5,6},{6,7},{7,8},{8,9},{9,10},{10,1... | collective-permute-start | bytes 196616 | tf_op jit(solution)/shard_map/ppermute | solution.py:215
  7.7 34.1 %copy-start = (bf16[1,64,4,128,128]{4,3,2,1,0:T(8,128)(2,1)S(1)}, bf16[1,64,4,128,128]{4,3,2,1,0:T(8,128)(2,1)}, u32[]{:S(2)}) copy-start(bf16[1,64,4,128,128]{4,3,2,1,0:T(8,128)(2,1)} %param.6) | copy-start | bytes 25165828
  24.0 43.2 %copy-start.4 = (bf16[64,128,128]{2,1,0:T(8,128)(2,1)S(1)}, bf16[64,128,128]{2,1,0:T(8,128)(2,1)}, u32[]{:S(2)}) copy-start(bf16[64,128,128]{2,1,0:T(8,128)(2,1)} %diag.7) | copy-start | bytes 6291460
  24.0 43.2 %copy-start.5 = (f32[4,64,4,128]{3,2,1,0:T(4,128)S(1)}, f32[4,64,4,128]{3,2,1,0:T(4,128)}, u32[]{:S(2)}) copy-start(f32[4,64,4,128]{3,2,1,0:T(4,128)} %param.10) | copy-start | bytes 1572868
  68.7 12.2 %all-to-all-start.4 = ((bf16[16,8,4,128]{3,2,1,0:T(4,128)(2,1)}), bf16[16,8,4,128]{3,2,1,0:T(4,128)(2,1)S(1)}, u32[]{:S(2)}, u32[]{:S(2)}) async-start(bf16[16,8,4,128]{3,2,1,0:T(4,128)(2,1)} %get-tuple-element.12), calls=%async_computation.4 | async-start | bytes 262144 | tf_op jit(solution)/shard_map/all_to_all | solution.py:219
  72.3 13.8 %collective-permute-start.2 = (f32[256,128]{1,0:T(8,128)S(1)}, f32[256,128]{1,0:T(8,128)S(1)}, u32[]{:S(2)}, u32[]{:S(2)}) collective-permute-start(f32[256,128]{1,0:T(8,128)S(1)} %get-tuple-element.13), channel_id=1, source_target_pairs={{4,0},{9,1},{2,3},{3,4},{5,6},{6,7},{7,8},{8,9},{10,11},{11,12},{1... | collective-permute-start | bytes 393224 | tf_op jit(solution)/shard_map/ppermute | solution.py:271
  80.9 3.4 %copy-start.1 = (bf16[1,64,4,128,128]{4,3,2,1,0:T(8,128)(2,1)S(1)}, bf16[1,64,4,128,128]{4,3,2,1,0:T(8,128)(2,1)}, u32[]{:S(2)}) copy-start(bf16[1,64,4,128,128]{4,3,2,1,0:T(8,128)(2,1)} %param.6) | copy-start | bytes 25165828
  87.4 12.2 %all-to-all-start.5 = ((bf16[16,8,4,128]{3,2,1,0:T(4,128)(2,1)}), bf16[16,8,4,128]{3,2,1,0:T(4,128)(2,1)S(1)}, u32[]{:S(2)}, u32[]{:S(2)}) async-start(bf16[16,8,4,128]{3,2,1,0:T(4,128)(2,1)} %get-tuple-element.14), calls=%async_computation.5 | async-start | bytes 262144 | tf_op jit(solution)/shard_map/all_to_all | solution.py:219
  90.9 13.8 %collective-permute-start.3 = (f32[256,128]{1,0:T(8,128)S(1)}, f32[256,128]{1,0:T(8,128)S(1)}, u32[]{:S(2)}, u32[]{:S(2)}) collective-permute-start(f32[256,128]{1,0:T(8,128)S(1)} %get-tuple-element.15), channel_id=1, source_target_pairs={{0,1},{1,0},{4,5},{9,10},{16,17},{17,16},{20,21},{25,26},{32,33},{... | collective-permute-start | bytes 393224 | tf_op jit(solution)/shard_map/ppermute | solution.py:282
  99.6 3.4 %copy-start.2 = (bf16[1,64,4,128,128]{4,3,2,1,0:T(8,128)(2,1)S(1)}, bf16[1,64,4,128,128]{4,3,2,1,0:T(8,128)(2,1)}, u32[]{:S(2)}) copy-start(bf16[1,64,4,128,128]{4,3,2,1,0:T(8,128)(2,1)} %param.6) | copy-start | bytes 25165828
  117.1 3.4 %copy-start.3 = (bf16[1,64,4,128,128]{4,3,2,1,0:T(8,128)(2,1)S(1)}, bf16[1,64,4,128,128]{4,3,2,1,0:T(8,128)(2,1)}, u32[]{:S(2)}) copy-start(bf16[1,64,4,128,128]{4,3,2,1,0:T(8,128)(2,1)} %param.6) | copy-start | bytes 25165828

commit v6 on v5

--- a/solution.py
+++ b/solution.py
@@ -43,9 +43,12 @@
     )(*operands)
 
 
-def pick_initial(asked, stored, tiles, h1, h2, out, h0, sem):
+def pick_initial(listed, stored, tiles, h1, h2, out, h0, asked, sem, list_sem):
     copy = pltpu.make_async_copy(stored, h0, sem)
     copy.start()
+    fetch = pltpu.make_async_copy(listed, asked, list_sem)
+    fetch.start()
+    fetch.wait()
     for r in range(ROWS):
         for p in range(CAP):
             at = asked[r, p]
@@ -181,31 +184,34 @@
         out[k, SHARE:] = item[mine, :]
 
 
-def share_driven(parts, excite, out):
+def share_driven(parts, excite, out, rows):
     total = parts[0, :SHARE].astype(f32)
     for k in range(1, LANES):
         total = total + parts[k, :SHARE].astype(f32)
     start = pl.multiple_of(lax.axis_index("delay") * SHARE, SHARE)
-    last = (excite[STEPS - 1, pl.ds(start, SHARE), :] - total).astype(bf16)
+    last = excite[STEPS - 1, pl.ds(start, SHARE), :] - total
+    values = [parts[STEPS - 2 - t, SHARE:].astype(f32) for t in range(STEPS - 1)] + [last]
+    for t, value in enumerate(values):
+        for b in range(SHARE // EXC):
+            at = EXC * (STEPS * b + t)
+            rows[at : at + EXC] = value[EXC * b : EXC * (b + 1)]
+    both = rows[...].astype(bf16)
     for k in range(LANES):
-        for t in range(STEPS - 1):
-            out[k, SHARE * t : SHARE * (t + 1)] = parts[STEPS - 2 - t, SHARE:]
-        out[k, SHARE * (STEPS - 1) :] = last
+        out[k] = both
 
 
 def last_solve(driven, diag, stored, out, sems):
     each = SHARE // EXC
     copies = []
     for i in range(NB):
-        value = jnp.dot(driven[i // each], diag[i], preferred_element_type=f32)
+        mine = slice(EXC * STEPS * (i % each), EXC * STEPS * (i % each + 1))
+        value = jnp.dot(driven[i // each, mine], diag[i], preferred_element_type=f32)
         for t in range(STEPS):
-            at = SHARE * t + EXC * (i % each)
-            out[t, i] = value[at : at + EXC]
+            out[t, i] = value[EXC * t : EXC * (t + 1)]
         if i % GROUP == GROUP - 1:
-            for t in range(STEPS):
-                part = (t, pl.ds(i - GROUP + 1, GROUP))
-                copies.append(pltpu.make_async_copy(out.at[part], stored.at[part], sems.at[len(copies)]))
-                copies[-1].start()
+            part = (slice(None), pl.ds(i - GROUP + 1, GROUP))
+            copies.append(pltpu.make_async_copy(out.at[part], stored.at[part], sems.at[len(copies)]))
+            copies[-1].start()
     for copy in copies:
         copy.wait()
 
@@ -234,9 +240,14 @@
     picked = call(
         pick_initial,
         sds((ROWS, KNOWN * CAP, EXC, B), bf16),
-        [pltpu.VMEM(h0.shape, bf16), pltpu.SemaphoreType.DMA],
+        [
+            pltpu.VMEM(h0.shape, bf16),
+            pltpu.SMEM((ROWS, CAP), jnp.int32),
+            pltpu.SemaphoreType.DMA,
+            pltpu.SemaphoreType.DMA,
+        ],
         (asked, h0, tiles, *later),
-        (0,),
+        (),
         (1, 2),
     )
     arrived = exchange(picked, "rows")
@@ -295,13 +306,15 @@
         fourth_step, sds((LANES, 2 * SHARE, B), bf16), [flat], (slots, tiles, arrived, item2), (0,)
     )
     parts = exchange(parts, "delay")
-    shares = call(share_driven, sds((LANES, STEPS * SHARE, B), bf16), [], (parts, excite), ())
+    shares = call(
+        share_driven, sds((LANES, STEPS * SHARE, B), bf16), [pltpu.VMEM((STEPS * SHARE, B), f32)], (parts, excite), ()
+    )
     driven = exchange(shares, "delay")
     final = (STEPS, NB, EXC, B)
     return call(
         last_solve,
         sds(final, f32),
-        [pltpu.VMEM(final, f32), pltpu.SemaphoreType.DMA((STEPS * NB // GROUP,))],
+        [pltpu.VMEM(final, f32), pltpu.SemaphoreType.DMA((NB // GROUP,))],
         (driven, diag_inverse),
         (),
         out_in_place=True,

time: 147 us -> 147 us (level)
  no operation moved by 1% of the time
where the time goes in v6:
time: 147 us; the launch traced here: 146 us
  blocking collectives  90.1 us (61%)
  starting transfers between devices  18.8 us (13%)
  Pallas kernels  13.6 us (9%)
  waiting for transfers between devices  12.4 us (8%)
  local copies, waits for them, and re-layouts  10.9 us (7%)
    all_to_all x7, blocking collectives, exchange(): lax.all_to_all(array, axis, split_axis=0, concat_axis=0, tiled=True, axis...  90.1 us
    pallas_call x11, Pallas kernels, call(): pl.pallas_call(kernel, out_shape=out_shape, in_specs=specs, out_specs=[VM...  13.6 us
    all_to_all x2, waiting for transfers between devices, exchange(): lax.all_to_all(array, axis, split_axis=0, concat_axis=0, tiled=True, axis...  12.4 us
    unnamed x14, local copies, waits for them, and re-layouts  10.2 us
    all_to_all x2, starting transfers between devices, exchange(): lax.all_to_all(array, axis, split_axis=0, concat_axis=0, tiled=True, axis...  7.05 us
    ppermute x2, starting transfers between devices, shifted(): return lax.ppermute(array, axis, [(i, i + by) for i in range(peers - by)])  6.95 us
    ppermute x1, starting transfers between devices, body(): lax.ppermute(item1, 'delay', [(0, 1), (1, 0)] + [(k, j) for k, j in steps...  3.5 us
  transfers between devices with their start and end apart: 6, of which 2 were waited for; matrix products, arithmetic and copies ran while one was open for 1% of the time, Pallas kernels for 2%

profile of v6, /device:TPU:2, one launch (start us, length us, event | category | flops | bytes accessed | tf_op | source)
XLA Modules:
  0.0 146.0 jit_solution(381835800593183286)
XLA Ops:
  0.0 0.0 copy-start.6
  0.0 4.2 %collective-permute-start.1 = (bf16[64,4,128]{2,1,0:T(4,128)(2,1)}, bf16[64,4,128]{2,1,0:T(4,128)(2,1)S(1)}, u32[]{:S(2)}, u32[]{:S(2)}) collective-permute-start(bf16[64,4,128]{2,1,0:T(4,128)(2,1)} %bitcast.31), channel_id=1, source_target_pairs={{0,2},{1,3},{2,4},{3,5},{4,6},{5,7},{6,8},{7,9},{8,10},{9,11},{10,... | collective-permute-start | bytes 196616 | tf_op jit(solution)/shard_map/ppermute | solution.py:221
  4.2 2.8 %collective-permute-start = (bf16[64,4,128]{2,1,0:T(4,128)(2,1)}, bf16[64,4,128]{2,1,0:T(4,128)(2,1)S(1)}, u32[]{:S(2)}, u32[]{:S(2)}) collective-permute-start(bf16[64,4,128]{2,1,0:T(4,128)(2,1)} %bitcast.32), channel_id=1, source_target_pairs={{0,1},{1,2},{2,3},{3,4},{4,5},{5,6},{6,7},{7,8},{8,9},{9,10},{10,1... | collective-permute-start | bytes 196616 | tf_op jit(solution)/shard_map/ppermute | solution.py:221
  7.0 0.8 copy.11
  7.7 0.0 copy-start
  7.7 16.2 %all_to_all.51 = s32[16,1,8]{2,1,0:T(1,128)S(1)} all-to-all(s32[16,1,8]{2,1,0:T(1,128)S(1)} %copy.11), channel_id=1, replica_groups=mesh['rows'=16,'delay'=16] {'rows'}, dimensions={0} | all-to-all | bytes 1024 | tf_op jit(solution)/shard_map/all_to_all | solution.py:225
  24.0 0.0 collective-permute-done.1.h2
  24.0 0.0 collective-permute-done.h1
  24.0 0.0 copy-start.4
  24.0 0.0 copy-start.5
  24.0 1.1 shard_map.64
  25.1 16.2 %all_to_all.52.arrived = bf16[16,24,4,128]{3,2,1,0:T(4,128)(2,1)S(1)} all-to-all(bf16[16,24,4,128]{3,2,1,0:T(4,128)(2,1)S(1)} %shard_map.64), channel_id=1, replica_groups=mesh['rows'=16,'delay'=16] {'rows'}, dimensions={0} | all-to-all | bytes 786432 | tf_op jit(solution)/shard_map/all_to_all | solution.py:225
  41.3 0.0 copy-done.6
  41.3 0.0 copy-done
  41.3 1.9 %shard_map.65 = bf16[4,256,128]{2,1,0:T(8,128)(2,1)S(1)} custom-call(s32[4,64]{1,0:T(4,128)S(1)} %bitcast.27, bf16[64,4,128,128]{3,2,1,0:T(8,128)(2,1)S(1)} %bitcast.12, bf16[16,24,4,128]{3,2,1,0:T(4,128)(2,1)S(1)} %all_to_all.52.arrived), custom_call_target="tpu_custom_call" | custom-call | tf_op jit(solution)/shard_map/pallas_call | solution.py:36
  43.2 12.0 %all_to_all.53.terms = bf16[4,256,128]{2,1,0:T(8,128)(2,1)S(1)} all-to-all(bf16[4,256,128]{2,1,0:T(8,128)(2,1)S(1)} %shard_map.65), channel_id=1, replica_groups={{0,4,8,12},{1,5,9,13},{2,6,10,14},{3,7,11,15},{16,20,24,28},{17,21,25,2..., dimensions={0} | all-to-all | bytes 524288 | tf_op jit(solution)/shard_map/all_to_all | solution.py:225
  55.3 11.3 %all_to_all.54.terms = bf16[4,256,128]{2,1,0:T(8,128)(2,1)S(1)} all-to-all(bf16[4,256,128]{2,1,0:T(8,128)(2,1)S(1)} %shard_map.66), channel_id=1, replica_groups={{0,1,2,3},{4,5,6,7},{8,9,10,11},{12,13,14,15},{16,17,18,19},{20,21,22,2..., dimensions={0} | all-to-all | bytes 524288 | tf_op jit(solution)/shard_map/all_to_all | solution.py:225
  66.6 0.0 copy-done.4
  66.6 0.0 copy-done.5
  66.6 1.5 %shard_map.67 = (f32[256,128]{1,0:T(8,128)S(1)}, bf16[256,128]{1,0:T(8,128)(2,1)S(1)}, bf16[16,8,4,128]{3,2,1,0:T(4,128)(2,1)}) custom-call(s32[16,8]{1,0:T(8,128)S(1)} %bitcast.24, bf16[4,256,128]{2,1,0:T(8,128)(2,1)S(1)} %all_to_all.54.terms, bf16[64,4,128]{2,1,0:T(4,128)(2,1)S(1)} %collective-permute-done.1.h2, f32[4,256,128]{2,1,0:T(8,128)S(1)} %bitcast.16, ...), custom_call_target="tpu_custom_call" | custom-call | tf_op jit(solution)/shard_map/pallas_call | solution.py:36
  68.1 3.5 %all-to-all-start.4 = ((bf16[16,8,4,128]{3,2,1,0:T(4,128)(2,1)}), bf16[16,8,4,128]{3,2,1,0:T(4,128)(2,1)S(1)}, u32[]{:S(2)}, u32[]{:S(2)}) async-start(bf16[16,8,4,128]{3,2,1,0:T(4,128)(2,1)} %get-tuple-element.12), calls=%async_computation.4 | async-start | bytes 262144 | tf_op jit(solution)/shard_map/all_to_all | solution.py:225
  71.6 1.3 collective-permute-start.2
  72.9 7.3 %all-to-all-done.4 = bf16[16,8,4,128]{3,2,1,0:T(4,128)(2,1)S(1)} async-done(((bf16[16,8,4,128]{3,2,1,0:T(4,128)(2,1)}), bf16[16,8,4,128]{3,2,1,0:T(4,128)(2,1)S(1)}, u32[]{:S(2)}, u32[]{:S(2)}) %all-to-all-start.4) | async-done | bytes 131104 | tf_op jit(solution)/shard_map/all_to_all | solution.py:225
  80.3 0.0 copy-start.1
  80.3 3.4 %copy-done.1 = bf16[1,64,4,128,128]{4,3,2,1,0:T(8,128)(2,1)S(1)} copy-done((bf16[1,64,4,128,128]{4,3,2,1,0:T(8,128)(2,1)S(1)}, bf16[1,64,4,128,128]{4,3,2,1,0:T(8,128)(2,1)}, u32[]{:S(2)}) %copy-start.1) | copy-done | bytes 8388632
  83.6 1.8 %shard_map.68.total = f32[256,128]{1,0:T(8,128)S(1)} custom-call(s32[4,64]{1,0:T(4,128)S(1)} %bitcast.28, bf16[64,4,128,128]{3,2,1,0:T(8,128)(2,1)S(1)} %bitcast.13, bf16[128,4,128]{2,1,0:T(4,128)(2,1)S(1)} %bitcast.21), custom_call_target="tpu_custom_call" | custom-call | tf_op jit(solution)/shard_map/pallas_call | solution.py:36
  85.4 0.0 collective-permute-done.2.came.before
  85.4 1.4 shard_map.69
  86.8 3.5 %all-to-all-start.5 = ((bf16[16,8,4,128]{3,2,1,0:T(4,128)(2,1)}), bf16[16,8,4,128]{3,2,1,0:T(4,128)(2,1)S(1)}, u32[]{:S(2)}, u32[]{:S(2)}) async-start(bf16[16,8,4,128]{3,2,1,0:T(4,128)(2,1)} %get-tuple-element.14), calls=%async_computation.5 | async-start | bytes 262144 | tf_op jit(solution)/shard_map/all_to_all | solution.py:225
  90.3 3.5 %collective-permute-start.3 = (f32[256,128]{1,0:T(8,128)S(1)}, f32[256,128]{1,0:T(8,128)S(1)}, u32[]{:S(2)}, u32[]{:S(2)}) collective-permute-start(f32[256,128]{1,0:T(8,128)S(1)} %get-tuple-element.15), channel_id=1, source_target_pairs={{0,1},{1,0},{4,5},{9,10},{16,17},{17,16},{20,21},{25,26},{32,33},{... | collective-permute-start | bytes 393224 | tf_op jit(solution)/shard_map/ppermute | solution.py:293
  93.9 5.1 %all-to-all-done.5 = bf16[16,8,4,128]{3,2,1,0:T(4,128)(2,1)S(1)} async-done(((bf16[16,8,4,128]{3,2,1,0:T(4,128)(2,1)}), bf16[16,8,4,128]{3,2,1,0:T(4,128)(2,1)S(1)}, u32[]{:S(2)}, u32[]{:S(2)}) %all-to-all-start.5) | async-done | bytes 131104 | tf_op jit(solution)/shard_map/all_to_all | solution.py:225
  99.0 0.0 copy-start.2
  99.0 3.4 %copy-done.2 = bf16[1,64,4,128,128]{4,3,2,1,0:T(8,128)(2,1)S(1)} copy-done((bf16[1,64,4,128,128]{4,3,2,1,0:T(8,128)(2,1)S(1)}, bf16[1,64,4,128,128]{4,3,2,1,0:T(8,128)(2,1)}, u32[]{:S(2)}) %copy-start.2) | copy-done | bytes 8388632
  102.3 1.8 %shard_map.70.total = f32[256,128]{1,0:T(8,128)S(1)} custom-call(s32[4,64]{1,0:T(4,128)S(1)} %bitcast.29, bf16[64,4,128,128]{3,2,1,0:T(8,128)(2,1)S(1)} %bitcast.14, bf16[128,4,128]{2,1,0:T(4,128)(2,1)S(1)} %bitcast.20), custom_call_target="tpu_custom_call" | custom-call | tf_op jit(solution)/shard_map/pallas_call | solution.py:36
  104.1 0.0 collective-permute-done.3.came
  104.1 0.8 shard_map.71
  105.0 11.5 %all_to_all.55 = bf16[16,8,4,128]{3,2,1,0:T(4,128)(2,1)S(1)} all-to-all(bf16[16,8,4,128]{3,2,1,0:T(4,128)(2,1)S(1)} %get-tuple-element.17), channel_id=1, replica_groups=mesh['rows'=16,'delay'=16] {'rows'}, dimensions={0} | all-to-all | bytes 262144 | tf_op jit(solution)/shard_map/all_to_all | solution.py:225
  116.5 0.0 copy-start.3
  116.5 3.4 %copy-done.3 = bf16[1,64,4,128,128]{4,3,2,1,0:T(8,128)(2,1)S(1)} copy-done((bf16[1,64,4,128,128]{4,3,2,1,0:T(8,128)(2,1)S(1)}, bf16[1,64,4,128,128]{4,3,2,1,0:T(8,128)(2,1)}, u32[]{:S(2)}) %copy-start.3) | copy-done | bytes 8388632
  119.9 1.8 %shard_map.72 = bf16[16,32,128]{2,1,0:T(8,128)(2,1)S(1)} custom-call(s32[4,64]{1,0:T(4,128)S(1)} %bitcast.30, bf16[64,4,128,128]{3,2,1,0:T(8,128)(2,1)S(1)} %bitcast.15, bf16[128,4,128]{2,1,0:T(4,128)(2,1)S(1)} %bitcast.22, bf16[256,128]{1,0:T(8,128)(2,1)S(1)} %get-tuple-element.18.item), custom_call_target="tpu_custom_call" | custom-call | tf_op jit(solution)/shard_map/pallas_call | solution.py:36
  121.7 11.1 %all_to_all.56.parts = bf16[16,32,128]{2,1,0:T(8,128)(2,1)S(1)} all-to-all(bf16[16,32,128]{2,1,0:T(8,128)(2,1)S(1)} %shard_map.72), channel_id=1, replica_groups=mesh['rows'=16,'delay'=16] {'delay'}, dimensions={0} | all-to-all | bytes 262144 | tf_op jit(solution)/shard_map/all_to_all | solution.py:225
  132.8 11.8 %all_to_all.57.driven = bf16[16,64,128]{2,1,0:T(8,128)(2,1)S(1)} all-to-all(bf16[16,64,128]{2,1,0:T(8,128)(2,1)S(1)} %shard_map.73), channel_id=1, replica_groups=mesh['rows'=16,'delay'=16] {'delay'}, dimensions={0} | all-to-all | bytes 524288 | tf_op jit(solution)/shard_map/all_to_all | solution.py:225
  144.6 1.4 shard_map.74
  (2 shorter events, 0.1 us)
Async XLA Ops:
  0.0 41.3 %copy-start.6 = (s32[1,64,4]{1,2,0:T(4,128)S(1)}, s32[1,64,4]{1,2,0:T(4,128)}, u32[]{:S(2)}) copy-start(s32[1,64,4]{1,2,0:T(4,128)} %param.8) | copy-start | bytes 3076
  0.0 24.0 %collective-permute-start.1 = (bf16[64,4,128]{2,1,0:T(4,128)(2,1)}, bf16[64,4,128]{2,1,0:T(4,128)(2,1)S(1)}, u32[]{:S(2)}, u32[]{:S(2)}) collective-permute-start(bf16[64,4,128]{2,1,0:T(4,128)(2,1)} %bitcast.31), channel_id=1, source_target_pairs={{0,2},{1,3},{2,4},{3,5},{4,6},{5,7},{6,8},{7,9},{8,10},{9,11},{10,... | collective-permute-start | bytes 196616 | tf_op jit(solution)/shard_map/ppermute | solution.py:221
  4.2 19.8 %collective-permute-start = (bf16[64,4,128]{2,1,0:T(4,128)(2,1)}, bf16[64,4,128]{2,1,0:T(4,128)(2,1)S(1)}, u32[]{:S(2)}, u32[]{:S(2)}) collective-permute-start(bf16[64,4,128]{2,1,0:T(4,128)(2,1)} %bitcast.32), channel_id=1, source_target_pairs={{0,1},{1,2},{2,3},{3,4},{4,5},{5,6},{6,7},{7,8},{8,9},{9,10},{10,1... | collective-permute-start | bytes 196616 | tf_op jit(solution)/shard_map/ppermute | solution.py:221
  7.7 33.5 %copy-start = (bf16[1,64,4,128,128]{4,3,2,1,0:T(8,128)(2,1)S(1)}, bf16[1,64,4,128,128]{4,3,2,1,0:T(8,128)(2,1)}, u32[]{:S(2)}) copy-start(bf16[1,64,4,128,128]{4,3,2,1,0:T(8,128)(2,1)} %param.6) | copy-start | bytes 25165828
  24.0 42.6 %copy-start.4 = (bf16[64,128,128]{2,1,0:T(8,128)(2,1)S(1)}, bf16[64,128,128]{2,1,0:T(8,128)(2,1)}, u32[]{:S(2)}) copy-start(bf16[64,128,128]{2,1,0:T(8,128)(2,1)} %diag.7) | copy-start | bytes 6291460
  24.0 42.6 %copy-start.5 = (f32[4,64,4,128]{3,2,1,0:T(4,128)S(1)}, f32[4,64,4,128]{3,2,1,0:T(4,128)}, u32[]{:S(2)}) copy-start(f32[4,64,4,128]{3,2,1,0:T(4,128)} %param.10) | copy-start | bytes 1572868
  68.1 12.2 %all-to-all-start.4 = ((bf16[16,8,4,128]{3,2,1,0:T(4,128)(2,1)}), bf16[16,8,4,128]{3,2,1,0:T(4,128)(2,1)S(1)}, u32[]{:S(2)}, u32[]{:S(2)}) async-start(bf16[16,8,4,128]{3,2,1,0:T(4,128)(2,1)} %get-tuple-element.12), calls=%async_computation.4 | async-start | bytes 262144 | tf_op jit(solution)/shard_map/all_to_all | solution.py:225
  71.6 13.8 %collective-permute-start.2 = (f32[256,128]{1,0:T(8,128)S(1)}, f32[256,128]{1,0:T(8,128)S(1)}, u32[]{:S(2)}, u32[]{:S(2)}) collective-permute-start(f32[256,128]{1,0:T(8,128)S(1)} %get-tuple-element.13), channel_id=1, source_target_pairs={{4,0},{9,1},{2,3},{3,4},{5,6},{6,7},{7,8},{8,9},{10,11},{11,12},{1... | collective-permute-start | bytes 393224 | tf_op jit(solution)/shard_map/ppermute | solution.py:282
  80.3 3.4 %copy-start.1 = (bf16[1,64,4,128,128]{4,3,2,1,0:T(8,128)(2,1)S(1)}, bf16[1,64,4,128,128]{4,3,2,1,0:T(8,128)(2,1)}, u32[]{:S(2)}) copy-start(bf16[1,64,4,128,128]{4,3,2,1,0:T(8,128)(2,1)} %param.6) | copy-start | bytes 25165828
  86.8 12.2 %all-to-all-start.5 = ((bf16[16,8,4,128]{3,2,1,0:T(4,128)(2,1)}), bf16[16,8,4,128]{3,2,1,0:T(4,128)(2,1)S(1)}, u32[]{:S(2)}, u32[]{:S(2)}) async-start(bf16[16,8,4,128]{3,2,1,0:T(4,128)(2,1)} %get-tuple-element.14), calls=%async_computation.5 | async-start | bytes 262144 | tf_op jit(solution)/shard_map/all_to_all | solution.py:225
  90.3 13.8 %collective-permute-start.3 = (f32[256,128]{1,0:T(8,128)S(1)}, f32[256,128]{1,0:T(8,128)S(1)}, u32[]{:S(2)}, u32[]{:S(2)}) collective-permute-start(f32[256,128]{1,0:T(8,128)S(1)} %get-tuple-element.15), channel_id=1, source_target_pairs={{0,1},{1,0},{4,5},{9,10},{16,17},{17,16},{20,21},{25,26},{32,33},{... | collective-permute-start | bytes 393224 | tf_op jit(solution)/shard_map/ppermute | solution.py:293
  99.0 3.4 %copy-start.2 = (bf16[1,64,4,128,128]{4,3,2,1,0:T(8,128)(2,1)S(1)}, bf16[1,64,4,128,128]{4,3,2,1,0:T(8,128)(2,1)}, u32[]{:S(2)}) copy-start(bf16[1,64,4,128,128]{4,3,2,1,0:T(8,128)(2,1)} %param.6) | copy-start | bytes 25165828
  116.5 3.4 %copy-start.3 = (bf16[1,64,4,128,128]{4,3,2,1,0:T(8,128)(2,1)S(1)}, bf16[1,64,4,128,128]{4,3,2,1,0:T(8,128)(2,1)}, u32[]{:S(2)}) copy-start(bf16[1,64,4,128,128]{4,3,2,1,0:T(8,128)(2,1)} %param.6) | copy-start | bytes 25165828

commit v7 on v6

--- a/solution.py
+++ b/solution.py
@@ -1,3 +1,5 @@
+import functools
+
 import jax
 import jax.numpy as jnp
 from jax import lax
@@ -118,8 +120,15 @@
         older(h2, moved)
 
     item[...] = driven[...].astype(bf16)
-    solve(driven, diag, solved)
-    pick(fetch, asked, solved, send)
+
+    @pl.when(me < 2)
+    def _():
+        solve(driven, diag, solved)
+        pick(fetch, asked, solved, send)
+
+    @pl.when(me >= 2)
+    def _():
+        fetch.wait()
 
 
 def tile_terms(slots, tiles, arrived, total):
@@ -127,6 +136,12 @@
         row = jnp.concatenate([arrived[slots[s, i]] for s in range(L)], axis=1)
         tile = tiles[i].reshape(L * B, B)
         total[EXC * i : EXC * (i + 1), :] = jnp.dot(row, tile, preferred_element_type=f32)
+
+
+def tile_terms_below(lanes, slots, tiles, arrived, total):
+    @pl.when(lax.axis_index("delay") < lanes)
+    def _():
+        tile_terms(slots, tiles, arrived, total)
 
 
 def second_step(listed, total, came, h2, excite, diag, item, send, driven, solved, asked, sem):
@@ -281,18 +296,14 @@
     pairs = [(k, j) for k, j in steps if k not in GIVERS]
     before = lax.ppermute(moved, "delay", [(GIVERS[0], 0), (GIVERS[1], 1)] + pairs)
     arrived = exchange(send, "rows").reshape(TAKEN, EXC, B)
-    total = call(tile_terms, sds((FLAT, B), f32), [], (slots, tiles, arrived), (0,))
+    total = call(functools.partial(tile_terms_below, 2), sds((FLAT, B), f32), [], (slots, tiles, arrived), (0,))
 
     item1, send = call(
-        second_step,
-        (sds((FLAT, B), f32), send_shape),
-        work,
-        (asked, total, before, later[1], excite, diag_inverse),
-        (),
+        second_step, (sds((FLAT, B), f32), send_shape), work, (asked, total, before, later[1], excite, diag_inverse), ()
     )
     came = lax.ppermute(item1, "delay", [(0, 1), (1, 0)] + [(k, j) for k, j in steps if k in GIVERS])
     arrived = exchange(send, "rows").reshape(TAKEN, EXC, B)
-    total = call(tile_terms, sds((FLAT, B), f32), [], (slots, tiles, arrived), (0,))
+    total = call(functools.partial(tile_terms_below, 1), sds((FLAT, B), f32), [], (slots, tiles, arrived), (0,))
 
     item2, send = call(
         third_step,
@@ -302,9 +313,7 @@
         (),
     )
     arrived = exchange(send, "rows").reshape(TAKEN, EXC, B)
-    parts = call(
-        fourth_step, sds((LANES, 2 * SHARE, B), bf16), [flat], (slots, tiles, arrived, item2), (0,)
-    )
+    parts = call(fourth_step, sds((LANES, 2 * SHARE, B), bf16), [flat], (slots, tiles, arrived, item2), (0,))
     parts = exchange(parts, "delay")
     shares = call(
         share_driven, sds((LANES, STEPS * SHARE, B), bf16), [pltpu.VMEM((STEPS * SHARE, B), f32)], (parts, excite), ()

time: 147 us -> 147 us (level)
  no operation moved by 1% of the time
where the time goes in v7:
time: 147 us; the launch traced here: 146 us
  blocking collectives  91.3 us (62%)
  starting transfers between devices  18.8 us (13%)
  waiting for transfers between devices  12.4 us (8%)
  Pallas kernels  12.4 us (8%)
  local copies, waits for them, and re-layouts  10.9 us (7%)
    all_to_all x7, blocking collectives, exchange(): lax.all_to_all(array, axis, split_axis=0, concat_axis=0, tiled=True, axis...  91.3 us
    all_to_all x2, waiting for transfers between devices, exchange(): lax.all_to_all(array, axis, split_axis=0, concat_axis=0, tiled=True, axis...  12.4 us
    pallas_call x11, Pallas kernels, call(): pl.pallas_call(kernel, out_shape=out_shape, in_specs=specs, out_specs=[VM...  12.4 us
    unnamed x14, local copies, waits for them, and re-layouts  10.2 us
    all_to_all x2, starting transfers between devices, exchange(): lax.all_to_all(array, axis, split_axis=0, concat_axis=0, tiled=True, axis...  7.05 us
    ppermute x2, starting transfers between devices, shifted(): return lax.ppermute(array, axis, [(i, i + by) for i in range(peers - by)])  6.95 us
    ppermute x1, starting transfers between devices, body(): lax.ppermute(item1, 'delay', [(0, 1), (1, 0)] + [(k, j) for k, j in steps...  3.5 us
  transfers between devices with their start and end apart: 6, of which 2 were waited for; matrix products, arithmetic and copies ran while one was open for 1% of the time, Pallas kernels for 2%

profile of v7, /device:TPU:2, one launch (start us, length us, event | category | flops | bytes accessed | tf_op | source)
XLA Modules:
  0.0 146.0 jit_solution(18050317302250980082)
XLA Ops:
  0.0 0.0 copy-start.6
  0.0 4.2 %collective-permute-start.1 = (bf16[64,4,128]{2,1,0:T(4,128)(2,1)}, bf16[64,4,128]{2,1,0:T(4,128)(2,1)S(1)}, u32[]{:S(2)}, u32[]{:S(2)}) collective-permute-start(bf16[64,4,128]{2,1,0:T(4,128)(2,1)} %bitcast.31), channel_id=1, source_target_pairs={{0,2},{1,3},{2,4},{3,5},{4,6},{5,7},{6,8},{7,9},{8,10},{9,11},{10,... | collective-permute-start | bytes 196616 | tf_op jit(solution)/shard_map/ppermute | solution.py:236
  4.2 2.8 %collective-permute-start = (bf16[64,4,128]{2,1,0:T(4,128)(2,1)}, bf16[64,4,128]{2,1,0:T(4,128)(2,1)S(1)}, u32[]{:S(2)}, u32[]{:S(2)}) collective-permute-start(bf16[64,4,128]{2,1,0:T(4,128)(2,1)} %bitcast.32), channel_id=1, source_target_pairs={{0,1},{1,2},{2,3},{3,4},{4,5},{5,6},{6,7},{7,8},{8,9},{9,10},{10,1... | collective-permute-start | bytes 196616 | tf_op jit(solution)/shard_map/ppermute | solution.py:236
  7.0 0.8 copy.11
  7.7 0.0 copy-start
  7.7 16.2 %all_to_all.51 = s32[16,1,8]{2,1,0:T(1,128)S(1)} all-to-all(s32[16,1,8]{2,1,0:T(1,128)S(1)} %copy.11), channel_id=1, replica_groups=mesh['rows'=16,'delay'=16] {'rows'}, dimensions={0} | all-to-all | bytes 1024 | tf_op jit(solution)/shard_map/all_to_all | solution.py:240
  24.0 0.0 collective-permute-done.1.h2
  24.0 0.0 collective-permute-done.h1
  24.0 0.0 copy-start.4
  24.0 0.0 copy-start.5
  24.0 1.1 shard_map.64
  25.1 16.2 %all_to_all.52.arrived = bf16[16,24,4,128]{3,2,1,0:T(4,128)(2,1)S(1)} all-to-all(bf16[16,24,4,128]{3,2,1,0:T(4,128)(2,1)S(1)} %shard_map.64), channel_id=1, replica_groups=mesh['rows'=16,'delay'=16] {'rows'}, dimensions={0} | all-to-all | bytes 786432 | tf_op jit(solution)/shard_map/all_to_all | solution.py:240
  41.3 0.0 copy-done.6
  41.3 0.0 copy-done
  41.3 1.9 %shard_map.65 = bf16[4,256,128]{2,1,0:T(8,128)(2,1)S(1)} custom-call(s32[4,64]{1,0:T(4,128)S(1)} %bitcast.27, bf16[64,4,128,128]{3,2,1,0:T(8,128)(2,1)S(1)} %bitcast.12, bf16[16,24,4,128]{3,2,1,0:T(4,128)(2,1)S(1)} %all_to_all.52.arrived), custom_call_target="tpu_custom_call" | custom-call | tf_op jit(solution)/shard_map/pallas_call | solution.py:38
  43.2 12.0 %all_to_all.53.terms = bf16[4,256,128]{2,1,0:T(8,128)(2,1)S(1)} all-to-all(bf16[4,256,128]{2,1,0:T(8,128)(2,1)S(1)} %shard_map.65), channel_id=1, replica_groups={{0,4,8,12},{1,5,9,13},{2,6,10,14},{3,7,11,15},{16,20,24,28},{17,21,25,2..., dimensions={0} | all-to-all | bytes 524288 | tf_op jit(solution)/shard_map/all_to_all | solution.py:240
  55.3 11.3 %all_to_all.54.terms = bf16[4,256,128]{2,1,0:T(8,128)(2,1)S(1)} all-to-all(bf16[4,256,128]{2,1,0:T(8,128)(2,1)S(1)} %shard_map.66), channel_id=1, replica_groups={{0,1,2,3},{4,5,6,7},{8,9,10,11},{12,13,14,15},{16,17,18,19},{20,21,22,2..., dimensions={0} | all-to-all | bytes 524288 | tf_op jit(solution)/shard_map/all_to_all | solution.py:240
  66.6 0.0 copy-done.4
  66.6 0.0 copy-done.5
  66.6 1.5 %shard_map.67 = (f32[256,128]{1,0:T(8,128)S(1)}, bf16[256,128]{1,0:T(8,128)(2,1)S(1)}, bf16[16,8,4,128]{3,2,1,0:T(4,128)(2,1)}) custom-call(s32[16,8]{1,0:T(8,128)S(1)} %bitcast.24, bf16[4,256,128]{2,1,0:T(8,128)(2,1)S(1)} %all_to_all.54.terms, bf16[64,4,128]{2,1,0:T(4,128)(2,1)S(1)} %collective-permute-done.1.h2, f32[4,256,128]{2,1,0:T(8,128)S(1)} %bitcast.16, ...), custom_call_target="tpu_custom_call" | custom-call | tf_op jit(solution)/shard_map/pallas_call | solution.py:38
  68.1 3.5 %all-to-all-start.4 = ((bf16[16,8,4,128]{3,2,1,0:T(4,128)(2,1)}), bf16[16,8,4,128]{3,2,1,0:T(4,128)(2,1)S(1)}, u32[]{:S(2)}, u32[]{:S(2)}) async-start(bf16[16,8,4,128]{3,2,1,0:T(4,128)(2,1)} %get-tuple-element.12), calls=%async_computation.4 | async-start | bytes 262144 | tf_op jit(solution)/shard_map/all_to_all | solution.py:240
  71.7 1.3 collective-permute-start.2
  73.0 7.3 %all-to-all-done.4 = bf16[16,8,4,128]{3,2,1,0:T(4,128)(2,1)S(1)} async-done(((bf16[16,8,4,128]{3,2,1,0:T(4,128)(2,1)}), bf16[16,8,4,128]{3,2,1,0:T(4,128)(2,1)S(1)}, u32[]{:S(2)}, u32[]{:S(2)}) %all-to-all-start.4) | async-done | bytes 131104 | tf_op jit(solution)/shard_map/all_to_all | solution.py:240
  80.3 0.0 copy-start.1
  80.3 3.4 %copy-done.1 = bf16[1,64,4,128,128]{4,3,2,1,0:T(8,128)(2,1)S(1)} copy-done((bf16[1,64,4,128,128]{4,3,2,1,0:T(8,128)(2,1)S(1)}, bf16[1,64,4,128,128]{4,3,2,1,0:T(8,128)(2,1)}, u32[]{:S(2)}) %copy-start.1) | copy-done | bytes 8388632
  83.7 1.8 %shard_map.68.total = f32[256,128]{1,0:T(8,128)S(1)} custom-call(s32[4,64]{1,0:T(4,128)S(1)} %bitcast.28, bf16[64,4,128,128]{3,2,1,0:T(8,128)(2,1)S(1)} %bitcast.13, bf16[128,4,128]{2,1,0:T(4,128)(2,1)S(1)} %bitcast.21), custom_call_target="tpu_custom_call" | custom-call | tf_op jit(solution)/shard_map/pallas_call | solution.py:38
  85.5 0.0 collective-permute-done.2.came.before
  85.5 1.4 shard_map.69
  86.8 3.5 %all-to-all-start.5 = ((bf16[16,8,4,128]{3,2,1,0:T(4,128)(2,1)}), bf16[16,8,4,128]{3,2,1,0:T(4,128)(2,1)S(1)}, u32[]{:S(2)}, u32[]{:S(2)}) async-start(bf16[16,8,4,128]{3,2,1,0:T(4,128)(2,1)} %get-tuple-element.14), calls=%async_computation.5 | async-start | bytes 262144 | tf_op jit(solution)/shard_map/all_to_all | solution.py:240
  90.4 3.5 %collective-permute-start.3 = (f32[256,128]{1,0:T(8,128)S(1)}, f32[256,128]{1,0:T(8,128)S(1)}, u32[]{:S(2)}, u32[]{:S(2)}) collective-permute-start(f32[256,128]{1,0:T(8,128)S(1)} %get-tuple-element.15), channel_id=1, source_target_pairs={{0,1},{1,0},{4,5},{9,10},{16,17},{17,16},{20,21},{25,26},{32,33},{... | collective-permute-start | bytes 393224 | tf_op jit(solution)/shard_map/ppermute | solution.py:304
  93.9 5.1 %all-to-all-done.5 = bf16[16,8,4,128]{3,2,1,0:T(4,128)(2,1)S(1)} async-done(((bf16[16,8,4,128]{3,2,1,0:T(4,128)(2,1)}), bf16[16,8,4,128]{3,2,1,0:T(4,128)(2,1)S(1)}, u32[]{:S(2)}, u32[]{:S(2)}) %all-to-all-start.5) | async-done | bytes 131104 | tf_op jit(solution)/shard_map/all_to_all | solution.py:240
  99.0 0.0 copy-start.2
  99.0 3.4 %copy-done.2 = bf16[1,64,4,128,128]{4,3,2,1,0:T(8,128)(2,1)S(1)} copy-done((bf16[1,64,4,128,128]{4,3,2,1,0:T(8,128)(2,1)S(1)}, bf16[1,64,4,128,128]{4,3,2,1,0:T(8,128)(2,1)}, u32[]{:S(2)}) %copy-start.2) | copy-done | bytes 8388632
  102.4 0.6 shard_map.70.total
  102.9 0.0 collective-permute-done.3.came
  103.0 0.8 shard_map.71
  103.8 11.5 %all_to_all.55 = bf16[16,8,4,128]{3,2,1,0:T(4,128)(2,1)S(1)} all-to-all(bf16[16,8,4,128]{3,2,1,0:T(4,128)(2,1)S(1)} %get-tuple-element.17), channel_id=1, replica_groups=mesh['rows'=16,'delay'=16] {'rows'}, dimensions={0} | all-to-all | bytes 262144 | tf_op jit(solution)/shard_map/all_to_all | solution.py:240
  115.3 0.0 copy-start.3
  115.3 3.4 %copy-done.3 = bf16[1,64,4,128,128]{4,3,2,1,0:T(8,128)(2,1)S(1)} copy-done((bf16[1,64,4,128,128]{4,3,2,1,0:T(8,128)(2,1)S(1)}, bf16[1,64,4,128,128]{4,3,2,1,0:T(8,128)(2,1)}, u32[]{:S(2)}) %copy-start.3) | copy-done | bytes 8388632
  118.7 1.8 %shard_map.72 = bf16[16,32,128]{2,1,0:T(8,128)(2,1)S(1)} custom-call(s32[4,64]{1,0:T(4,128)S(1)} %bitcast.30, bf16[64,4,128,128]{3,2,1,0:T(8,128)(2,1)S(1)} %bitcast.15, bf16[128,4,128]{2,1,0:T(4,128)(2,1)S(1)} %bitcast.22, bf16[256,128]{1,0:T(8,128)(2,1)S(1)} %get-tuple-element.18.item), custom_call_target="tpu_custom_call" | custom-call | tf_op jit(solution)/shard_map/pallas_call | solution.py:38
  120.5 12.3 %all_to_all.56.parts = bf16[16,32,128]{2,1,0:T(8,128)(2,1)S(1)} all-to-all(bf16[16,32,128]{2,1,0:T(8,128)(2,1)S(1)} %shard_map.72), channel_id=1, replica_groups=mesh['rows'=16,'delay'=16] {'delay'}, dimensions={0} | all-to-all | bytes 262144 | tf_op jit(solution)/shard_map/all_to_all | solution.py:240
  132.9 11.8 %all_to_all.57.driven = bf16[16,64,128]{2,1,0:T(8,128)(2,1)S(1)} all-to-all(bf16[16,64,128]{2,1,0:T(8,128)(2,1)S(1)} %shard_map.73), channel_id=1, replica_groups=mesh['rows'=16,'delay'=16] {'delay'}, dimensions={0} | all-to-all | bytes 524288 | tf_op jit(solution)/shard_map/all_to_all | solution.py:240
  144.6 1.4 shard_map.74
  (2 shorter events, 0.1 us)
Async XLA Ops:
  0.0 41.3 %copy-start.6 = (s32[1,64,4]{1,2,0:T(4,128)S(1)}, s32[1,64,4]{1,2,0:T(4,128)}, u32[]{:S(2)}) copy-start(s32[1,64,4]{1,2,0:T(4,128)} %param.8) | copy-start | bytes 3076
  0.0 24.0 %collective-permute-start.1 = (bf16[64,4,128]{2,1,0:T(4,128)(2,1)}, bf16[64,4,128]{2,1,0:T(4,128)(2,1)S(1)}, u32[]{:S(2)}, u32[]{:S(2)}) collective-permute-start(bf16[64,4,128]{2,1,0:T(4,128)(2,1)} %bitcast.31), channel_id=1, source_target_pairs={{0,2},{1,3},{2,4},{3,5},{4,6},{5,7},{6,8},{7,9},{8,10},{9,11},{10,... | collective-permute-start | bytes 196616 | tf_op jit(solution)/shard_map/ppermute | solution.py:236
  4.2 19.8 %collective-permute-start = (bf16[64,4,128]{2,1,0:T(4,128)(2,1)}, bf16[64,4,128]{2,1,0:T(4,128)(2,1)S(1)}, u32[]{:S(2)}, u32[]{:S(2)}) collective-permute-start(bf16[64,4,128]{2,1,0:T(4,128)(2,1)} %bitcast.32), channel_id=1, source_target_pairs={{0,1},{1,2},{2,3},{3,4},{4,5},{5,6},{6,7},{7,8},{8,9},{9,10},{10,1... | collective-permute-start | bytes 196616 | tf_op jit(solution)/shard_map/ppermute | solution.py:236
  7.7 33.5 %copy-start = (bf16[1,64,4,128,128]{4,3,2,1,0:T(8,128)(2,1)S(1)}, bf16[1,64,4,128,128]{4,3,2,1,0:T(8,128)(2,1)}, u32[]{:S(2)}) copy-start(bf16[1,64,4,128,128]{4,3,2,1,0:T(8,128)(2,1)} %param.6) | copy-start | bytes 25165828
  24.0 42.6 %copy-start.4 = (bf16[64,128,128]{2,1,0:T(8,128)(2,1)S(1)}, bf16[64,128,128]{2,1,0:T(8,128)(2,1)}, u32[]{:S(2)}) copy-start(bf16[64,128,128]{2,1,0:T(8,128)(2,1)} %diag.7) | copy-start | bytes 6291460
  24.0 42.6 %copy-start.5 = (f32[4,64,4,128]{3,2,1,0:T(4,128)S(1)}, f32[4,64,4,128]{3,2,1,0:T(4,128)}, u32[]{:S(2)}) copy-start(f32[4,64,4,128]{3,2,1,0:T(4,128)} %param.10) | copy-start | bytes 1572868
  68.1 12.2 %all-to-all-start.4 = ((bf16[16,8,4,128]{3,2,1,0:T(4,128)(2,1)}), bf16[16,8,4,128]{3,2,1,0:T(4,128)(2,1)S(1)}, u32[]{:S(2)}, u32[]{:S(2)}) async-start(bf16[16,8,4,128]{3,2,1,0:T(4,128)(2,1)} %get-tuple-element.12), calls=%async_computation.4 | async-start | bytes 262144 | tf_op jit(solution)/shard_map/all_to_all | solution.py:240
  71.7 13.8 %collective-permute-start.2 = (f32[256,128]{1,0:T(8,128)S(1)}, f32[256,128]{1,0:T(8,128)S(1)}, u32[]{:S(2)}, u32[]{:S(2)}) collective-permute-start(f32[256,128]{1,0:T(8,128)S(1)} %get-tuple-element.13), channel_id=1, source_target_pairs={{4,0},{9,1},{2,3},{3,4},{5,6},{6,7},{7,8},{8,9},{10,11},{11,12},{1... | collective-permute-start | bytes 393224 | tf_op jit(solution)/shard_map/ppermute | solution.py:297
  80.3 3.4 %copy-start.1 = (bf16[1,64,4,128,128]{4,3,2,1,0:T(8,128)(2,1)S(1)}, bf16[1,64,4,128,128]{4,3,2,1,0:T(8,128)(2,1)}, u32[]{:S(2)}) copy-start(bf16[1,64,4,128,128]{4,3,2,1,0:T(8,128)(2,1)} %param.6) | copy-start | bytes 25165828
  86.8 12.2 %all-to-all-start.5 = ((bf16[16,8,4,128]{3,2,1,0:T(4,128)(2,1)}), bf16[16,8,4,128]{3,2,1,0:T(4,128)(2,1)S(1)}, u32[]{:S(2)}, u32[]{:S(2)}) async-start(bf16[16,8,4,128]{3,2,1,0:T(4,128)(2,1)} %get-tuple-element.14), calls=%async_computation.5 | async-start | bytes 262144 | tf_op jit(solution)/shard_map/all_to_all | solution.py:240
  90.4 12.6 %collective-permute-start.3 = (f32[256,128]{1,0:T(8,128)S(1)}, f32[256,128]{1,0:T(8,128)S(1)}, u32[]{:S(2)}, u32[]{:S(2)}) collective-permute-start(f32[256,128]{1,0:T(8,128)S(1)} %get-tuple-element.15), channel_id=1, source_target_pairs={{0,1},{1,0},{4,5},{9,10},{16,17},{17,16},{20,21},{25,26},{32,33},{... | collective-permute-start | bytes 393224 | tf_op jit(solution)/shard_map/ppermute | solution.py:304
  99.0 3.4 %copy-start.2 = (bf16[1,64,4,128,128]{4,3,2,1,0:T(8,128)(2,1)S(1)}, bf16[1,64,4,128,128]{4,3,2,1,0:T(8,128)(2,1)}, u32[]{:S(2)}) copy-start(bf16[1,64,4,128,128]{4,3,2,1,0:T(8,128)(2,1)} %param.6) | copy-start | bytes 25165828
  115.3 3.4 %copy-start.3 = (bf16[1,64,4,128,128]{4,3,2,1,0:T(8,128)(2,1)S(1)}, bf16[1,64,4,128,128]{4,3,2,1,0:T(8,128)(2,1)}, u32[]{:S(2)}) copy-start(bf16[1,64,4,128,128]{4,3,2,1,0:T(8,128)(2,1)} %param.6) | copy-start | bytes 25165828

commit v8 on v7

--- a/solution.py
+++ b/solution.py
@@ -62,12 +62,15 @@
             out[r, p] = h0[asked[r, p]]
 
 
-def initial_terms(slots, tiles, arrived, out, wide, packed, total):
+def initial_terms(listed, tiles, arrived, out, wide, packed, total, slots, sem):
+    fetch = pltpu.make_async_copy(listed, slots, sem)
+    fetch.start()
     for o in range(ROWS):
         for t in range(KNOWN):
             here = arrived[o, CAP * t : CAP * (t + 1)]
             wide[CAP * o : CAP * (o + 1), EXC * t : EXC * (t + 1), :] = here.astype(f32)
     packed[...] = wide[...].astype(bf16)
+    fetch.wait()
     for i in range(NB):
         row = jnp.concatenate([packed[slots[s, i]] for s in range(L)], axis=1)
         tile = tiles[i].reshape(L * B, B)
@@ -105,8 +108,12 @@
 
 def first_step(listed, terms, h2, excite, diag, moved, item, send, driven, solved, asked, sem):
     fetch = pltpu.make_async_copy(listed, asked, sem)
-    fetch.start()
     me = lax.axis_index("delay")
+
+    @pl.when(me < 2)
+    def _():
+        fetch.start()
+
     whole = sum(terms[x].astype(f32) for x in range(4))
     driven[...] = excite[0] - whole
     gives = (me == GIVERS[0]) | (me == GIVERS[1])
@@ -115,7 +122,7 @@
     def _():
         moved[...] = whole
 
-    @pl.when(jnp.logical_not(gives))
+    @pl.when(jnp.logical_not(gives) & (me > 1))
     def _():
         older(h2, moved)
 
@@ -125,10 +132,6 @@
     def _():
         solve(driven, diag, solved)
         pick(fetch, asked, solved, send)
-
-    @pl.when(me >= 2)
-    def _():
-        fetch.wait()
 
 
 def tile_terms(slots, tiles, arrived, total):
@@ -146,8 +149,12 @@
 
 def second_step(listed, total, came, h2, excite, diag, item, send, driven, solved, asked, sem):
     fetch = pltpu.make_async_copy(listed, asked, sem)
-    fetch.start()
     me = lax.axis_index("delay")
+
+    @pl.when(me == 0)
+    def _():
+        fetch.start()
+
     value = total[...] + came[...]
     driven[...] = excite[1] - value
 
@@ -156,10 +163,6 @@
         item[...] = driven[...].astype(bf16).astype(f32)
         solve(driven, diag, solved)
         pick(fetch, asked, solved, send)
-
-    @pl.when(me != 0)
-    def _():
-        fetch.wait()
 
     @pl.when(me == 1)
     def _():
@@ -270,9 +273,15 @@
     terms = call(
         initial_terms,
         sds((4, FLAT, B), bf16),
-        [pltpu.VMEM(wide, f32), pltpu.VMEM(wide, bf16), pltpu.VMEM((KNOWN, FLAT, B), f32)],
+        [
+            pltpu.VMEM(wide, f32),
+            pltpu.VMEM(wide, bf16),
+            pltpu.VMEM((KNOWN, FLAT, B), f32),
+            pltpu.SMEM(slots.shape, jnp.int32),
+            pltpu.SemaphoreType.DMA,
+        ],
         (slots, tiles, arrived),
-        (0,),
+        (),
     )
     along_x = [[4 * y + x for x in range(4)] for y in range(4)]
     along_y = [[4 * y + x for y in range(4)] for x in range(4)]

time: 147 us -> 147 us (level)
  no operation moved by 1% of the time
where the time goes in v8:
time: 147 us; the launch traced here: 146 us
  blocking collectives  92 us (63%)
  starting transfers between devices  19.4 us (13%)
  waiting for transfers between devices  11.8 us (8%)
  Pallas kernels  11.6 us (8%)
  local copies, waits for them, and re-layouts  10.9 us (7%)
    all_to_all x7, blocking collectives, exchange(): lax.all_to_all(array, axis, split_axis=0, concat_axis=0, tiled=True, axis...  92 us
    all_to_all x2, waiting for transfers between devices, exchange(): lax.all_to_all(array, axis, split_axis=0, concat_axis=0, tiled=True, axis...  11.8 us
    pallas_call x11, Pallas kernels, call(): pl.pallas_call(kernel, out_shape=out_shape, in_specs=specs, out_specs=[VM...  11.6 us
    unnamed x14, local copies, waits for them, and re-layouts  10.2 us
    all_to_all x2, starting transfers between devices, exchange(): lax.all_to_all(array, axis, split_axis=0, concat_axis=0, tiled=True, axis...  7.05 us
    ppermute x2, starting transfers between devices, shifted(): return lax.ppermute(array, axis, [(i, i + by) for i in range(peers - by)])  6.95 us
    ppermute x1, starting transfers between devices, body(): lax.ppermute(item1, 'delay', [(0, 1), (1, 0)] + [(k, j) for k, j in steps...  4.15 us
  transfers between devices with their start and end apart: 6, of which 2 were waited for; matrix products, arithmetic and copies ran while one was open for 1% of the time, Pallas kernels for 2%

profile of v8, /device:TPU:2, one launch (start us, length us, event | category | flops | bytes accessed | tf_op | source)
XLA Modules:
  0.0 145.9 jit_solution(15092184701131795760)
XLA Ops:
  0.0 0.0 copy-start.6
  0.0 4.2 %collective-permute-start.1 = (bf16[64,4,128]{2,1,0:T(4,128)(2,1)}, bf16[64,4,128]{2,1,0:T(4,128)(2,1)S(1)}, u32[]{:S(2)}, u32[]{:S(2)}) collective-permute-start(bf16[64,4,128]{2,1,0:T(4,128)(2,1)} %bitcast.31), channel_id=1, source_target_pairs={{0,2},{1,3},{2,4},{3,5},{4,6},{5,7},{6,8},{7,9},{8,10},{9,11},{10,... | collective-permute-start | bytes 196616 | tf_op jit(solution)/shard_map/ppermute | solution.py:239
  4.2 2.8 %collective-permute-start = (bf16[64,4,128]{2,1,0:T(4,128)(2,1)}, bf16[64,4,128]{2,1,0:T(4,128)(2,1)S(1)}, u32[]{:S(2)}, u32[]{:S(2)}) collective-permute-start(bf16[64,4,128]{2,1,0:T(4,128)(2,1)} %bitcast.32), channel_id=1, source_target_pairs={{0,1},{1,2},{2,3},{3,4},{4,5},{5,6},{6,7},{7,8},{8,9},{9,10},{10,1... | collective-permute-start | bytes 196616 | tf_op jit(solution)/shard_map/ppermute | solution.py:239
  7.0 0.8 copy.11
  7.7 0.0 copy-start
  7.7 16.2 %all_to_all.51 = s32[16,1,8]{2,1,0:T(1,128)S(1)} all-to-all(s32[16,1,8]{2,1,0:T(1,128)S(1)} %copy.11), channel_id=1, replica_groups=mesh['rows'=16,'delay'=16] {'rows'}, dimensions={0} | all-to-all | bytes 1024 | tf_op jit(solution)/shard_map/all_to_all | solution.py:243
  24.0 0.0 collective-permute-done.1.h2
  24.0 0.0 collective-permute-done.h1
  24.0 0.0 copy-start.4
  24.0 0.0 copy-start.5
  24.0 1.1 shard_map.64
  25.1 16.2 %all_to_all.52.arrived = bf16[16,24,4,128]{3,2,1,0:T(4,128)(2,1)S(1)} all-to-all(bf16[16,24,4,128]{3,2,1,0:T(4,128)(2,1)S(1)} %shard_map.64), channel_id=1, replica_groups=mesh['rows'=16,'delay'=16] {'rows'}, dimensions={0} | all-to-all | bytes 786432 | tf_op jit(solution)/shard_map/all_to_all | solution.py:243
  41.3 0.0 copy-done.6
  41.3 0.0 copy-done
  41.3 1.9 %shard_map.65 = bf16[4,256,128]{2,1,0:T(8,128)(2,1)S(1)} custom-call(s32[4,64]{1,0:T(4,128)S(1)} %bitcast.27, bf16[64,4,128,128]{3,2,1,0:T(8,128)(2,1)S(1)} %bitcast.12, bf16[16,24,4,128]{3,2,1,0:T(4,128)(2,1)S(1)} %all_to_all.52.arrived), custom_call_target="tpu_custom_call" | custom-call | tf_op jit(solution)/shard_map/pallas_call | solution.py:38
  43.1 12.0 %all_to_all.53.terms = bf16[4,256,128]{2,1,0:T(8,128)(2,1)S(1)} all-to-all(bf16[4,256,128]{2,1,0:T(8,128)(2,1)S(1)} %shard_map.65), channel_id=1, replica_groups={{0,4,8,12},{1,5,9,13},{2,6,10,14},{3,7,11,15},{16,20,24,28},{17,21,25,2..., dimensions={0} | all-to-all | bytes 524288 | tf_op jit(solution)/shard_map/all_to_all | solution.py:243
  55.2 11.3 %all_to_all.54.terms = bf16[4,256,128]{2,1,0:T(8,128)(2,1)S(1)} all-to-all(bf16[4,256,128]{2,1,0:T(8,128)(2,1)S(1)} %shard_map.66), channel_id=1, replica_groups={{0,1,2,3},{4,5,6,7},{8,9,10,11},{12,13,14,15},{16,17,18,19},{20,21,22,2..., dimensions={0} | all-to-all | bytes 524288 | tf_op jit(solution)/shard_map/all_to_all | solution.py:243
  66.5 0.0 copy-done.4
  66.5 0.0 copy-done.5
  66.5 1.5 %shard_map.67 = (f32[256,128]{1,0:T(8,128)S(1)}, bf16[256,128]{1,0:T(8,128)(2,1)S(1)}, bf16[16,8,4,128]{3,2,1,0:T(4,128)(2,1)}) custom-call(s32[16,8]{1,0:T(8,128)S(1)} %bitcast.24, bf16[4,256,128]{2,1,0:T(8,128)(2,1)S(1)} %all_to_all.54.terms, bf16[64,4,128]{2,1,0:T(4,128)(2,1)S(1)} %collective-permute-done.1.h2, f32[4,256,128]{2,1,0:T(8,128)S(1)} %bitcast.16, ...), custom_call_target="tpu_custom_call" | custom-call | tf_op jit(solution)/shard_map/pallas_call | solution.py:38
  68.0 3.5 %all-to-all-start.4 = ((bf16[16,8,4,128]{3,2,1,0:T(4,128)(2,1)}), bf16[16,8,4,128]{3,2,1,0:T(4,128)(2,1)S(1)}, u32[]{:S(2)}, u32[]{:S(2)}) async-start(bf16[16,8,4,128]{3,2,1,0:T(4,128)(2,1)} %get-tuple-element.12), calls=%async_computation.4 | async-start | bytes 262144 | tf_op jit(solution)/shard_map/all_to_all | solution.py:243
  71.6 1.3 collective-permute-start.2
  72.9 7.3 %all-to-all-done.4 = bf16[16,8,4,128]{3,2,1,0:T(4,128)(2,1)S(1)} async-done(((bf16[16,8,4,128]{3,2,1,0:T(4,128)(2,1)}), bf16[16,8,4,128]{3,2,1,0:T(4,128)(2,1)S(1)}, u32[]{:S(2)}, u32[]{:S(2)}) %all-to-all-start.4) | async-done | bytes 131104 | tf_op jit(solution)/shard_map/all_to_all | solution.py:243
  80.2 0.0 copy-start.1
  80.2 3.4 %copy-done.1 = bf16[1,64,4,128,128]{4,3,2,1,0:T(8,128)(2,1)S(1)} copy-done((bf16[1,64,4,128,128]{4,3,2,1,0:T(8,128)(2,1)S(1)}, bf16[1,64,4,128,128]{4,3,2,1,0:T(8,128)(2,1)}, u32[]{:S(2)}) %copy-start.1) | copy-done | bytes 8388632
  83.6 1.8 %shard_map.68.total = f32[256,128]{1,0:T(8,128)S(1)} custom-call(s32[4,64]{1,0:T(4,128)S(1)} %bitcast.28, bf16[64,4,128,128]{3,2,1,0:T(8,128)(2,1)S(1)} %bitcast.13, bf16[128,4,128]{2,1,0:T(4,128)(2,1)S(1)} %bitcast.21), custom_call_target="tpu_custom_call" | custom-call | tf_op jit(solution)/shard_map/pallas_call | solution.py:38
  85.4 0.0 collective-permute-done.2.came.before
  85.4 0.7 shard_map.69
  86.1 3.5 %all-to-all-start.5 = ((bf16[16,8,4,128]{3,2,1,0:T(4,128)(2,1)}), bf16[16,8,4,128]{3,2,1,0:T(4,128)(2,1)S(1)}, u32[]{:S(2)}, u32[]{:S(2)}) async-start(bf16[16,8,4,128]{3,2,1,0:T(4,128)(2,1)} %get-tuple-element.14), calls=%async_computation.5 | async-start | bytes 262144 | tf_op jit(solution)/shard_map/all_to_all | solution.py:243
  89.6 4.1 %collective-permute-start.3 = (f32[256,128]{1,0:T(8,128)S(1)}, f32[256,128]{1,0:T(8,128)S(1)}, u32[]{:S(2)}, u32[]{:S(2)}) collective-permute-start(f32[256,128]{1,0:T(8,128)S(1)} %get-tuple-element.15), channel_id=1, source_target_pairs={{0,1},{1,0},{4,5},{9,10},{16,17},{17,16},{20,21},{25,26},{32,33},{... | collective-permute-start | bytes 393224 | tf_op jit(solution)/shard_map/ppermute | solution.py:313
  93.8 4.5 %all-to-all-done.5 = bf16[16,8,4,128]{3,2,1,0:T(4,128)(2,1)S(1)} async-done(((bf16[16,8,4,128]{3,2,1,0:T(4,128)(2,1)}), bf16[16,8,4,128]{3,2,1,0:T(4,128)(2,1)S(1)}, u32[]{:S(2)}, u32[]{:S(2)}) %all-to-all-start.5) | async-done | bytes 131104 | tf_op jit(solution)/shard_map/all_to_all | solution.py:243
  98.2 0.0 copy-start.2
  98.2 3.4 %copy-done.2 = bf16[1,64,4,128,128]{4,3,2,1,0:T(8,128)(2,1)S(1)} copy-done((bf16[1,64,4,128,128]{4,3,2,1,0:T(8,128)(2,1)S(1)}, bf16[1,64,4,128,128]{4,3,2,1,0:T(8,128)(2,1)}, u32[]{:S(2)}) %copy-start.2) | copy-done | bytes 8388632
  101.6 0.6 shard_map.70.total
  102.2 0.0 collective-permute-done.3.came
  102.2 0.8 shard_map.71
  103.1 11.5 %all_to_all.55 = bf16[16,8,4,128]{3,2,1,0:T(4,128)(2,1)S(1)} all-to-all(bf16[16,8,4,128]{3,2,1,0:T(4,128)(2,1)S(1)} %get-tuple-element.17), channel_id=1, replica_groups=mesh['rows'=16,'delay'=16] {'rows'}, dimensions={0} | all-to-all | bytes 262144 | tf_op jit(solution)/shard_map/all_to_all | solution.py:243
  114.6 0.0 copy-start.3
  114.6 3.4 %copy-done.3 = bf16[1,64,4,128,128]{4,3,2,1,0:T(8,128)(2,1)S(1)} copy-done((bf16[1,64,4,128,128]{4,3,2,1,0:T(8,128)(2,1)S(1)}, bf16[1,64,4,128,128]{4,3,2,1,0:T(8,128)(2,1)}, u32[]{:S(2)}) %copy-start.3) | copy-done | bytes 8388632
  117.9 1.8 %shard_map.72 = bf16[16,32,128]{2,1,0:T(8,128)(2,1)S(1)} custom-call(s32[4,64]{1,0:T(4,128)S(1)} %bitcast.30, bf16[64,4,128,128]{3,2,1,0:T(8,128)(2,1)S(1)} %bitcast.15, bf16[128,4,128]{2,1,0:T(4,128)(2,1)S(1)} %bitcast.22, bf16[256,128]{1,0:T(8,128)(2,1)S(1)} %get-tuple-element.18.item), custom_call_target="tpu_custom_call" | custom-call | tf_op jit(solution)/shard_map/pallas_call | solution.py:38
  119.8 13.0 %all_to_all.56.parts = bf16[16,32,128]{2,1,0:T(8,128)(2,1)S(1)} all-to-all(bf16[16,32,128]{2,1,0:T(8,128)(2,1)S(1)} %shard_map.72), channel_id=1, replica_groups=mesh['rows'=16,'delay'=16] {'delay'}, dimensions={0} | all-to-all | bytes 262144 | tf_op jit(solution)/shard_map/all_to_all | solution.py:243
  132.8 11.8 %all_to_all.57.driven = bf16[16,64,128]{2,1,0:T(8,128)(2,1)S(1)} all-to-all(bf16[16,64,128]{2,1,0:T(8,128)(2,1)S(1)} %shard_map.73), channel_id=1, replica_groups=mesh['rows'=16,'delay'=16] {'delay'}, dimensions={0} | all-to-all | bytes 524288 | tf_op jit(solution)/shard_map/all_to_all | solution.py:243
  144.5 1.4 shard_map.74
  (2 shorter events, 0.1 us)
Async XLA Ops:
  0.0 41.3 %copy-start.6 = (s32[1,64,4]{1,2,0:T(4,128)S(1)}, s32[1,64,4]{1,2,0:T(4,128)}, u32[]{:S(2)}) copy-start(s32[1,64,4]{1,2,0:T(4,128)} %param.8) | copy-start | bytes 3076
  0.0 24.0 %collective-permute-start.1 = (bf16[64,4,128]{2,1,0:T(4,128)(2,1)}, bf16[64,4,128]{2,1,0:T(4,128)(2,1)S(1)}, u32[]{:S(2)}, u32[]{:S(2)}) collective-permute-start(bf16[64,4,128]{2,1,0:T(4,128)(2,1)} %bitcast.31), channel_id=1, source_target_pairs={{0,2},{1,3},{2,4},{3,5},{4,6},{5,7},{6,8},{7,9},{8,10},{9,11},{10,... | collective-permute-start | bytes 196616 | tf_op jit(solution)/shard_map/ppermute | solution.py:239
  4.2 19.8 %collective-permute-start = (bf16[64,4,128]{2,1,0:T(4,128)(2,1)}, bf16[64,4,128]{2,1,0:T(4,128)(2,1)S(1)}, u32[]{:S(2)}, u32[]{:S(2)}) collective-permute-start(bf16[64,4,128]{2,1,0:T(4,128)(2,1)} %bitcast.32), channel_id=1, source_target_pairs={{0,1},{1,2},{2,3},{3,4},{4,5},{5,6},{6,7},{7,8},{8,9},{9,10},{10,1... | collective-permute-start | bytes 196616 | tf_op jit(solution)/shard_map/ppermute | solution.py:239
  7.7 33.5 %copy-start = (bf16[1,64,4,128,128]{4,3,2,1,0:T(8,128)(2,1)S(1)}, bf16[1,64,4,128,128]{4,3,2,1,0:T(8,128)(2,1)}, u32[]{:S(2)}) copy-start(bf16[1,64,4,128,128]{4,3,2,1,0:T(8,128)(2,1)} %param.6) | copy-start | bytes 25165828
  24.0 42.6 %copy-start.4 = (bf16[64,128,128]{2,1,0:T(8,128)(2,1)S(1)}, bf16[64,128,128]{2,1,0:T(8,128)(2,1)}, u32[]{:S(2)}) copy-start(bf16[64,128,128]{2,1,0:T(8,128)(2,1)} %diag.7) | copy-start | bytes 6291460
  24.0 42.6 %copy-start.5 = (f32[4,64,4,128]{3,2,1,0:T(4,128)S(1)}, f32[4,64,4,128]{3,2,1,0:T(4,128)}, u32[]{:S(2)}) copy-start(f32[4,64,4,128]{3,2,1,0:T(4,128)} %param.10) | copy-start | bytes 1572868
  68.0 12.2 %all-to-all-start.4 = ((bf16[16,8,4,128]{3,2,1,0:T(4,128)(2,1)}), bf16[16,8,4,128]{3,2,1,0:T(4,128)(2,1)S(1)}, u32[]{:S(2)}, u32[]{:S(2)}) async-start(bf16[16,8,4,128]{3,2,1,0:T(4,128)(2,1)} %get-tuple-element.12), calls=%async_computation.4 | async-start | bytes 262144 | tf_op jit(solution)/shard_map/all_to_all | solution.py:243
  71.6 13.8 %collective-permute-start.2 = (f32[256,128]{1,0:T(8,128)S(1)}, f32[256,128]{1,0:T(8,128)S(1)}, u32[]{:S(2)}, u32[]{:S(2)}) collective-permute-start(f32[256,128]{1,0:T(8,128)S(1)} %get-tuple-element.13), channel_id=1, source_target_pairs={{4,0},{9,1},{2,3},{3,4},{5,6},{6,7},{7,8},{8,9},{10,11},{11,12},{1... | collective-permute-start | bytes 393224 | tf_op jit(solution)/shard_map/ppermute | solution.py:306
  80.2 3.4 %copy-start.1 = (bf16[1,64,4,128,128]{4,3,2,1,0:T(8,128)(2,1)S(1)}, bf16[1,64,4,128,128]{4,3,2,1,0:T(8,128)(2,1)}, u32[]{:S(2)}) copy-start(bf16[1,64,4,128,128]{4,3,2,1,0:T(8,128)(2,1)} %param.6) | copy-start | bytes 25165828
  86.1 12.2 %all-to-all-start.5 = ((bf16[16,8,4,128]{3,2,1,0:T(4,128)(2,1)}), bf16[16,8,4,128]{3,2,1,0:T(4,128)(2,1)S(1)}, u32[]{:S(2)}, u32[]{:S(2)}) async-start(bf16[16,8,4,128]{3,2,1,0:T(4,128)(2,1)} %get-tuple-element.14), calls=%async_computation.5 | async-start | bytes 262144 | tf_op jit(solution)/shard_map/all_to_all | solution.py:243
  89.6 12.6 %collective-permute-start.3 = (f32[256,128]{1,0:T(8,128)S(1)}, f32[256,128]{1,0:T(8,128)S(1)}, u32[]{:S(2)}, u32[]{:S(2)}) collective-permute-start(f32[256,128]{1,0:T(8,128)S(1)} %get-tuple-element.15), channel_id=1, source_target_pairs={{0,1},{1,0},{4,5},{9,10},{16,17},{17,16},{20,21},{25,26},{32,33},{... | collective-permute-start | bytes 393224 | tf_op jit(solution)/shard_map/ppermute | solution.py:313
  98.2 3.4 %copy-start.2 = (bf16[1,64,4,128,128]{4,3,2,1,0:T(8,128)(2,1)S(1)}, bf16[1,64,4,128,128]{4,3,2,1,0:T(8,128)(2,1)}, u32[]{:S(2)}) copy-start(bf16[1,64,4,128,128]{4,3,2,1,0:T(8,128)(2,1)} %param.6) | copy-start | bytes 25165828
  114.6 3.4 %copy-start.3 = (bf16[1,64,4,128,128]{4,3,2,1,0:T(8,128)(2,1)S(1)}, bf16[1,64,4,128,128]{4,3,2,1,0:T(8,128)(2,1)}, u32[]{:S(2)}) copy-start(bf16[1,64,4,128,128]{4,3,2,1,0:T(8,128)(2,1)} %param.6) | copy-start | bytes 25165828
